TPU v7x, 32 devices: a whole 2x2x4 slice. The times are simulated.
32 devices in a mesh: dp: 8 (over z, y), seq: 4 (over x, core).
Axes of the slice: x: 2, y: 2, z: 4, core: 2. Of those that a mesh axis runs over, the one named last changes fastest.
Arguments:
- tokens: bfloat16 [24, 1024, 768], P('dp', 'seq'), may hold values from -6 to 6
- prefix_len: int32 [24], P('dp'), may hold values from 0 to 1023
- timestep: int32 [24], P('dp'), may hold values from 1 to 1023
- norm_gain: bfloat16 [768], P('dp'), may hold values from 0.25 to 1.75
- norm_bias: bfloat16 [768], P('dp'), may hold values from -4 to 4
- proj_in: bfloat16 [768, 2304], P('dp'), may hold values from -0.21875 to 0.21875
- proj_in_bias: bfloat16 [2304], P('dp'), may hold values from -4 to 4
- proj_out: bfloat16 [768, 768], P('dp'), may hold values from -0.875 to 0.875
- proj_out_bias: bfloat16 [768], P('dp'), may hold values from -4 to 4
- time_table: bfloat16 [1024, 768], P('dp'), may hold values from -6 to 6
- ada_weight: bfloat16 [768, 2304], P('dp'), may hold values from -0.21875 to 0.21875
- ada_bias: bfloat16 [2304], P('dp'), may hold values from -6 to 6
- mlp_up: bfloat16 [768, 3072], P('dp'), may hold values from -0.21875 to 0.21875
- mlp_up_bias: bfloat16 [3072], P('dp'), may hold values from -4 to 4
- mlp_down: bfloat16 [3072, 768], P('dp'), may hold values from -0.109375 to 0.109375
- mlp_down_bias: bfloat16 [768], P('dp'), may hold values from -4 to 4
- out_grad: bfloat16 [24, 1024, 768], P('dp', 'seq'), may hold values from -6 to 6
Outputs:
- block_out: bfloat16 [24, 1024, 768], P('dp', 'seq')
- tokens_grad: float32 [24, 1024, 768], P('dp', 'seq')
- norm_gain_grad: float32 [768], P('dp')
- norm_bias_grad: float32 [768], P('dp')
- proj_in_grad: float32 [768, 2304], P('dp')
- proj_in_bias_grad: float32 [2304], P('dp')
- proj_out_grad: float32 [768, 768], P('dp')
- proj_out_bias_grad: float32 [768], P('dp')
- time_table_grad: float32 [1024, 768], P('dp')
- ada_weight_grad: float32 [768, 2304], P('dp')
- ada_bias_grad: float32 [2304], P('dp')
- mlp_up_grad: float32 [768, 3072], P('dp')
- mlp_up_bias_grad: float32 [3072], P('dp')
- mlp_down_grad: float32 [3072, 768], P('dp')
- mlp_down_bias_grad: float32 [768], P('dp')
All inputs are finite; a program needn't handle non-finite values.
Results may differ from a plain program's by a relative error of at most 0.012.
Values may be sent and summed in bfloat16 or wider, within the bound.
No kernel may reach another device: no remote copies, remote signals or barrier semaphores. Data moves between devices by JAX's collectives and lax.ppermute only.
A program may use at most 192 MiB of HBM per device.

v0:
```python
import functools
import math

import jax
import jax.numpy as jnp
import numpy as np
from jax import lax
from jax.experimental import pallas as pl
from jax.experimental.pallas import tpu as pltpu
from jax.sharding import PartitionSpec as P

H = 12
HD = 64
EPS = 1e-05
NEG = -1e30
COST = 30
F32 = jnp.float32
BF16 = jnp.bfloat16
HIGHEST = lax.Precision.HIGHEST
VMEM_LIMIT = 62 * 1024 * 1024
ROWS = 48
EXTRA = 16


def standardize(values):
    centred = values - jnp.mean(values, axis=-1, keepdims=True)
    inverse = lax.rsqrt(jnp.mean(centred * centred, axis=-1, keepdims=True) + EPS)
    return centred * inverse, inverse


def norm_back(gradient, normed, inverse):
    return inverse * (
        gradient
        - jnp.mean(gradient, axis=-1, keepdims=True)
        - normed * jnp.mean(gradient * normed, axis=-1, keepdims=True)
    )


def dot(left, right):
    return jnp.dot(left, right, preferred_element_type=F32)


def dot_bt(left, right):
    return lax.dot_general(left, right, (((1,), (1,)), ((), ())), preferred_element_type=F32)


def dot_at(left, right):
    return lax.dot_general(left, right, (((0,), (0,)), ((), ())), preferred_element_type=F32)


TAIL_P = 0.55
TAIL = (
    0.001045374169866761,
    0.2933056852691112,
    0.41788788917041303,
    -0.08811700935317877,
    0.8046529189842585,
    -0.5409110079247637,
    0.11213617568673577,
)


def gelu_both(values):
    bell = jnp.exp(values * values * -0.5)
    inner = 1.0 / (1.0 + (TAIL_P / math.sqrt(2.0)) * jnp.abs(values))
    tail = TAIL[6]
    for coefficient in TAIL[5::-1]:
        tail = tail * inner + coefficient
    tail = tail * bell * 0.5
    cumulative = jnp.where(values >= 0.0, 1.0 - tail, tail)
    return values * cumulative, cumulative + values * bell * (1.0 / math.sqrt(2.0 * math.pi))


def after(value, *others):
    return lax.optimization_barrier((value, others))[0]


def seq_swap(value, mask):
    return lax.ppermute(value, "seq", [(s, s ^ mask) for s in range(lax.axis_size("seq"))])


def dp_swap(value, mask):
    return lax.ppermute(value, "dp", [(d, d ^ mask) for d in range(lax.axis_size("dp"))])


def dp_collect(value):
    mine = [value] + [dp_swap(value, m) for m in range(2, lax.axis_size("dp"), 2)]
    return mine, dp_swap(jnp.stack(mine), 1)


def quad(value):
    across = seq_swap(value, 2)
    return value, across, seq_swap(jnp.stack([value, across]), 1)


def dp_turn(value, outer_only=False):
    groups = None
    if outer_only:
        outer = lax.axis_size("dp") // 2
        groups = [[o * 2 + i for o in range(outer)] for i in range(2)]
    return lax.all_to_all(
        value, "dp", split_axis=0, concat_axis=0, tiled=True, axis_index_groups=groups
    )


def dp_all(value):
    return dp_turn(jnp.broadcast_to(value[None], (lax.axis_size("dp"),) + value.shape))


def run(body, grid, meta, ins, outs, scratch=(), cost=(0, 0, 0), name=None, held=()):
    specs = [pl.BlockSpec(block, index) for _, block, index in ins]
    specs += [pl.BlockSpec(memory_space=pl.ANY) for _ in held]
    first = 1 + len(ins)
    kernel = body
    if held:

        def kernel(meta, *refs):
            return body(meta, *refs[: len(ins)], *refs[len(ins) + len(held) :])

    return pl.pallas_call(
        kernel,
        grid_spec=pltpu.PrefetchScalarGridSpec(
            num_scalar_prefetch=1,
            grid=grid,
            in_specs=specs,
            out_specs=[pl.BlockSpec(block, index) for _, _, block, index in outs],
            scratch_shapes=list(scratch),
        ),
        out_shape=[jax.ShapeDtypeStruct(shape, dtype) for shape, dtype, _, _ in outs],
        input_output_aliases={first + n: k for n, (_, k) in enumerate(held)},
        compiler_params=pltpu.CompilerParams(
            dimension_semantics=("arbitrary",) * len(grid), vmem_limit_bytes=VMEM_LIMIT
        ),
        cost_estimate=pl.CostEstimate(
            flops=int(cost[0] * COST), bytes_accessed=int(cost[1] * COST), transcendentals=0
        ),
        name=name,
    )(meta, *[array for array, _, _ in ins], *[array for array, _ in held])


def whole(array):
    zeros = (0,) * array.ndim
    return (array, array.shape, lambda *_: zeros)


def out_whole(shape, dtype):
    zeros = (0,) * len(shape)
    return (shape, dtype, shape, lambda *_: zeros)


def partner_lanes(tile):
    lane = lax.broadcasted_iota(jnp.int32, tile.shape, 1)
    ahead = pltpu.roll(tile, 96, 1)
    behind = pltpu.roll(tile, 32, 1)
    return jnp.where((lane & (HD // 2)) == 0, ahead, behind)


def qkv_kernel(meta, x0, x1, gain, bias, w, b, cosine, sine, out):
    half = w.shape[1] // 3
    tokens = jnp.where(pl.program_id(0) == 0, x0[0], x1[0]).astype(F32)
    normed, _ = standardize(tokens)
    attn_input = (normed * gain[...] + bias[...]).astype(BF16)
    projected = dot(attn_input, w[...]) + b[...]
    cos, sin = cosine[...], sine[...]
    scale = HD**-0.5
    lane = lax.broadcasted_iota(jnp.int32, cos.shape, 1)
    for t in range(2 * half // 128):
        tile = projected[:, t * 128 : (t + 1) * 128]
        turned = tile * cos + partner_lanes(tile) * sin
        if (t + 1) * 128 <= half:
            turned = turned * scale
        elif t * 128 < half:
            turned = turned * jnp.where(lane < half - t * 128, scale, 1.0)
        out[0, :, t * 128 : (t + 1) * 128] = turned.astype(BF16)
    out[0, :, 2 * half :] = projected[:, 2 * half :].astype(BF16)


def qkv_call(meta, base, x0, x1, gain, bias, w, b, cosine, sine):
    count, rows, width = x0.shape
    last = count - 1
    return run(
        qkv_kernel,
        (2, count),
        meta,
        [
            (x0, (1, rows, width), lambda p, q, m: (jnp.where(p == 0, q, last), 0, 0)),
            (x1, (1, rows, width), lambda p, q, m: (jnp.where(p == 0, 0, q), 0, 0)),
            whole(gain),
            whole(bias),
            whole(w),
            whole(b),
            (cosine, (rows, 128), lambda p, q, m: (base + p, 0)),
            (sine, (rows, 128), lambda p, q, m: (base + p, 0)),
        ],
        [
            (
                (count, 2 * rows, w.shape[1]),
                BF16,
                (1, rows, w.shape[1]),
                lambda p, q, m: (q, p, 0),
            )
        ],
        cost=(4 * count * rows * width * w.shape[1], 10 * count * rows * width, 0),
        name="qkv",
    )[0]


def fold(rows):
    half = rows.shape[0] // 2
    return jnp.concatenate([rows[:half], rows[half:]], axis=1)


def unfold(pair):
    width = pair.shape[1] // 2
    return jnp.concatenate([pair[:, :width], pair[:, width:]], axis=0)


def attend_kernel(base, meta, qa, qb, o0, o1, weights, recips):
    b, k = pl.program_id(0), pl.program_id(1)
    j = base + k
    s, prefix = meta[0], meta[4 + b]
    rows = o0.shape[1] * 2
    hw = o0.shape[2] // 2
    heads = hw // HD
    half = qa.shape[1]
    source = qb if base else qa
    mine = source[0, pl.ds(pl.multiple_of(k * rows, rows), rows), :hw]
    at = (s ^ j) * rows + lax.broadcasted_iota(jnp.int32, (rows, 1), 0)
    hidden_from = jnp.where(at < prefix, 1.0, 0.0)
    lane = lax.broadcasted_iota(jnp.int32, (1, rows), 1)
    fills = []
    for side in range(2):
        places = [(s ^ (2 * side + piece)) * rows + lane for piece in range(half // rows)]
        where = jnp.concatenate(places, axis=1)
        fills.append(jnp.where(where < prefix, 0.0, NEG))
    lane128 = lax.broadcasted_iota(jnp.int32, (rows, 128), 1)
    kept = jnp.zeros((rows, 128), F32)
    outs = []
    for h in range(heads):
        q = mine[:, h * HD : (h + 1) * HD]
        scores = []
        for side, ref in enumerate((qa, qb)):
            keys = ref[0, :, hw + h * HD : hw + (h + 1) * HD]
            scores.append(dot_bt(q, keys) + hidden_from * fills[side])
        top = jnp.maximum(
            jnp.max(scores[0], axis=1, keepdims=True), jnp.max(scores[1], axis=1, keepdims=True)
        )
        sums = jnp.zeros((rows, 1), F32)
        mixed = jnp.zeros((rows, HD), F32)
        for side, ref in enumerate((qa, qb)):
            v = ref[0, :, 2 * hw + h * HD : 2 * hw + (h + 1) * HD]
            e = jnp.exp(scores[side] - top)
            sums = sums + jnp.sum(e, axis=1, keepdims=True)
            e = e.astype(BF16)
            weights[0, h, :, side * half : (side + 1) * half] = e
            mixed = mixed + dot(e, v)
        recip = 1.0 / sums
        kept = jnp.where(lane128 == h, recip, kept)
        outs.append((mixed * recip).astype(BF16))
    recips[0] = kept
    folded = fold(jnp.concatenate(outs, axis=1))
    for n, ref in enumerate((o0, o1)):

        @pl.when(k == n)
        def _(ref=ref):
            ref[0] = folded


def attend_call(meta, base, qa, qb, rows, held=()):
    count, half, cols = qa.shape
    hw = cols // 3
    heads = hw // HD
    keys = 2 * half
    block = (1, rows // 2, 2 * hw)
    return run(
        functools.partial(attend_kernel, base),
        (count, half // rows),
        meta,
        [
            (qa, (1, half, cols), lambda b, k, m: (b, 0, 0)),
            (qb, (1, half, cols), lambda b, k, m: (b, 0, 0)),
        ],
        [((count,) + block[1:], BF16, block, lambda b, k, m: (b, 0, 0)) for _ in range(2)]
        + [
            (
                (count, heads, keys, keys),
                BF16,
                (1, heads, rows, keys),
                lambda b, k, m: (b, 0, base + k, 0),
            ),
            ((count, keys, 128), F32, (1, rows, 128), lambda b, k, m: (b, base + k, 0)),
        ],
        cost=(
            2 * count * heads * keys * keys * HD * 4,
            count * heads * keys * keys,
            count * heads * keys * keys // 2,
        ),
        name="attend",
        held=[(x, 2 + n) for n, x in enumerate(held)],
    )


def back_kernel(meta, qa, qb, weights, recips, o0, o1, o2, o3, g0, g1, g2, g3, out, dk, dv, og, go):
    j = pl.program_id(1)
    rows = o0.shape[1] * 2
    hw = o0.shape[2] // 2
    heads = hw // HD
    half = qa.shape[1]
    place = lax.rem(j, 2) * rows
    scale = HD**-0.5
    for k, (o, g) in enumerate(((o0, g0), (o1, g1), (o2, g2), (o3, g3))):

        @pl.when(j == k)
        def _(o=o, g=g):
            grad = g[...].astype(F32)
            go[...] = unfold(grad)
            og[...] = unfold(grad * o[0].astype(F32))

    @pl.when(j == 0)
    def _():
        dk[...] = jnp.zeros_like(dk)
        dv[...] = jnp.zeros_like(dv)

    mine = jnp.where(j < 2, qa[0, pl.ds(place, rows), :hw], qb[0, pl.ds(place, rows), :hw])
    query_grads = []
    for h in range(heads):
        cols = slice(h * HD, (h + 1) * HD)
        recip = recips[0, :, h : h + 1]
        grad = (go[:, cols] * recip).astype(BF16)
        centre = jnp.sum(og[:, cols], axis=1, keepdims=True) * recip
        q = mine[:, cols]
        dq = jnp.zeros((rows, HD), F32)
        for side, ref in enumerate((qa, qb)):
            k = ref[0, :, hw + h * HD : hw + (h + 1) * HD]
            v = ref[0, :, 2 * hw + h * HD : 2 * hw + (h + 1) * HD]
            e = weights[0, h, :, side * half : (side + 1) * half]
            ds = (e.astype(F32) * (dot_bt(grad, v) - centre)).astype(BF16)
            dq = dq + dot(ds, k)
            span = pl.ds(side * half, half)
            dk[h, span] += dot_at(ds, q)
            dv[h, span] += dot_at(e, grad)
        query_grads.append((dq * scale).astype(BF16))
    out[0, pl.ds(pl.multiple_of(j * rows, rows), rows), :hw] = jnp.concatenate(query_grads, axis=1)

    @pl.when(j == pl.num_programs(1) - 1)
    def _():
        out[0, :, hw : 2 * hw] = jnp.concatenate(
            [dk[h].astype(BF16) for h in range(heads)], axis=1
        )
        out[0, :, 2 * hw :] = jnp.concatenate([dv[h].astype(BF16) for h in range(heads)], axis=1)


def back_call(meta, base, some, qa, qb, weights, recips, olds, grads, held=()):
    count, half, cols = qa.shape
    hw = cols // 3
    heads = hw // HD
    keys = 2 * half
    rows = olds[0].shape[1] * 2
    block = (1,) + olds[0].shape[1:]
    piece = lambda b, j, m: (base + b, 0, 0)
    ins = [
        (qa, (1, half, cols), piece),
        (qb, (1, half, cols), piece),
        (weights, (1, heads, rows, keys), lambda b, j, m: (base + b, 0, j, 0)),
        (recips, (1, rows, 128), lambda b, j, m: (base + b, j, 0)),
    ]
    ins += [(x, block, piece) for x in olds]
    for k, x in enumerate(grads):
        first = base + (x.shape[0] - ROWS - count * block[1]) // block[1]
        ins.append((x, block[1:], lambda b, j, m, first=first: (first + b, 0)))
    return run(
        back_kernel,
        (some, keys // rows),
        meta,
        ins,
        [((count, keys, cols), BF16, (1, keys, cols), piece)],
        scratch=[
            pltpu.VMEM((heads, keys, HD), F32),
            pltpu.VMEM((heads, keys, HD), F32),
            pltpu.VMEM((rows, hw), F32),
            pltpu.VMEM((rows, hw), F32),
        ],
        cost=(8 * some * heads * keys * keys * HD * 4, 2 * some * heads * keys * keys, 0),
        name="attend_back",
        held=[(x, 0) for x in held],
    )[0]


def mix_kernel(meta, m0, m1, m2, m3, tokens, w_own, w_other, out_bias, mods, residual, mlp_in, w):
    b = pl.program_id(0)
    s, c, prefix = meta[0], meta[1], meta[4 + b]
    rows, width = tokens.shape[1:]
    hw = m0.shape[2] // 2

    @pl.when(b == 0)
    def _():
        for j in range(4):
            there = pl.ds(pl.multiple_of((s ^ j) * hw, hw), hw)
            own, other = w_own[there], w_other[there]
            even = c == 0
            w[j * hw : (j + 1) * hw, : width // 2] = jnp.where(even, own, other)
            w[j * hw : (j + 1) * hw, width // 2 :] = jnp.where(even, other, own)

    total = tokens[0].astype(F32) + out_bias[...]
    for j, ref in enumerate((m0, m1, m2, m3)):
        total = total + dot(unfold(ref[0]), w[j * hw : (j + 1) * hw])
    residual[0] = total
    normed, _ = standardize(total)
    at = s * rows + lax.broadcasted_iota(jnp.int32, (rows, 1), 0)
    clean = at < prefix
    count = pl.num_programs(0)
    noisy_row, clean_row = mods[pl.ds(b, 1)], mods[pl.ds(count, 1)]
    shift, scale = (
        jnp.where(
            clean,
            clean_row[:, part * width : (part + 1) * width],
            noisy_row[:, part * width : (part + 1) * width],
        )
        for part in range(2)
    )
    mlp_in[0] = (normed * (1.0 + scale) + shift).astype(BF16)


def mix_call(meta, parts, tokens, w_own, w_other, out_bias, mods):
    count, rows, width = tokens.shape
    seq = lambda b, m: (b, 0, 0)
    block = (1, rows, width)
    return run(
        mix_kernel,
        (count,),
        meta,
        [(p, (1,) + p.shape[1:], seq) for p in parts]
        + [(tokens, block, seq), whole(w_own), whole(w_other), whole(out_bias), whole(mods)],
        [
            (tokens.shape, F32, block, seq),
            (tokens.shape, BF16, block, seq),
            out_whole((width, width), BF16),
        ],
        cost=(2 * count * rows * width * width, 12 * count * rows * width, 0),
        name="mix",
    )


def mlp_kernel(
    meta,
    x0,
    x1,
    og0,
    og1,
    up,
    up_bias,
    down,
    mods,
    own_branch,
    own_input,
    other,
    up_here,
    up_away,
    down_here,
    down_away,
    up_bias_grad,
    up_acc,
    down_acc,
):
    p, b = pl.program_id(0), pl.program_id(1)
    count = pl.num_programs(1)
    s, i, prefix = meta[0], meta[3], meta[4 + b]
    rows, width = x0.shape[1:]
    first = p == 0
    x = jnp.where(first, x0[0], x1[0])
    incoming = jnp.where(first, og0[0], og1[0]).astype(F32)
    at = (s ^ p) * rows + lax.broadcasted_iota(jnp.int32, (rows, 1), 0)
    gate = jnp.where(
        at < prefix, mods[pl.ds(count, 1), 2 * width :], mods[pl.ds(b, 1), 2 * width :]
    )
    grad = (incoming * gate).astype(BF16)
    hidden, slope = gelu_both(dot(x, up[...]) + up_bias[...])
    hidden = hidden.astype(BF16)
    branch = dot(hidden, down[...])
    pre = (dot_bt(grad, down[...]) * slope)
    pre_low = pre.astype(BF16)
    back = dot_bt(pre_low, up[...])
    sums = jnp.sum(pre_low.astype(F32), axis=0, keepdims=True)

    @pl.when(first)
    def _():
        own_branch[0] = branch
        own_input[0] = back

    @pl.when(p == 1)
    def _():
        other[0, 0] = branch.astype(BF16)
        other[1, 0] = back.astype(BF16)

    start = jnp.logical_and(first, b == 0)

    @pl.when(start)
    def _():
        up_acc[...] = dot_at(x, pre_low)
        down_acc[...] = dot_at(hidden, grad)
        up_bias_grad[...] = sums

    @pl.when(jnp.logical_not(start))
    def _():
        up_acc[...] += dot_at(x, pre_low)
        down_acc[...] += dot_at(hidden, grad)
        up_bias_grad[...] += sums

    @pl.when(jnp.logical_and(p == 1, b == count - 1))
    def _():
        outer, deep = up_here.shape[0], up_here.shape[1]

        def blocks(o, _):
            for parity in range(2):
                d = 2 * o + parity
                upper = up_acc[pl.ds(pl.multiple_of(d * deep, deep), deep)].astype(BF16)
                base = d * (2 * deep)
                lower = jnp.concatenate(
                    [
                        down_acc[pl.ds(pl.multiple_of(base + n * deep, deep), deep)]
                        for n in range(2)
                    ],
                    axis=1,
                ).astype(BF16)

                @pl.when(i == parity)
                def _(upper=upper, lower=lower):
                    up_here[pl.ds(o, 1)] = upper[None]
                    down_here[pl.ds(o, 1)] = lower[None]

                @pl.when(i != parity)
                def _(upper=upper, lower=lower):
                    up_away[pl.ds(o, 1)] = upper[None]
                    down_away[pl.ds(o, 1)] = lower[None]

            return 0

        lax.fori_loop(0, outer, blocks, 0)


def mlp_call(meta, x0, x1, og0, og1, up, up_bias, down, mods, ranks):
    count, rows, width = x0.shape
    hidden = up.shape[1]
    last = count - 1
    block = (1, rows, width)
    first = lambda p, b, m: (jnp.where(p == 0, b, last), 0, 0)
    second = lambda p, b, m: (jnp.where(p == 0, 0, b), 0, 0)
    shared = (ranks // 2, width // ranks, hidden)
    return run(
        mlp_kernel,
        (2, count),
        meta,
        [
            (x0, block, first),
            (x1, block, second),
            (og0, block, first),
            (og1, block, second),
            whole(up),
            whole(up_bias),
            whole(down),
            whole(mods),
        ],
        [
            (x0.shape, F32, block, first),
            (x0.shape, F32, block, first),
            (
                (2,) + x0.shape,
                BF16,
                (2,) + block,
                lambda p, b, m: (0, jnp.where(p == 0, 0, b), 0, 0),
            ),
            out_whole(shared, BF16),
            out_whole(shared, BF16),
            out_whole(shared, BF16),
            out_whole(shared, BF16),
            out_whole((1, hidden), F32),
        ],
        scratch=[pltpu.VMEM((width, hidden), F32), pltpu.VMEM((hidden, width), F32)],
        cost=(24 * count * rows * width * hidden, 20 * count * rows * width, 0),
        name="mlp",
    )


def turn_kernel(
    meta,
    residual,
    out_grad,
    own_branch,
    own_input,
    got,
    down_bias,
    mods,
    m0,
    m1,
    m2,
    m3,
    w,
    block_out,
    resid_grad,
    g0,
    g1,
    g2,
    g3,
    biases,
    out_here,
    sums,
    acc,
):
    b = pl.program_id(0)
    count = pl.num_programs(0)
    s, c, prefix = meta[0], meta[1], meta[4 + b]
    rows, width = residual.shape[1:]
    hw = m0.shape[2] // 2
    resid = residual[0]
    incoming = out_grad[0].astype(F32)
    at = s * rows + lax.broadcasted_iota(jnp.int32, (rows, 1), 0)
    clean = at < prefix
    noisy_row, clean_row = mods[pl.ds(b, 1)], mods[pl.ds(count, 1)]
    scale, gate = (
        jnp.where(
            clean,
            clean_row[:, part * width : (part + 1) * width],
            noisy_row[:, part * width : (part + 1) * width],
        )
        for part in (1, 2)
    )
    branch = own_branch[0] + got[0, 0].astype(F32) + down_bias[...]
    input_two = own_input[0] + got[1, 0].astype(F32)
    block_out[0] = (resid + gate * branch).astype(BF16)
    normed, inverse = standardize(resid)
    grads = incoming + norm_back(input_two * (1.0 + scale), normed, inverse)
    resid_grad[0] = grads
    low = grads.astype(BF16)
    keep = jnp.where(clean, 1.0, 0.0)
    kept = []
    for part, value in enumerate((input_two, input_two * normed, incoming * branch)):
        value = value.astype(BF16).astype(F32)
        cols = slice(part * width, (part + 1) * width)
        everything = jnp.sum(value, axis=0, keepdims=True)
        old = jnp.sum(value * keep, axis=0, keepdims=True)
        kept.append((everything - old, old))
    branch_low = (incoming * gate).astype(BF16).astype(F32)
    down_sum = jnp.sum(branch_low, axis=0, keepdims=True)
    out_sum = jnp.sum(low.astype(F32), axis=0, keepdims=True)

    @pl.when(b == 0)
    def _():
        acc[...] = jnp.zeros_like(acc)
        biases[...] = jnp.zeros_like(biases)
        sums[...] = jnp.zeros_like(sums)

    for part, (noisy, old) in enumerate(kept):
        cols = slice(part * width, (part + 1) * width)
        sums[pl.ds(b, 1), cols] = noisy
        sums[pl.ds(count, 1), cols] += old
    biases[0:1] += down_sum
    biases[1:2] += out_sum
    for j, (m, g) in enumerate(((m0, g0), (m1, g1), (m2, g2), (m3, g3))):
        at = (width if j == 1 else 0) + b * (rows // 2)
        at = pl.ds(pl.multiple_of(at, rows // 2), rows // 2)
        g[at] = fold(dot_bt(low, w[j * hw : (j + 1) * hw])).astype(BF16)
        acc[j * hw : (j + 1) * hw] += dot_at(unfold(m[0]), low)

    @pl.when(b == count - 1)
    def _():
        for j in range(4):
            here = pl.ds(pl.multiple_of((s ^ j) * hw, hw), hw)
            block = acc[j * hw : (j + 1) * hw].astype(BF16)
            left, right = block[:, : width // 2], block[:, width // 2 :]
            even = c == 0
            out_here[here] = jnp.where(even, left, right)
            g1[here] = jnp.where(even, right, left)
        cols = g0.shape[1]
        kinds = ROWS * cols // (2 * 3 * width)
        value = sums[:kinds]
        high = value.astype(BF16)
        low_part = (value - high.astype(F32)).astype(BF16)
        lines = [
            x[k : k + 1, n * cols : (n + 1) * cols]
            for x in (high, low_part)
            for k in range(kinds)
            for n in range(3 * width // cols)
        ]
        lines = jnp.concatenate(lines, axis=0)
        for g in (g0, g1, g2, g3):
            g[g.shape[0] - ROWS :] = lines


def turn_call(meta, residual, out_grad, own_branch, own_input, got, down_bias, mods, parts, w):
    count, rows, width = residual.shape
    seq = lambda b, m: (b, 0, 0)
    block = (1, rows, width)
    return run(
        turn_kernel,
        (count,),
        meta,
        [
            (residual, block, seq),
            (out_grad, block, seq),
            (own_branch, block, seq),
            (own_input, block, seq),
            (got, (2,) + block, lambda b, m: (0, b, 0, 0)),
            whole(down_bias),
            whole(mods),
        ]
        + [(p, (1,) + p.shape[1:], seq) for p in parts]
        + [whole(w)],
        [
            (residual.shape, BF16, block, seq),
            (residual.shape, F32, block, seq),
        ]
        + [
            out_whole((extra + p.shape[0] * p.shape[1] + ROWS, p.shape[2]), BF16)
            for p, extra in zip(parts, (0, width, 0, 0))
        ]
        + [out_whole((8, width), F32), out_whole((width, width // 2), BF16)],
        scratch=[pltpu.VMEM((8, 3 * width), F32), pltpu.VMEM((width, width), F32)],
        cost=(4 * count * rows * width * width, 24 * count * rows * width, 0),
        name="turn",
    )


def rows_kernel(meta, g0, g1, g2, g3, out):
    def value(g):
        high = g[: g.shape[0] // 2].astype(F32)
        return high + g[g.shape[0] // 2 :].astype(F32)

    both = (value(g0) + value(g1)) + (value(g2) + value(g3))
    each = out.shape[1] // g0.shape[1]
    for k in range(out.shape[0]):
        out[k : k + 1] = jnp.concatenate(
            [both[k * each + n : k * each + n + 1] for n in range(each)], axis=1
        )


def proj_grad_kernel(meta, x0, x1, x2, x3, raw, w, gain, bias, up_bias, biases, cosine, sine, out, even, odd, acc, in_bias):
    b, k = pl.program_id(0), pl.program_id(1)
    hw = w.shape[1] // 3

    @pl.when(jnp.logical_and(b == 0, k == 0))
    def _():
        acc[...] = jnp.zeros_like(acc)
        in_bias[...] = jnp.zeros_like(in_bias)

    x = jnp.where(k < 2, jnp.where(k == 0, x0[0], x1[0]), jnp.where(k == 2, x2[0], x3[0]))
    normed, _ = standardize(x.astype(F32))
    cos, sin = cosine[...], sine[...]
    tiles = []
    for t in range(2 * hw // 128):
        tile = raw[0, :, t * 128 : (t + 1) * 128].astype(F32)
        tiles.append((tile * cos - partner_lanes(tile) * sin).astype(BF16))
    tiles.append(raw[0, :, 2 * hw :])
    grads = jnp.concatenate(tiles, axis=1)
    out[0] = grads
    acc[...] += dot_at(normed.astype(BF16), grads)
    in_bias[...] += jnp.sum(grads.astype(F32), axis=0, keepdims=True)

    @pl.when(jnp.logical_and(b == pl.num_programs(0) - 1, k == 3))
    def _():
        ranks = 2 * even.shape[0]
        deep, cols = acc.shape[0] // ranks, acc.shape[1]
        wide = w[...].astype(F32)
        lane = lax.broadcasted_iota(jnp.int32, (acc.shape[0], 128), 1)
        sums = jnp.where(
            lane == 0,
            jnp.sum(acc[...] * wide, axis=1, keepdims=True),
            jnp.sum(wide * in_bias[...], axis=1, keepdims=True),
        )
        sums = jnp.transpose(sums)
        flat = jnp.concatenate(
            [in_bias[...], up_bias[...], sums[0:1], sums[1:2], biases[1:2], biases[0:1]], axis=1
        )
        count = flat.shape[1] // cols
        extra = jnp.concatenate(
            [flat[:, r * cols : (r + 1) * cols] for r in range(count)]
            + [jnp.zeros((EXTRA - count, cols), F32)],
            axis=0,
        ).astype(BF16)
        gains, biases_in = (
            jnp.transpose(jnp.broadcast_to(x[...], (128, x.shape[1])))[:, :1] for x in (gain, bias)
        )
        acc[...] = acc[...] * gains + biases_in * in_bias[...]
        d = meta[2]
        for m in range(ranks):
            at = pl.ds(pl.multiple_of((d ^ m) * deep, deep), deep)
            ref = odd if m % 2 else even
            ref[m // 2, :deep] = acc[at].astype(BF16)
            ref[m // 2, deep:] = extra


def proj_grad_call(meta, xs, raw, w, gain, bias, up_bias, biases, cosine, sine, ranks):
    count, rows, width = xs[0].shape
    cols = w.shape[1]
    seq = lambda b, k, m: (b, 0, 0)
    part = lambda b, k, m: (b, k, 0)
    keys = raw.shape[1]
    shared = (ranks // 2, width // ranks + EXTRA, cols)
    return run(
        proj_grad_kernel,
        (count, keys // rows),
        meta,
        [(x, (1, rows, width), seq) for x in xs]
        + [(raw, (1, rows, cols), part)]
        + [whole(x) for x in (w, gain, bias, up_bias, biases)]
        + [(t, (rows, 128), lambda b, k, m: (k, 0)) for t in (cosine, sine)],
        [
            (raw.shape, BF16, (1, rows, cols), part),
            out_whole(shared, BF16),
            out_whole(shared, BF16),
        ],
        scratch=[pltpu.VMEM((width, cols), F32), pltpu.VMEM((1, cols), F32)],
        cost=(2 * count * keys * width * cols, 6 * count * keys * width, 0),
        name="proj_grad",
    )


def token_grad_kernel(meta, g1, g3, w, sent):
    sent[0, 0] = dot_bt(g1[0], w[...]).astype(BF16)
    sent[1, 0] = dot_bt(g3[0], w[...]).astype(BF16)


def token_grad_call(meta, grads, w, shape):
    count, rows, width = shape
    cols = w.shape[1]
    return run(
        token_grad_kernel,
        (count,),
        meta,
        [
            (grads, (1, rows, cols), lambda b, m: (b, 1, 0)),
            (grads, (1, rows, cols), lambda b, m: (b, 3, 0)),
            whole(w),
        ],
        [((2,) + shape, BF16, (2, 1, rows, width), lambda b, m: (0, b, 0, 0))],
        name="token_grad",
    )[0]


def across_kernel(meta, g2, w, got, across):
    across[0] = (dot_bt(g2[0], w[...]) + got[0, 0].astype(F32)).astype(BF16)


def across_call(meta, grads, w, got):
    _, count, rows, width = got.shape
    cols = w.shape[1]
    return run(
        across_kernel,
        (count,),
        meta,
        [
            (grads, (1, rows, cols), lambda b, m: (b, 2, 0)),
            whole(w),
            (got, (1, 1, rows, width), lambda b, m: (1, b, 0, 0)),
        ],
        [((count, rows, width), BF16, (1, rows, width), lambda b, m: (b, 0, 0))],
        name="across",
    )[0]


def last_kernel(meta, tokens, resid_grad, g0, w, got, across, gain, out):
    normed, inverse = standardize(tokens[0].astype(F32))
    grad = dot_bt(g0[0], w[...]) + got[0, 0].astype(F32) + across[0].astype(F32)
    out[0] = resid_grad[0] + norm_back(grad * gain[...], normed, inverse)


def last_call(meta, tokens, resid_grad, grads, w, got, across, gain):
    count, rows, width = tokens.shape
    cols = w.shape[1]
    seq = lambda b, m: (b, 0, 0)
    block = (1, rows, width)
    return run(
        last_kernel,
        (count,),
        meta,
        [
            (tokens, block, seq),
            (resid_grad, block, seq),
            (grads, (1, rows, cols), seq),
            whole(w),
            (got, (1,) + block, lambda b, m: (0, b, 0, 0)),
            (across, block, seq),
            whole(gain),
        ],
        [(tokens.shape, F32, block, seq)],
        cost=(2 * count * rows * width * cols, 20 * count * rows * width, 0),
        name="last",
    )[0]


def pack_in_kernel(meta, proj_in, *refs):
    *vectors, out = refs
    s = meta[0]
    deep, width = proj_in.shape[0], proj_in.shape[1] // 3
    cols = out.shape[1]
    hw = cols // 3
    for k in range(width // hw):

        @pl.when(s == k)
        def _(k=k):
            for t in range(3):
                start = t * width + k * hw
                out[:deep, t * hw : (t + 1) * hw] = proj_in[:, start : start + hw]

    out[deep:] = jnp.zeros((out.shape[0] - deep, cols), BF16)
    steps = vectors.pop()[...]
    vectors = [v[...].astype(F32) for v in vectors]
    vectors += [(steps >> 5).astype(F32), (steps & 31).astype(F32)]
    vec = jnp.concatenate(vectors, axis=1)
    size = vec.shape[1]
    for r in range(pl.cdiv(size, cols)):
        width_r = min(cols, size - r * cols)
        out[deep + r : deep + r + 1, :width_r] = vec[:, r * cols : r * cols + width_r].astype(BF16)


def place_in_kernel(sizes, meta, *refs):
    outer = len(refs) - 13
    pieces, odd, rows, refs = refs[:outer], refs[outer], refs[outer + 1], refs[outer + 2 :]
    w, gain, bias, in_b, out_bias, ada_bias, up_b, down_bias, chosen, wanted, table = refs
    ranks = 2 * outer
    s, c, d = meta[0], meta[1], meta[2]
    deep, cols = w.shape[0] // ranks, w.shape[1]
    hw = cols // 3
    for m in range(ranks):
        piece = odd.at[m // 2] if m % 2 else pieces[m // 2]
        owner = d ^ m
        w[pl.ds(pl.multiple_of(owner * deep, deep), deep)] = piece[:deep]
        table[pl.ds(owner, 1)] = piece[deep:].astype(F32)[None]
    used = -(-sum(sizes) // cols)
    flat = [
        jnp.concatenate([table[k, r : r + 1] for r in range(used)], axis=1) for k in range(ranks)
    ]
    full, start = [], 0
    for size in sizes:
        full.append([f[:, start : start + size] for f in flat])
        start += size
    steps = [high * 32.0 + low for high, low in zip(full[7], full[8])]
    full = [jnp.concatenate(x, axis=1) for x in full]
    gain[...], bias[...], out_bias[...], ada_bias[...], down_bias[...] = (
        full[0],
        full[1],
        full[3],
        full[4],
        full[6],
    )
    width = w.shape[0]
    half = sizes[5] // 2
    for k in range(width // hw):

        @pl.when(s == k)
        def _(k=k):
            in_b[...] = jnp.concatenate(
                [full[2][:, t * width + k * hw : t * width + (k + 1) * hw] for t in range(3)], axis=1
            )

    for k in range(2):

        @pl.when(c == k)
        def _(k=k):
            up_b[...] = jnp.concatenate(
                [full[5][:, (2 * n + k) * half : (2 * n + k + 1) * half] for n in range(ranks)],
                axis=1,
            )

    want = jnp.concatenate([x for step in steps for x in (step, jnp.zeros((1, 1), F32))], axis=1)
    wanted[...] = want
    at = d * rows.shape[0] + lax.broadcasted_iota(jnp.int32, (rows.shape[0], 1), 0)
    picked = dot_at((at.astype(F32) == want).astype(BF16), rows[...]).astype(BF16)
    part = rows.shape[1] // ranks
    for k in range(ranks):
        chosen[k] = picked[:, k * part : (k + 1) * part]


def pack_rest_kernel(meta, up, down, proj_out, out):
    c = meta[1]
    deep = up.shape[0]
    width = down.shape[1]
    half = down.shape[0] // 2
    ff = up.shape[1] // 2
    for k in range(2):

        @pl.when(c == k)
        def _(k=k):
            for d in range(ff // half):
                out[:, d * half : (d + 1) * half] = up[:, (2 * d + k) * half : (2 * d + k + 1) * half]
            out[:, ff : ff + width] = down[k * half : k * half + deep]
            out[:, ff + width : ff + 2 * width] = down[k * half + deep : (k + 1) * half]
            out[:, ff + 2 * width :] = proj_out[:, k * width // 2 : (k + 1) * width // 2]


def place_rest_kernel(meta, *refs):
    *pieces, up, down, out = refs
    d = meta[2]
    deep = up.shape[0] // len(pieces)
    ff, width = up.shape[1], down.shape[1]
    for m, piece in enumerate(pieces):
        owner = d ^ m
        base = pl.multiple_of(owner * deep, deep)
        up[pl.ds(base, deep)] = piece[:, :ff]
        out[pl.ds(base, deep)] = piece[:, ff + 2 * width :]
        base = pl.multiple_of(owner * (2 * deep), deep)
        down[pl.ds(base, deep)] = piece[:, ff : ff + width]
        base = pl.multiple_of(owner * (2 * deep) + deep, deep)
        down[pl.ds(base, deep)] = piece[:, ff + width : ff + 2 * width]


def half_kernel(meta, here, came, *outs):
    o = meta[2] // 2
    for m, out in enumerate(outs):
        at = pl.ds(o ^ m, 1)
        out[...] = (here[at].astype(F32) + came[at].astype(F32))[0].astype(BF16)


def join_kernel(meta, down_here, down_away, out_here, out_came, here, away):
    i = meta[3]
    outer, deep, wide = down_here.shape
    here[:, :, :wide] = down_here[...]
    away[:, :, :wide] = down_away[...]
    for k in range(2 * outer):
        rows = slice(k * deep, (k + 1) * deep)
        value = (out_here[rows].astype(F32) + out_came[rows].astype(F32)).astype(BF16)

        @pl.when(i == k % 2)
        def _(k=k, value=value):
            here[k // 2, :, wide:] = value

        @pl.when(i != k % 2)
        def _(k=k, value=value):
            away[k // 2, :, wide:] = value


def pair_kernel(meta, even, came, *outs):
    for m, out in enumerate(outs):
        out[...] = (even[m].astype(F32) + came[m].astype(F32)).astype(out.dtype)


def pair_call(meta, even, odd):
    outer = even.shape[0]
    pieces = run(
        pair_kernel,
        (1,),
        meta,
        [whole(even), whole(dp_swap(odd, 1))],
        [out_whole(even.shape[1:], even.dtype) for _ in range(outer)],
        name="pair",
    )
    return pieces[0], [pieces[0]] + [dp_swap(p, 2 * m) for m, p in enumerate(pieces) if m]


def total(refs):
    result = 0.0
    for ref in refs:
        for k in range(ref.shape[0] if len(ref.shape) == 3 else 1):
            result = result + (ref[k] if len(ref.shape) == 3 else ref[...]).astype(F32)
    return result


def gather_kernel(counts, meta, *refs):
    *refs, out = refs
    start, place = 0, 0
    for n in counts:
        value = total(refs[start : start + n])
        out[:, place : place + value.shape[1]] = value.astype(BF16)
        start, place = start + n, place + value.shape[1]


def gather_call(meta, groups):
    refs = [x for g in groups for x in g]
    shape = (groups[0][0].shape[-2], sum(g[0].shape[-1] for g in groups))
    return run(
        functools.partial(gather_kernel, tuple(len(g) for g in groups)),
        (1,),
        meta,
        [whole(x) for x in refs],
        [out_whole(shape, BF16)],
        name="gather",
    )[0]


def close_rest_kernel(meta, own, across, pair, up, down, out):
    c = meta[1]
    deep = own.shape[0]
    width = out.shape[1]
    half = down.shape[0] // 2
    ff = up.shape[1] // 2
    mine = own[...].astype(F32) + across[...].astype(F32)
    other = pair[0].astype(F32) + pair[1].astype(F32)
    for k in range(2):
        value = jnp.where(c == k, mine, other)
        for d in range(ff // half):
            up[:, (2 * d + k) * half : (2 * d + k + 1) * half] = value[:, d * half : (d + 1) * half]
        down[k * half : k * half + deep] = value[:, ff : ff + width]
        down[k * half + deep : (k + 1) * half] = value[:, ff + width : ff + 2 * width]
        out[:, k * width // 2 : (k + 1) * width // 2] = value[:, ff + 2 * width :]


def close_in_kernel(ranks, meta, own, across, beside, beyond, w, gain, bias, in_bias, out_bias, up_bias, down_bias, held):
    s, d = meta[0], meta[2]
    deep, width = w.shape[0], w.shape[1] // 3
    cols = own.shape[1]
    hw = cols // 3
    held[pl.ds(s, 1)] = own[...].astype(F32)[None]
    held[pl.ds(s ^ 2, 1)] = across[...].astype(F32)[None]
    held[pl.ds(s ^ 1, 1)] = beside[...].astype(F32)[None]
    held[pl.ds(s ^ 3, 1)] = beyond[...].astype(F32)[None]
    for k in range(4):
        for t in range(3):
            w[:, t * width + k * hw : t * width + (k + 1) * hw] = held[k, :deep, t * hw : (t + 1) * hw]
    rows = [
        jnp.concatenate([held[k, deep + r : deep + r + 1] for r in range(EXTRA)], axis=1)
        for k in range(4)
    ]
    biases = jnp.concatenate(
        [rows[k][:, t * hw : (t + 1) * hw] for t in range(3) for k in range(4)], axis=1
    )
    ff = 2 * width
    ups = [rows[0][:, cols : cols + ff] + rows[2][:, cols : cols + ff]]
    ups.append(rows[1][:, cols : cols + ff] + rows[3][:, cols : cols + ff])
    rest = rows[0] + rows[1] + rows[2] + rows[3]
    rest = rest[:, cols + ff :]
    part, third, half = width // ranks, 3 * width // ranks, ff // ranks
    for k in range(ranks):

        @pl.when(d == k)
        def _(k=k):
            for n, out in enumerate((gain, bias, out_bias, down_bias)):
                out[...] = rest[0, n * width + k * part : n * width + (k + 1) * part]
            in_bias[...] = biases[0, k * third : (k + 1) * third]
            up_bias[...] = jnp.concatenate([u[:, k * half : (k + 1) * half] for u in ups], axis=1)[0]


def shards(
    tokens,
    prefix_len,
    timestep,
    norm_gain,
    norm_bias,
    proj_in,
    proj_in_bias,
    proj_out,
    proj_out_bias,
    time_table,
    ada_weight,
    ada_bias,
    mlp_up,
    mlp_up_bias,
    mlp_down,
    mlp_down_bias,
    out_grad,
):
    count, local_len, width = tokens.shape
    members = lax.axis_size("seq")
    ranks = lax.axis_size("dp")
    s = lax.axis_index("seq")
    d = lax.axis_index("dp")
    hw = H // members * HD
    deep = proj_in.shape[0]
    half_ff = mlp_down.shape[0] // 2
    ff = ranks * half_ff
    half_out = width // 2
    meta = jnp.concatenate([jnp.stack([s, s % 2, d, d % 2]).astype(jnp.int32), prefix_len])

    tok_x = seq_swap(tokens, 2)

    half_width = HD // 2
    frequency = np.exp(np.arange(half_width) * (-math.log(10000.0) / half_width))
    angles = np.arange(local_len)[:, None] * frequency[None, :]
    cos_in, sin_in = (jnp.asarray(f(angles), F32)[None] for f in (np.cos, np.sin))
    starts = (jnp.stack([s ^ j for j in range(members)]) * local_len).astype(F32)
    starts = starts[:, None] * jnp.asarray(frequency, F32)[None, :]
    cos_at, sin_at = jnp.cos(starts)[:, None], jnp.sin(starts)[:, None]
    cosine = (cos_at * cos_in - sin_at * sin_in).reshape(-1, half_width)
    sine = (sin_at * cos_in + cos_at * sin_in).reshape(-1, half_width)
    cosine = jnp.concatenate([cosine] * 4, axis=1)
    sine = jnp.concatenate([-sine, sine] * 2, axis=1)

    vectors = [
        norm_gain,
        norm_bias,
        proj_in_bias,
        proj_out_bias,
        ada_bias,
        mlp_up_bias,
        mlp_down_bias,
        timestep,
    ]
    sizes = tuple(v.shape[0] for v in (*vectors, timestep))
    pack_in = run(
        pack_in_kernel,
        (1,),
        meta,
        [whole(proj_in), *(whole(v[None]) for v in vectors)],
        [out_whole((deep + EXTRA, 3 * hw), BF16)],
        name="pack_in",
    )[0]
    in_even = [pack_in] + [dp_swap(pack_in, m) for m in range(2, ranks, 2)]
    pack_rest = run(
        pack_rest_kernel,
        (1,),
        meta,
        [whole(after(mlp_up, pack_in)), whole(mlp_down), whole(proj_out)],
        [out_whole((deep, ff + 2 * width + half_out), BF16)],
        name="pack_rest",
    )[0]
    in_even = after(in_even, pack_rest, cosine, sine)
    in_stack = jnp.stack(in_even)
    in_odd = dp_swap(in_stack, 1)
    tok_c = seq_swap(after(tokens, in_stack), 1)
    kinds = count + 1
    in_w, gain, bias, in_b, out_bias, ada_bias_full, up_b, down_bias, chosen, wanted = run(
        functools.partial(place_in_kernel, sizes),
        (1,),
        meta,
        [whole(x) for x in (*in_even, in_odd, time_table)],
        [
            out_whole((width, 3 * hw), BF16),
            out_whole((1, width), F32),
            out_whole((1, width), F32),
            out_whole((1, 3 * hw), F32),
            out_whole((1, width), F32),
            out_whole((1, 3 * width), F32),
            out_whole((1, ff), F32),
            out_whole((1, width), F32),
            out_whole((ranks, ranks * kinds, width // ranks), BF16),
            out_whole((1, ranks * kinds), F32),
        ],
        scratch=[pltpu.VMEM((ranks, EXTRA, 3 * hw), F32)],
        name="place_in",
    )
    chosen_got = dp_turn(chosen)

    outer = ranks // 2
    early = max(1, outer // 4)
    one, two = slice(1, 1 + early), slice(1 + early, 1 + 2 * early)
    three = slice(1 + 2 * early, outer)
    rest_even = [pack_rest] + [
        dp_swap(after(pack_rest, in_even) if m > early else pack_rest, 2 * m)
        for m in range(1, 1 + 2 * early)
    ]
    rest_odd = [dp_swap(after(pack_rest, in_w), 1)]

    cosine_near = cosine
    qkv_near = qkv_call(meta, 0, tokens, tok_c, gain, bias, in_w, in_b, cosine_near, sine)
    rest_even += [
        dp_swap(after(pack_rest, qkv_near), 2 * m) for m in range(1 + 2 * early, outer)
    ]
    rest_even[one] = after(rest_even[one], qkv_near)
    rest_odd += [dp_swap(piece, 1) for piece in rest_even[one]]
    tok_x = after(tok_x, in_stack)
    tok_d = seq_swap(tok_x, 1)
    qkv_far = qkv_call(meta, 2, tok_x, tok_d, gain, bias, in_w, in_b, after(cosine, qkv_near, rest_odd[0]), sine)
    near_again = after(qkv_near, rest_even[two])
    rest_even[two] = after(rest_even[two], qkv_far)
    rest_odd += [dp_swap(piece, 1) for piece in rest_even[two]]
    mixed_2, mixed_3, weights, recips = attend_call(meta, 2, near_again, qkv_far, local_len)
    across_2, across_3 = seq_swap(mixed_2, 2), seq_swap(mixed_3, 3)
    embedded = jnp.sum(after(chosen_got, mixed_2).astype(F32), axis=0)
    activated = jax.nn.silu(embedded).astype(BF16)
    mod_parts = dot(activated, ada_weight).reshape(ranks, kinds, 3 * width)
    mod_got = dp_turn(mod_parts)
    near_again = after(
        qkv_near, mixed_2, mod_parts, rest_odd[one], rest_odd[two], rest_even[three]
    )
    rest_even[three] = after(rest_even[three], mixed_2)
    rest_odd += [dp_swap(piece, 1) for piece in rest_even[three]]
    mixed_0, mixed_1, weights, recips = attend_call(
        meta, 0, near_again, qkv_far, local_len, (weights, recips)
    )
    mixed = [mixed_0, mixed_1, mixed_2, mixed_3]
    mixed_own = [mixed_0, seq_swap(mixed_1, 1), across_2, across_3]
    mods = jnp.sum(after(mod_got, mixed_0), axis=0) + ada_bias_full
    up_w, down_w, out_own = run(
        place_rest_kernel,
        (1,),
        meta,
        [whole(x) for pair in zip([after(pack_rest, mixed_0), *rest_even[1:]], rest_odd) for x in pair],
        [
            out_whole((width, ff), BF16),
            out_whole((ff, width), BF16),
            out_whole((width, half_out), BF16),
        ],
        name="place_rest",
    )
    out_other = seq_swap(out_own, 1)
    og_other = seq_swap(after(out_grad, up_w), 1)

    residual, mlp_own, out_rel = mix_call(
        meta, mixed_own, tokens, out_own, out_other, out_bias, mods
    )
    mlp_other = seq_swap(mlp_own, 1)
    own_branch, own_input, other, up_here, up_away, down_here, down_away, up_bias_part = mlp_call(
        meta, mlp_own, mlp_other, out_grad, og_other, up_w, up_b, down_w, mods, ranks
    )
    got = seq_swap(other, 1)
    up_came = dp_swap(up_away, 1)
    block_out, resid_grad, *others = turn_call(
        meta, residual, out_grad, own_branch, own_input, got, down_bias, mods, mixed_own, out_rel
    )
    grads_sent, (biases, out_here) = others[:4], others[4:]
    head_grads = [grads_sent[0]] + [seq_swap(grads_sent[j], j) for j in (1, 2, 3)]

    def halves(here, came):
        return run(
            half_kernel,
            (1,),
            meta,
            [whole(here), whole(came)],
            [out_whole(here.shape[1:], BF16) for _ in range(outer)],
            name="half",
        )

    def spread(pieces):
        return [pieces[0]] + [dp_swap(p, 2 * m) for m, p in enumerate(pieces) if m]

    joined = (outer, deep, ff + half_out)
    down_here, down_away = run(
        join_kernel,
        (1,),
        meta,
        [
            whole(down_here),
            whole(down_away),
            whole(out_here),
            (head_grads[1], (width, half_out), lambda i, m: (0, 0)),
        ],
        [out_whole(joined, BF16), out_whole(joined, BF16)],
        name="join",
    )
    down_came = dp_swap(down_away, 1)
    up_half = halves(after(up_here, down_away), up_came)
    up_got = spread(after(up_half, head_grads))

    raw = back_call(
        meta, 0, count, after(qkv_near, up_half), qkv_far, weights, recips, mixed, head_grads
    )
    down_half = halves(after(down_here, raw), down_came)
    down_got = spread(down_half)
    up_sum = gather_call(meta, [after(up_got, raw)])
    row_grad = run(
        rows_kernel,
        (1,),
        meta,
        [
            (g, (ROWS, g.shape[1]), lambda i, m, n=g.shape[0] // ROWS - 1: (n, 0))
            for g in after(head_grads, down_half)
        ],
        [out_whole((kinds, 3 * width), F32)],
        name="rows",
    )[0]
    rows_got = dp_all(row_grad)
    grads, in_even, in_odd = proj_grad_call(
        meta,
        (tokens, tok_c, tok_x, tok_d),
        after(raw, down_half, up_sum, row_grad),
        in_w,
        gain,
        bias,
        up_bias_part,
        biases,
        cosine,
        sine,
        ranks,
    )
    in_came = dp_swap(in_odd, 1)
    sent = token_grad_call(meta, grads, in_w, tokens.shape)
    rest_sum = gather_call(meta, [(up_sum,), after(down_got, sent, rows_got)])
    came = seq_swap(after(sent, rest_sum), 1)
    rest_x = seq_swap(rest_sum, 2)
    across = across_call(meta, after(grads, rest_sum), in_w, came)
    across_got = seq_swap(across, 2)

    in_pieces = run(
        pair_kernel,
        (1,),
        meta,
        [whole(after(in_even, across)), whole(in_came)],
        [out_whole(in_even.shape[1:], BF16) for _ in range(outer)],
        name="pair",
    )
    in_got = spread(in_pieces)
    exact = functools.partial(lax.dot_general, precision=HIGHEST, preferred_element_type=F32)
    all_rows = after(rows_got, in_pieces[0]).reshape(ranks * kinds, 3 * width)
    act_rows_grad = exact(all_rows, ada_weight.astype(F32), (((1,), (1,)), ((), ())))
    embed_grad = jax.vjp(jax.nn.silu, embedded)[1](act_rows_grad)[0]
    ada_bias_grad = lax.dynamic_slice_in_dim(
        jnp.sum(after(all_rows, in_pieces[0]), axis=0), d * ada_bias.shape[0], ada_bias.shape[0], 0
    )
    ada_grad = exact(activated.astype(F32), after(all_rows, in_pieces[0]), (((0,), (0,)), ((), ())))
    rest_x = after(rest_x, in_pieces[0])
    rest_pair = seq_swap(jnp.stack([rest_sum, rest_x]), 1)
    up_final, down_final, out_final = run(
        close_rest_kernel,
        (1,),
        meta,
        [whole(x) for x in (after(rest_sum, in_pieces[0]), rest_x, rest_pair)],
        [
            out_whole(mlp_up.shape, F32),
            out_whole(mlp_down.shape, F32),
            out_whole(proj_out.shape, F32),
        ],
        name="close_rest",
    )

    in_sum = gather_call(meta, [after(in_got, ada_bias_grad, ada_grad, up_final)])
    in_parts = [in_sum] + [seq_swap(in_sum, j) for j in (2, 1, 3)]
    embed_got = dp_all(after(embed_grad, in_sum))
    tokens_grad = last_call(
        meta, tokens, after(resid_grad, in_sum), grads, in_w, came, across_got, gain
    )
    embed_all = after(embed_got, tokens_grad).transpose(1, 0, 2).reshape(ranks * kinds, width)
    table_at = d * time_table.shape[0] + jnp.arange(time_table.shape[0], dtype=jnp.int32)
    selector = (table_at.astype(F32)[:, None] == wanted).astype(F32)
    table_grad = exact(selector, embed_all, (((1,), (0,)), ((), ())))
    part, third, ff_part = width // ranks, 3 * width // ranks, 4 * width // ranks
    in_final, gain_f, bias_f, in_bias_f, out_bias_f, up_bias_f, down_bias_f = run(
        functools.partial(close_in_kernel, ranks),
        (1,),
        meta,
        [whole(x) for x in in_parts],
        [
            out_whole(proj_in.shape, F32),
            out_whole((part,), F32),
            out_whole((part,), F32),
            out_whole((third,), F32),
            out_whole((part,), F32),
            out_whole((ff_part,), F32),
            out_whole((part,), F32),
        ],
        scratch=[pltpu.VMEM((members, deep + EXTRA, 3 * hw), F32)],
        name="close_in",
    )
    return (
        block_out,
        tokens_grad,
        gain_f.reshape(-1),
        bias_f.reshape(-1),
        in_final,
        in_bias_f.reshape(-1),
        out_final,
        out_bias_f.reshape(-1),
        table_grad,
        ada_grad,
        ada_bias_grad,
        up_final,
        up_bias_f.reshape(-1),
        down_final,
        down_bias_f.reshape(-1),
    )


def solution(mesh):
    rows = P("dp", None)
    vector = P("dp")
    stream = P("dp", "seq", None)
    in_specs = (
        stream,
        vector,
        vector,
        vector,
        vector,
        rows,
        vector,
        rows,
        vector,
        rows,
        rows,
        vector,
        rows,
        vector,
        rows,
        vector,
        stream,
    )
    out_specs = (
        stream,
        stream,
        vector,
        vector,
        rows,
        vector,
        rows,
        vector,
        rows,
        rows,
        vector,
        rows,
        vector,
        rows,
        vector,
    )
    return jax.shard_map(shards, mesh=mesh, in_specs=in_specs, out_specs=out_specs, check_vma=False)
```

profile of v0, /device:TPU:0, one launch (start us, length us, event | category | flops | bytes accessed | tf_op | source)
XLA Modules:
  0.0 371.5 jit_solution(5869323420315412888)
XLA Ops:
  5.7 2.6 pack_in.1.refs_0_
  8.3 3.0 collective-permute-start
  11.4 2.6 collective-permute-start.1
  14.0 1.7 collective-permute-start.6
  17.7 2.9 pack_rest.1.refs_0_
  20.5 1.9 pad_maximum_fusion.2
  22.4 3.0 collective-permute-done.1.refs_2_
  26.7 1.6 collective-permute-start.4
  28.3 2.2 collective-permute-start.9
  31.5 10.6 %collective-permute-done.4.refs_4_ = bf16[4,112,576]{2,1,0:T(8,128)(2,1)S(1)} collective-permute-done((bf16[4,112,576]{2,1,0:T(8,128)(2,1)S(1)}, bf16[4,112,576]{2,1,0:T(8,128)(2,1)S(1)}, u32[]{:S(2)}, u32[]{:S(2)}) %collective-permute-start.4) | collective-permute-done | bytes 516128 | tf_op jit(solution)/shard_map/ppermute | solution.py:83
  42.9 3.5 place_in.1
  46.4 1.6 collective-permute-start.8
  48.0 4.5 %all-to-all-start = ((bf16[8,32,96]{2,1,0:T(8,128)(2,1)}), bf16[8,32,96]{2,1,0:T(8,128)(2,1)}, u32[]{:S(2)}, u32[]{:S(2)}) async-start(bf16[8,32,96]{2,1,0:T(8,128)(2,1)} %get-tuple-element.152), calls=%async_computation | async-start | bytes 131072 | tf_op jit(solution)/shard_map/all_to_all | solution.py:101
  52.5 1.3 reduce
  53.9 8.4 %qkv.2.qa.refs_0_ = bf16[3,512,576]{2,1,0:T(8,128)(2,1)} custom-call(s32[7]{0:T(128)} %concatenate.13.meta, bf16[3,256,768]{2,1,0:T(8,128)(2,1)} %tokens.3, bf16[3,256,768]{2,1,0:T(8,128)(2,1)} %collective-permute-done.3.x1, f32[1,768]{1,0:T(1,128)} %get-tuple-element.142.gain, f32[1,768]{1,0:T(1,128)} %get-tuple-element.143.bias, ...), custom_call_target="tpu_custom_call" | custom-call | flops 40768634880 | bytes 176947200 | tf_op jit(solution)/shard_map/qkv/pallas_call | solution.py:120
  62.3 1.6 collective-permute-done.8.refs_1_
  63.9 1.6 collective-permute-start.10
  65.5 2.2 collective-permute-start.12
  67.7 8.4 %qkv.3.qb.refs_1_ = bf16[3,512,576]{2,1,0:T(8,128)(2,1)} custom-call(s32[7]{0:T(128)} %concatenate.13.meta, bf16[3,256,768]{2,1,0:T(8,128)(2,1)} %collective-permute-done.6.x0.x2, bf16[3,256,768]{2,1,0:T(8,128)(2,1)} %collective-permute-done.7.x1.x3, f32[1,768]{1,0:T(1,128)} %get-tuple-element.142.gain, f32[1,768]{1,0:T(1,128)} %get-tuple-element.143.bias, ...), custom_call_target="tpu_custom_call" | custom-call | flops 40768634880 | bytes 176947200 | tf_op jit(solution)/shard_map/qkv/pallas_call | solution.py:120
  76.8 14.3 %attend.2 = (bf16[3,128,384]{2,1,0:T(8,128)(2,1)}, bf16[3,128,384]{2,1,0:T(8,128)(2,1)}, bf16[3,3,1024,1024]{3,2,1,0:T(8,128)(2,1)}, f32[3,1024,128]{2,1,0:T(8,128)}) custom-call(s32[7]{0:T(128)} %concatenate.13.meta, bf16[3,512,576]{2,1,0:T(8,128)(2,1)} %qkv.2.qa.refs_0_, bf16[3,512,576]{2,1,0:T(8,128)(2,1)} %qkv.3.qb.refs_1_), custom_call_target="tpu_custom_call" | custom-call | flops 144955146240 | bytes 283115520 | tf_op jit(solution)/shard_map/attend/pallas_call | solution.py:120
  91.1 1.5 collective-permute-start.14
  95.1 4.2 %all-to-all-start.1 = ((f32[8,4,2304]{2,1,0:T(4,128)}), f32[8,4,2304]{2,1,0:T(4,128)}, u32[]{:S(2)}, u32[]{:S(2)}) async-start(f32[8,4,2304]{2,1,0:T(4,128)} %reshape.143), calls=%async_computation.1 | async-start | bytes 589824 | tf_op jit(solution)/shard_map/all_to_all | solution.py:101
  99.3 1.7 collective-permute-start.16
  101.1 14.4 %attend.3 = (bf16[3,128,384]{2,1,0:T(8,128)(2,1)}, bf16[3,128,384]{2,1,0:T(8,128)(2,1)}, bf16[3,3,1024,1024]{3,2,1,0:T(8,128)(2,1)}, f32[3,1024,128]{2,1,0:T(8,128)}) custom-call(s32[7]{0:T(128)} %concatenate.13.meta, bf16[3,512,576]{2,1,0:T(8,128)(2,1)} %qkv.2.qa.refs_0_, ...), custom_call_target="tpu_custom_call", output_to_operand_aliasing={{2}: (3, {}), {3}: (4, {})} | custom-call | flops 144955146240 | bytes 283115520 | tf_op jit(solution)/shard_map/attend/pallas_call | solution.py:120
  115.5 3.2 collective-permute-done.16.refs_7_
  118.7 5.9 %place_rest.1 = (bf16[768,1536]{1,0:T(8,128)(2,1)}, bf16[1536,768]{1,0:T(8,128)(2,1)}, bf16[768,384]{1,0:T(8,128)(2,1)}) custom-call(s32[7]{0:T(128)} %concatenate.13.meta, bf16[96,3456]{1,0:T(8,128)(2,1)} %pack_rest.1.refs_0_, bf16[96,3456]{1,0:T(8,128)(2,1)} %copy-done.7, bf16[96,3456]{1,0:T(8,128)(2,1)} %collective-permute-done.9.refs_2_, ...), custom_call_target="tpu_custom_call" | custom-call | tf_op jit(solution)/shard_map/place_rest/pallas_call | solution.py:120
  128.0 6.4 %mix.1 = (f32[3,256,768]{2,1,0:T(8,128)}, bf16[3,256,768]{2,1,0:T(8,128)(2,1)}, bf16[768,768]{1,0:T(8,128)(2,1)}) custom-call(s32[7]{0:T(128)} %concatenate.13.meta, bf16[3,128,384]{2,1,0:T(8,128)(2,1)} %get-tuple-element.160.m0.o0, bf16[3,128,384]{2,1,0:T(8,128)(2,1)} %copy-done.26, bf16[3,128,384]{2,1,0:T(8,128)(2,1)} %collective-permute-done.14.m2, ...), custom_call_target="tpu_custom_call" | custom-call | flops 27179089920 | bytes 212336640 | tf_op jit(solution)/shard_map/mix/pallas_call | solution.py:120
  134.6 3.0 collective-permute-done.18.x1
  137.6 38.3 %mlp.1 = (f32[3,256,768]{2,1,0:T(8,128)}, f32[3,256,768]{2,1,0:T(8,128)}, bf16[2,3,256,768]{3,2,1,0:T(8,128)(2,1)}, bf16[4,96,1536]{2,1,0:T(8,128)(2,1)}, bf16[4...) custom-call(s32[7]{0:T(128)} %concatenate.13.meta, ...), custom_call_target="tpu_custom_call" | custom-call | flops 652298158080 | bytes 353894400 | tf_op jit(solution)/shard_map/mlp/pallas_call | solution.py:120
  177.2 3.7 collective-permute-done.20.got
  180.8 12.8 %turn.1 = (bf16[3,256,768]{2,1,0:T(8,128)(2,1)}, f32[3,256,768]{2,1,0:T(8,128)}, bf16[432,384]{1,0:T(8,128)(2,1)}, bf16[1200,384]{1,0:T(8,128)(2,1)}, bf16[432,3...) custom-call(s32[7]{0:T(128)} %concatenate.13.meta, ...), custom_call_target="tpu_custom_call" | custom-call | flops 54358179840 | bytes 424673280 | tf_op jit(solution)/shard_map/turn/pallas_call | solution.py:120
  197.3 4.6 %join.1 = (bf16[4,96,1920]{2,1,0:T(8,128)(2,1)}, bf16[4,96,1920]{2,1,0:T(8,128)(2,1)}) custom-call(s32[7]{0:T(128)} %concatenate.13.meta, bf16[4,96,1536]{2,1,0:T(8,128)(2,1)} %get-tuple-element.183.down_here, bf16[4,96,1536]{2,1,0:T(8,128)(2,1)} %get-tuple-element.184.down_away, bf16[768,384]{1,0:T(8,128)(2,1)} %get-tuple-element.185.out_here, ...), custom_call_target="tpu_custom_call" | custom-call | tf_op jit(solution)/shard_map/join/pallas_call | solution.py:120
  202.9 1.7 collective-permute-done.22.came
  204.6 3.4 half.2
  208.0 2.6 collective-permute-done.24.g3
  210.6 1.5 collective-permute-start.26
  212.1 2.4 collective-permute-start.27
  215.0 41.9 %attend_back.1.raw = bf16[3,1024,576]{2,1,0:T(8,128)(2,1)} custom-call(s32[7]{0:T(128)} %concatenate.13.meta, bf16[3,512,576]{2,1,0:T(8,128)(2,1)} %qkv.2.qa.refs_0_, bf16[3,512,576]{2,1,0:T(8,128)(2,1)} %qkv.3.qb.refs_1_, bf16[3,3,1024,1024]{3,2,1,0:T(8,128)(2,1)} %get-tuple-element.195.weights, f32[3,1024,128]{2,1,0:T(8,128)} %get-tuple-element.196.recips, ...), custom_call_target="tpu_custom_call" | custom-call | flops 579820584960 | bytes 566231040 | tf_op jit(solution)/shard_map/attend_back/pallas_call | solution.py:120
  256.9 2.8 gather.3.refs_0_
  259.7 3.7 half.3
  263.9 3.3 collective-permute-start.30
  267.8 2.1 rows.1
  269.9 1.5 broadcast_in_dim.51
  271.4 4.6 %all-to-all-start.2 = ((f32[8,4,2304]{2,1,0:T(4,128)}), f32[8,4,2304]{2,1,0:T(4,128)S(1)}, u32[]{:S(2)}, u32[]{:S(2)}) async-start(f32[8,4,2304]{2,1,0:T(4,128)} %broadcast_in_dim.51), calls=%async_computation.2 | async-start | bytes 589824 | tf_op jit(solution)/shard_map/all_to_all | solution.py:101
  276.0 18.7 %proj_grad.1 = (bf16[3,1024,576]{2,1,0:T(8,128)(2,1)}, bf16[4,112,576]{2,1,0:T(8,128)(2,1)}, bf16[4,112,576]{2,1,0:T(8,128)(2,1)}) custom-call(s32[7]{0:T(128)} %concatenate.13.meta, bf16[3,256,768]{2,1,0:T(8,128)(2,1)} %tokens.3, bf16[3,256,768]{2,1,0:T(8,128)(2,1)} %collective-permute-done.3.x1, bf16[3,256,768]{2,1,0:T(8,128)(2,1)} %collective-permute-done.6.x0.x2, ...), custom_call_target="tpu_custom_call" | custom-call | flops 81537269760 | bytes 424673280 | tf_op jit(solution)/shard_map/proj_grad/pallas_call | solution.py:120
  294.7 6.0 %token_grad.1 = bf16[2,3,256,768]{3,2,1,0:T(8,128)(2,1)} custom-call(s32[7]{0:T(128)} %concatenate.13.meta, bf16[3,1024,576]{2,1,0:T(8,128)(2,1)} %get-tuple-element.227.g1.g3.g2.g0, bf16[3,1024,576]{2,1,0:T(8,128)(2,1)} %get-tuple-element.227.g1.g3.g2.g0, bf16[768,576]{1,0:T(8,128)(2,1)} %get-tuple-element.144.w), custom_call_target="tpu_custom_call" | custom-call | tf_op jit(solution)/shard_map/token_grad/pallas_call | solution.py:120
  300.7 5.2 %all-to-all-done.2 = f32[8,4,2304]{2,1,0:T(4,128)S(1)} async-done(((f32[8,4,2304]{2,1,0:T(4,128)}), f32[8,4,2304]{2,1,0:T(4,128)S(1)}, u32[]{:S(2)}, u32[]{:S(2)}) %all-to-all-start.2) | async-done | bytes 294944 | tf_op jit(solution)/shard_map/all_to_all | solution.py:101
  306.0 3.1 gather.4.own
  310.6 3.3 collective-permute-done.32.got
  313.9 5.2 %across.1 = bf16[3,256,768]{2,1,0:T(8,128)(2,1)} custom-call(s32[7]{0:T(128)} %concatenate.13.meta, bf16[3,1024,576]{2,1,0:T(8,128)(2,1)} %get-tuple-element.227.g1.g3.g2.g0, bf16[768,576]{1,0:T(8,128)(2,1)} %get-tuple-element.144.w, bf16[2,3,256,768]{3,2,1,0:T(8,128)(2,1)} %collective-permute-done.32.got), custom_call_target="tpu_custom_call" | custom-call | tf_op jit(solution)/shard_map/across/pallas_call | solution.py:120
  319.2 5.8 %collective-permute-done.33.came = bf16[4,112,576]{2,1,0:T(8,128)(2,1)} collective-permute-done((bf16[4,112,576]{2,1,0:T(8,128)(2,1)}, bf16[4,112,576]{2,1,0:T(8,128)(2,1)}, u32[]{:S(2)}, u32[]{:S(2)}) %collective-permute-start.33) | collective-permute-done | bytes 516128 | tf_op jit(solution)/shard_map/ppermute | solution.py:83
  325.0 2.7 pair.1
  329.0 1.5 collective-permute-start.39
  330.9 2.8 collective-permute-start.35
  333.7 1.4 collective-permute-start.36
  335.8 1.5 fusion.7
  337.8 4.2 %close_rest.1 = (f32[96,3072]{1,0:T(8,128)}, f32[384,768]{1,0:T(8,128)}, f32[96,768]{1,0:T(8,128)}) custom-call(s32[7]{0:T(128)} %concatenate.13.meta, bf16[96,3456]{1,0:T(8,128)(2,1)} %gather.4.own, bf16[96,3456]{1,0:T(8,128)(2,1)} %copy-done.3, bf16[2,96,3456]{2,1,0:T(8,128)(2,1)} %collective-permute-done.38.pair), custom_call_target="tpu_custom_call" | custom-call | tf_op jit(solution)/shard_map/close_rest/pallas_call | solution.py:120
  342.0 2.8 collective-permute-done.35.refs_2_
  345.5 2.5 gather.5.own
  348.5 1.6 collective-permute-start.42
  350.8 5.5 %all-to-all-start.3 = ((f32[8,32,96]{2,1,0:T(8,128)}), f32[8,32,96]{2,1,0:T(8,128)S(1)}, u32[]{:S(2)}, u32[]{:S(2)}) async-start(f32[8,32,96]{2,1,0:T(8,128)} %broadcast_in_dim.52), calls=%async_computation.3 | async-start | bytes 262144 | tf_op jit(solution)/shard_map/all_to_all | solution.py:101
  356.3 1.8 collective-permute-done.39.across
  358.1 7.5 %last.1 = f32[3,256,768]{2,1,0:T(8,128)} custom-call(s32[7]{0:T(128)} %concatenate.13.meta, bf16[3,256,768]{2,1,0:T(8,128)(2,1)} %tokens.3, f32[3,256,768]{2,1,0:T(8,128)} %get-tuple-element.244.resid_grad, bf16[3,1024,576]{2,1,0:T(8,128)(2,1)} %get-tuple-element.227.g1.g3.g2.g0, bf16[768,576]{1,0:T(8,128)(2,1)} %get-tuple-element.144.w, ...), custom_call_target="tpu_custom_call" | custom-call | flops 20384317440 | bytes 353894400 | tf_op jit(solution)/shard_map/last/pallas_call | solution.py:120
  367.0 3.2 close_in.1
  (140 shorter events, 33.3 us)
Async XLA Ops:
  0.6 93.4 %copy-start = (bf16[96,2304]{1,0:T(8,128)(2,1)S(1)}, bf16[96,2304]{1,0:T(8,128)(2,1)}, u32[]{:S(2)}) copy-start(bf16[96,2304]{1,0:T(8,128)(2,1)} %param.30) | copy-start | bytes 1327108
  8.3 14.1 %collective-permute-start = (bf16[112,576]{1,0:T(8,128)(2,1)}, bf16[112,576]{1,0:T(8,128)(2,1)}, u32[]{:S(2)}, u32[]{:S(2)}) collective-permute-start(bf16[112,576]{1,0:T(8,128)(2,1)} %pack_in.1.refs_0_), channel_id=1, source_target_pairs={{0,8},{4,12},{8,0},{12,4},{16,24},{20,28},{24,16},{28,20},{1,9},{5... | collective-permute-start | bytes 387080 | tf_op jit(solution)/shard_map/ppermute | solution.py:83
  11.4 14.0 %collective-permute-start.1 = (bf16[112,576]{1,0:T(8,128)(2,1)}, bf16[112,576]{1,0:T(8,128)(2,1)}, u32[]{:S(2)}, u32[]{:S(2)}) collective-permute-start(bf16[112,576]{1,0:T(8,128)(2,1)} %pack_in.1.refs_0_), channel_id=1, source_target_pairs={{0,16},{4,20},{8,24},{12,28},{16,0},{20,4},{24,8},{28,12},{1,17},{... | collective-permute-start | bytes 387080 | tf_op jit(solution)/shard_map/ppermute | solution.py:83
  14.0 11.5 %collective-permute-start.2 = (bf16[112,576]{1,0:T(8,128)(2,1)}, bf16[112,576]{1,0:T(8,128)(2,1)}, u32[]{:S(2)}, u32[]{:S(2)}) collective-permute-start(bf16[112,576]{1,0:T(8,128)(2,1)} %pack_in.1.refs_0_), channel_id=1, source_target_pairs={{0,24},{4,28},{8,16},{12,20},{16,8},{20,12},{24,0},{28,4},{1,25},{... | collective-permute-start | bytes 387080 | tf_op jit(solution)/shard_map/ppermute | solution.py:83
  14.0 39.9 %collective-permute-start.6 = (bf16[3,256,768]{2,1,0:T(8,128)(2,1)}, bf16[3,256,768]{2,1,0:T(8,128)(2,1)}, u32[]{:S(2)}, u32[]{:S(2)}) collective-permute-start(bf16[3,256,768]{2,1,0:T(8,128)(2,1)} %tokens.3), channel_id=1, source_target_pairs={{0,2},{1,3},{2,0},{3,1},{4,6},{5,7},{6,4},{7,5},{8,10},{9,11},{10,... | collective-permute-start | bytes 3538952 | tf_op jit(solution)/shard_map/ppermute | solution.py:79
  20.5 4.9 %copy-start.4 = (bf16[112,576]{1,0:T(8,128)(2,1)S(1)}, bf16[112,576]{1,0:T(8,128)(2,1)}, u32[]{:S(2)}) copy-start(bf16[112,576]{1,0:T(8,128)(2,1)} %pack_in.1.refs_0_) | copy-start | bytes 387076
  26.6 27.3 %collective-permute-start.3 = (bf16[3,256,768]{2,1,0:T(8,128)(2,1)}, bf16[3,256,768]{2,1,0:T(8,128)(2,1)}, u32[]{:S(2)}, u32[]{:S(2)}) collective-permute-start(bf16[3,256,768]{2,1,0:T(8,128)(2,1)} %tokens.3), channel_id=1, source_target_pairs={{0,1},{1,0},{2,3},{3,2},{4,5},{5,4},{6,7},{7,6},{8,9},{9,8},{10,11... | collective-permute-start | bytes 3538952 | tf_op jit(solution)/shard_map/ppermute | solution.py:79
  26.7 15.4 %collective-permute-start.4 = (bf16[4,112,576]{2,1,0:T(8,128)(2,1)S(1)}, bf16[4,112,576]{2,1,0:T(8,128)(2,1)S(1)}, u32[]{:S(2)}, u32[]{:S(2)}) collective-permute-start(bf16[4,112,576]{2,1,0:T(8,128)(2,1)S(1)} %pad_maximum_fusion.1), channel_id=1, source_target_pairs={{0,4},{4,0},{8,12},{12,8},{16,20},{20,16},{24,28},{28,24},{1,5},{5... | collective-permute-start | bytes 1548296 | tf_op jit(solution)/shard_map/ppermute | solution.py:83
  28.3 35.7 %collective-permute-start.9 = (bf16[96,3456]{1,0:T(8,128)(2,1)}, bf16[96,3456]{1,0:T(8,128)(2,1)}, u32[]{:S(2)}, u32[]{:S(2)}) collective-permute-start(bf16[96,3456]{1,0:T(8,128)(2,1)} %pack_rest.1.refs_0_), channel_id=1, source_target_pairs={{0,8},{4,12},{8,0},{12,4},{16,24},{20,28},{24,16},{28,20},{1,9},{5... | collective-permute-start | bytes 1990664 | tf_op jit(solution)/shard_map/ppermute | solution.py:83
  30.5 33.4 %collective-permute-start.5 = (bf16[96,3456]{1,0:T(8,128)(2,1)}, bf16[96,3456]{1,0:T(8,128)(2,1)}, u32[]{:S(2)}, u32[]{:S(2)}) collective-permute-start(bf16[96,3456]{1,0:T(8,128)(2,1)} %pack_rest.1.refs_0_), channel_id=1, source_target_pairs={{0,16},{4,20},{8,24},{12,28},{16,0},{20,4},{24,8},{28,12},{1,17},{... | collective-permute-start | bytes 1990664 | tf_op jit(solution)/shard_map/ppermute | solution.py:83
  46.4 17.5 %collective-permute-start.8 = (bf16[96,3456]{1,0:T(8,128)(2,1)}, bf16[96,3456]{1,0:T(8,128)(2,1)S(1)}, u32[]{:S(2)}, u32[]{:S(2)}) collective-permute-start(bf16[96,3456]{1,0:T(8,128)(2,1)} %pack_rest.1.refs_0_), channel_id=1, source_target_pairs={{0,4},{4,0},{8,12},{12,8},{16,20},{20,16},{24,28},{28,24},{1,5},{5... | collective-permute-start | bytes 1990664 | tf_op jit(solution)/shard_map/ppermute | solution.py:83
  48.0 44.6 %all-to-all-start = ((bf16[8,32,96]{2,1,0:T(8,128)(2,1)}), bf16[8,32,96]{2,1,0:T(8,128)(2,1)}, u32[]{:S(2)}, u32[]{:S(2)}) async-start(bf16[8,32,96]{2,1,0:T(8,128)(2,1)} %get-tuple-element.152), calls=%async_computation | async-start | bytes 131072 | tf_op jit(solution)/shard_map/all_to_all | solution.py:101
  53.9 13.9 %collective-permute-start.7 = (bf16[3,256,768]{2,1,0:T(8,128)(2,1)}, bf16[3,256,768]{2,1,0:T(8,128)(2,1)}, u32[]{:S(2)}, u32[]{:S(2)}) collective-permute-start(bf16[3,256,768]{2,1,0:T(8,128)(2,1)} %collective-permute-done.6.x0.x2), channel_id=1, source_target_pairs={{0,1},{1,0},{2,3},{3,2},{4,5},{5,4},{6,7},{7,6},{8,9},{9,8},{10,11... | collective-permute-start | bytes 3538952 | tf_op jit(solution)/shard_map/ppermute | solution.py:79
  63.9 12.2 %copy-start.7 = (bf16[96,3456]{1,0:T(8,128)(2,1)}, bf16[96,3456]{1,0:T(8,128)(2,1)S(1)}, u32[]{:S(2)}) copy-start(bf16[96,3456]{1,0:T(8,128)(2,1)S(1)} %collective-permute-done.8.refs_1_) | copy-start | bytes 1990660
  63.9 37.1 %collective-permute-start.10 = (bf16[96,3456]{1,0:T(8,128)(2,1)}, bf16[96,3456]{1,0:T(8,128)(2,1)}, u32[]{:S(2)}, u32[]{:S(2)}) collective-permute-start(bf16[96,3456]{1,0:T(8,128)(2,1)} %collective-permute-done.9.refs_2_), channel_id=1, source_target_pairs={{0,4},{4,0},{8,12},{12,8},{16,20},{20,16},{24,28},{28,24},{1,5},{5... | collective-permute-start | bytes 1990664 | tf_op jit(solution)/shard_map/ppermute | solution.py:83
  65.5 33.8 %collective-permute-start.12 = (bf16[96,3456]{1,0:T(8,128)(2,1)}, bf16[96,3456]{1,0:T(8,128)(2,1)}, u32[]{:S(2)}, u32[]{:S(2)}) collective-permute-start(bf16[96,3456]{1,0:T(8,128)(2,1)} %pack_rest.1.refs_0_), channel_id=1, source_target_pairs={{0,24},{4,28},{8,16},{12,20},{16,8},{20,12},{24,0},{28,4},{1,25},{... | collective-permute-start | bytes 1990664 | tf_op jit(solution)/shard_map/ppermute | solution.py:83
  76.1 24.9 %collective-permute-start.11 = (bf16[96,3456]{1,0:T(8,128)(2,1)}, bf16[96,3456]{1,0:T(8,128)(2,1)}, u32[]{:S(2)}, u32[]{:S(2)}) collective-permute-start(bf16[96,3456]{1,0:T(8,128)(2,1)} %collective-permute-done.5.refs_4_), channel_id=1, source_target_pairs={{0,4},{4,0},{8,12},{12,8},{16,20},{20,16},{24,28},{28,24},{1,5},{5... | collective-permute-start | bytes 1990664 | tf_op jit(solution)/shard_map/ppermute | solution.py:83
  91.1 35.7 %collective-permute-start.14 = (bf16[3,128,384]{2,1,0:T(8,128)(2,1)}, bf16[3,128,384]{2,1,0:T(8,128)(2,1)}, u32[]{:S(2)}, u32[]{:S(2)}) collective-permute-start(bf16[3,128,384]{2,1,0:T(8,128)(2,1)} %get-tuple-element.151.o2), channel_id=1, source_target_pairs={{0,2},{1,3},{2,0},{3,1},{4,6},{5,7},{6,4},{7,5},{8,10},{9,11},{10,... | collective-permute-start | bytes 884744 | tf_op jit(solution)/shard_map/ppermute | solution.py:79
  95.1 20.4 %all-to-all-start.1 = ((f32[8,4,2304]{2,1,0:T(4,128)}), f32[8,4,2304]{2,1,0:T(4,128)}, u32[]{:S(2)}, u32[]{:S(2)}) async-start(f32[8,4,2304]{2,1,0:T(4,128)} %reshape.143), calls=%async_computation.1 | async-start | bytes 589824 | tf_op jit(solution)/shard_map/all_to_all | solution.py:101
  99.3 19.3 %collective-permute-start.16 = (bf16[96,3456]{1,0:T(8,128)(2,1)}, bf16[96,3456]{1,0:T(8,128)(2,1)}, u32[]{:S(2)}, u32[]{:S(2)}) collective-permute-start(bf16[96,3456]{1,0:T(8,128)(2,1)} %collective-permute-done.12.refs_6_), channel_id=1, source_target_pairs={{0,4},{4,0},{8,12},{12,8},{16,20},{20,16},{24,28},{28,24},{1,5},{5... | collective-permute-start | bytes 1990664 | tf_op jit(solution)/shard_map/ppermute | solution.py:83
  101.0 25.7 %collective-permute-start.15 = (bf16[3,128,384]{2,1,0:T(8,128)(2,1)}, bf16[3,128,384]{2,1,0:T(8,128)(2,1)}, u32[]{:S(2)}, u32[]{:S(2)}) collective-permute-start(bf16[3,128,384]{2,1,0:T(8,128)(2,1)} %get-tuple-element.162.o3), channel_id=1, source_target_pairs={{0,3},{1,2},{2,1},{3,0},{4,7},{5,6},{6,5},{7,4},{8,11},{9,10},{10,... | collective-permute-start | bytes 884744 | tf_op jit(solution)/shard_map/ppermute | solution.py:79
  115.4 9.1 %copy-start.25 = (bf16[3,128,384]{2,1,0:T(8,128)(2,1)S(1)}, bf16[3,128,384]{2,1,0:T(8,128)(2,1)}, u32[]{:S(2)}) copy-start(bf16[3,128,384]{2,1,0:T(8,128)(2,1)} %get-tuple-element.161.o1) | copy-start | bytes 884740
  115.4 9.6 %copy-start.24 = (bf16[3,256,768]{2,1,0:T(8,128)(2,1)S(1)}, bf16[3,256,768]{2,1,0:T(8,128)(2,1)}, u32[]{:S(2)}) copy-start(bf16[3,256,768]{2,1,0:T(8,128)(2,1)} %out_grad.1) | copy-start | bytes 3538948
  115.4 10.7 %copy-start.22 = (f32[2304]{0:T(1024)S(1)}, f32[2304]{0:T(1024)}, u32[]{:S(2)}) copy-start(f32[2304]{0:T(1024)} %reduce) | copy-start | bytes 27652
  124.5 3.5 collective-permute-start.17
  124.5 2.7 collective-permute-start.13
  125.0 9.5 %collective-permute-start.19 = (bf16[3,256,768]{2,1,0:T(8,128)(2,1)S(1)}, bf16[3,256,768]{2,1,0:T(8,128)(2,1)}, u32[]{:S(2)}, u32[]{:S(2)}) collective-permute-start(bf16[3,256,768]{2,1,0:T(8,128)(2,1)S(1)} %copy-done.24), channel_id=1, source_target_pairs={{0,1},{1,0},{2,3},{3,2},{4,5},{5,4},{6,7},{7,6},{8,9},{9,8},{10,11... | collective-permute-start | bytes 3538952 | tf_op jit(solution)/shard_map/ppermute | solution.py:79
  134.4 3.2 collective-permute-start.18
  175.9 4.9 %collective-permute-start.20 = (bf16[2,3,256,768]{3,2,1,0:T(8,128)(2,1)}, bf16[2,3,256,768]{3,2,1,0:T(8,128)(2,1)}, u32[]{:S(2)}, u32[]{:S(2)}) collective-permute-start(bf16[2,3,256,768]{3,2,1,0:T(8,128)(2,1)} %get-tuple-element.177), channel_id=1, source_target_pairs={{0,1},{1,0},{2,3},{3,2},{4,5},{5,4},{6,7},{7,6},{8,9},{9,8},{10,11... | collective-permute-start | bytes 7077896 | tf_op jit(solution)/shard_map/ppermute | solution.py:79
  176.1 28.6 %collective-permute-start.22 = (bf16[4,96,1536]{2,1,0:T(8,128)(2,1)}, bf16[4,96,1536]{2,1,0:T(8,128)(2,1)}, u32[]{:S(2)}, u32[]{:S(2)}) collective-permute-start(bf16[4,96,1536]{2,1,0:T(8,128)(2,1)} %get-tuple-element.189), channel_id=1, source_target_pairs={{0,4},{4,0},{8,12},{12,8},{16,20},{20,16},{24,28},{28,24},{1,5},{5... | collective-permute-start | bytes 3538952 | tf_op jit(solution)/shard_map/ppermute | solution.py:83
  193.6 2.8 collective-permute-start.21
  193.8 14.2 %collective-permute-start.23 = (bf16[432,384]{1,0:T(8,128)(2,1)}, bf16[432,384]{1,0:T(8,128)(2,1)S(1)}, u32[]{:S(2)}, u32[]{:S(2)}) collective-permute-start(bf16[432,384]{1,0:T(8,128)(2,1)} %get-tuple-element.198), channel_id=1, source_target_pairs={{0,2},{1,3},{2,0},{3,1},{4,6},{5,7},{6,4},{7,5},{8,10},{9,11},{10,... | collective-permute-start | bytes 995336 | tf_op jit(solution)/shard_map/ppermute | solution.py:79
  194.3 16.3 %collective-permute-start.24 = (bf16[432,384]{1,0:T(8,128)(2,1)}, bf16[432,384]{1,0:T(8,128)(2,1)S(1)}, u32[]{:S(2)}, u32[]{:S(2)}) collective-permute-start(bf16[432,384]{1,0:T(8,128)(2,1)} %get-tuple-element.199), channel_id=1, source_target_pairs={{0,3},{1,2},{2,1},{3,0},{4,7},{5,6},{6,5},{7,4},{8,11},{9,10},{10,... | collective-permute-start | bytes 995336 | tf_op jit(solution)/shard_map/ppermute | solution.py:79
  201.8 57.8 %collective-permute-start.25 = (bf16[4,96,1920]{2,1,0:T(8,128)(2,1)}, bf16[4,96,1920]{2,1,0:T(8,128)(2,1)}, u32[]{:S(2)}, u32[]{:S(2)}) collective-permute-start(bf16[4,96,1920]{2,1,0:T(8,128)(2,1)} %get-tuple-element.187), channel_id=1, source_target_pairs={{0,4},{4,0},{8,12},{12,8},{16,20},{20,16},{24,28},{28,24},{1,5},{5... | collective-permute-start | bytes 4423688 | tf_op jit(solution)/shard_map/ppermute | solution.py:83
  208.0 7.0 %copy-start.12 = (bf16[432,384]{1,0:T(8,128)(2,1)}, bf16[432,384]{1,0:T(8,128)(2,1)S(1)}, u32[]{:S(2)}) copy-start(bf16[432,384]{1,0:T(8,128)(2,1)S(1)} %collective-permute-done.23.g2) | copy-start | bytes 995332
  210.6 4.4 %copy-start.13 = (bf16[432,384]{1,0:T(8,128)(2,1)}, bf16[432,384]{1,0:T(8,128)(2,1)S(1)}, u32[]{:S(2)}) copy-start(bf16[432,384]{1,0:T(8,128)(2,1)S(1)} %collective-permute-done.24.g3) | copy-start | bytes 995332
  210.6 46.3 %collective-permute-start.26 = (bf16[96,1536]{1,0:T(8,128)(2,1)}, bf16[96,1536]{1,0:T(8,128)(2,1)}, u32[]{:S(2)}, u32[]{:S(2)}) collective-permute-start(bf16[96,1536]{1,0:T(8,128)(2,1)} %get-tuple-element.207), channel_id=1, source_target_pairs={{0,8},{4,12},{8,0},{12,4},{16,24},{20,28},{24,16},{28,20},{1,9},{5... | collective-permute-start | bytes 884744 | tf_op jit(solution)/shard_map/ppermute | solution.py:83
  212.1 44.8 %collective-permute-start.27 = (bf16[96,1536]{1,0:T(8,128)(2,1)}, bf16[96,1536]{1,0:T(8,128)(2,1)}, u32[]{:S(2)}, u32[]{:S(2)}) collective-permute-start(bf16[96,1536]{1,0:T(8,128)(2,1)} %get-tuple-element.208), channel_id=1, source_target_pairs={{0,16},{4,20},{8,24},{12,28},{16,0},{20,4},{24,8},{28,12},{1,17},{... | collective-permute-start | bytes 884744 | tf_op jit(solution)/shard_map/ppermute | solution.py:83
  214.5 42.4 %collective-permute-start.28 = (bf16[96,1536]{1,0:T(8,128)(2,1)}, bf16[96,1536]{1,0:T(8,128)(2,1)}, u32[]{:S(2)}, u32[]{:S(2)}) collective-permute-start(bf16[96,1536]{1,0:T(8,128)(2,1)} %get-tuple-element.209), channel_id=1, source_target_pairs={{0,24},{4,28},{8,16},{12,20},{16,8},{20,12},{24,0},{28,4},{1,25},{... | collective-permute-start | bytes 884744 | tf_op jit(solution)/shard_map/ppermute | solution.py:83
  263.4 37.3 %collective-permute-start.29 = (bf16[96,1920]{1,0:T(8,128)(2,1)}, bf16[96,1920]{1,0:T(8,128)(2,1)S(1)}, u32[]{:S(2)}, u32[]{:S(2)}) collective-permute-start(bf16[96,1920]{1,0:T(8,128)(2,1)} %get-tuple-element.203), channel_id=1, source_target_pairs={{0,8},{4,12},{8,0},{12,4},{16,24},{20,28},{24,16},{28,20},{1,9},{5... | collective-permute-start | bytes 1105928 | tf_op jit(solution)/shard_map/ppermute | solution.py:83
  263.9 36.7 %collective-permute-start.30 = (bf16[96,1920]{1,0:T(8,128)(2,1)}, bf16[96,1920]{1,0:T(8,128)(2,1)S(1)}, u32[]{:S(2)}, u32[]{:S(2)}) collective-permute-start(bf16[96,1920]{1,0:T(8,128)(2,1)} %get-tuple-element.204), channel_id=1, source_target_pairs={{0,16},{4,20},{8,24},{12,28},{16,0},{20,4},{24,8},{28,12},{1,17},{... | collective-permute-start | bytes 1105928 | tf_op jit(solution)/shard_map/ppermute | solution.py:83
  267.2 33.4 %collective-permute-start.31 = (bf16[96,1920]{1,0:T(8,128)(2,1)}, bf16[96,1920]{1,0:T(8,128)(2,1)S(1)}, u32[]{:S(2)}, u32[]{:S(2)}) collective-permute-start(bf16[96,1920]{1,0:T(8,128)(2,1)} %get-tuple-element.205), channel_id=1, source_target_pairs={{0,24},{4,28},{8,16},{12,20},{16,8},{20,12},{24,0},{28,4},{1,25},{... | collective-permute-start | bytes 1105928 | tf_op jit(solution)/shard_map/ppermute | solution.py:83
  271.4 34.5 %all-to-all-start.2 = ((f32[8,4,2304]{2,1,0:T(4,128)}), f32[8,4,2304]{2,1,0:T(4,128)S(1)}, u32[]{:S(2)}, u32[]{:S(2)}) async-start(f32[8,4,2304]{2,1,0:T(4,128)} %broadcast_in_dim.51), calls=%async_computation.2 | async-start | bytes 589824 | tf_op jit(solution)/shard_map/all_to_all | solution.py:101
  300.6 5.3 %copy-start.9 = (bf16[96,1920]{1,0:T(8,128)(2,1)}, bf16[96,1920]{1,0:T(8,128)(2,1)S(1)}, u32[]{:S(2)}) copy-start(bf16[96,1920]{1,0:T(8,128)(2,1)S(1)} %collective-permute-done.29.refs_2_) | copy-start | bytes 1105924
  300.7 5.3 %copy-start.10 = (bf16[96,1920]{1,0:T(8,128)(2,1)}, bf16[96,1920]{1,0:T(8,128)(2,1)S(1)}, u32[]{:S(2)}) copy-start(bf16[96,1920]{1,0:T(8,128)(2,1)S(1)} %collective-permute-done.30.refs_3_) | copy-start | bytes 1105924
  300.7 5.3 %copy-start.11 = (bf16[96,1920]{1,0:T(8,128)(2,1)}, bf16[96,1920]{1,0:T(8,128)(2,1)S(1)}, u32[]{:S(2)}) copy-start(bf16[96,1920]{1,0:T(8,128)(2,1)S(1)} %collective-permute-done.31.refs_4_) | copy-start | bytes 1105924
  305.9 3.1 copy-start.5
  309.1 4.9 %collective-permute-start.32 = (bf16[2,3,256,768]{3,2,1,0:T(8,128)(2,1)}, bf16[2,3,256,768]{3,2,1,0:T(8,128)(2,1)}, u32[]{:S(2)}, u32[]{:S(2)}) collective-permute-start(bf16[2,3,256,768]{3,2,1,0:T(8,128)(2,1)} %token_grad.1), channel_id=1, source_target_pairs={{0,1},{1,0},{2,3},{3,2},{4,5},{5,4},{6,7},{7,6},{8,9},{9,8},{10,11... | collective-permute-start | bytes 7077896 | tf_op jit(solution)/shard_map/ppermute | solution.py:79
  309.1 18.7 %collective-permute-start.37 = (bf16[96,3456]{1,0:T(8,128)(2,1)}, bf16[96,3456]{1,0:T(8,128)(2,1)S(1)}, u32[]{:S(2)}, u32[]{:S(2)}) collective-permute-start(bf16[96,3456]{1,0:T(8,128)(2,1)} %gather.4.own), channel_id=1, source_target_pairs={{0,2},{1,3},{2,0},{3,1},{4,6},{5,7},{6,4},{7,5},{8,10},{9,11},{10,... | collective-permute-start | bytes 1990664 | tf_op jit(solution)/shard_map/ppermute | solution.py:79
  309.6 15.4 %collective-permute-start.33 = (bf16[4,112,576]{2,1,0:T(8,128)(2,1)}, bf16[4,112,576]{2,1,0:T(8,128)(2,1)}, u32[]{:S(2)}, u32[]{:S(2)}) collective-permute-start(bf16[4,112,576]{2,1,0:T(8,128)(2,1)} %get-tuple-element.230), channel_id=1, source_target_pairs={{0,4},{4,0},{8,12},{12,8},{16,20},{20,16},{24,28},{28,24},{1,5},{5... | collective-permute-start | bytes 1548296 | tf_op jit(solution)/shard_map/ppermute | solution.py:83
  319.2 8.5 %copy-start.1 = (bf16[96,3456]{1,0:T(8,128)(2,1)S(1)}, bf16[96,3456]{1,0:T(8,128)(2,1)}, u32[]{:S(2)}) copy-start(bf16[96,3456]{1,0:T(8,128)(2,1)} %gather.4.own) | copy-start | bytes 1990660
  327.7 2.8 copy-start.6
  327.7 6.0 %copy-start.27 = (bf16[112,576]{1,0:T(8,128)(2,1)S(1)}, bf16[112,576]{1,0:T(8,128)(2,1)}, u32[]{:S(2)}) copy-start(bf16[112,576]{1,0:T(8,128)(2,1)} %get-tuple-element.234) | copy-start | bytes 387076
  327.8 8.0 %copy-start.15 = (f32[32,96]{1,0:T(8,128)S(1)}, f32[32,96]{1,0:T(8,128)}, u32[]{:S(2)}) copy-start(f32[32,96]{1,0:T(8,128)} %copy-done.14) | copy-start | bytes 36868
  329.0 8.8 %collective-permute-start.38 = (bf16[2,96,3456]{2,1,0:T(8,128)(2,1)}, bf16[2,96,3456]{2,1,0:T(8,128)(2,1)}, u32[]{:S(2)}, u32[]{:S(2)}) collective-permute-start(bf16[2,96,3456]{2,1,0:T(8,128)(2,1)} %pad_maximum_fusion), channel_id=1, source_target_pairs={{0,1},{1,0},{2,3},{3,2},{4,5},{5,4},{6,7},{7,6},{8,9},{9,8},{10,11... | collective-permute-start | bytes 3981320 | tf_op jit(solution)/shard_map/ppermute | solution.py:79
  329.0 29.1 %collective-permute-start.39 = (bf16[3,256,768]{2,1,0:T(8,128)(2,1)}, bf16[3,256,768]{2,1,0:T(8,128)(2,1)}, u32[]{:S(2)}, u32[]{:S(2)}) collective-permute-start(bf16[3,256,768]{2,1,0:T(8,128)(2,1)} %across.1), channel_id=1, source_target_pairs={{0,2},{1,3},{2,0},{3,1},{4,6},{5,7},{6,4},{7,5},{8,10},{9,11},{10,... | collective-permute-start | bytes 3538952 | tf_op jit(solution)/shard_map/ppermute | solution.py:79
  330.7 11.3 %collective-permute-start.34 = (bf16[112,576]{1,0:T(8,128)(2,1)}, bf16[112,576]{1,0:T(8,128)(2,1)S(1)}, u32[]{:S(2)}, u32[]{:S(2)}) collective-permute-start(bf16[112,576]{1,0:T(8,128)(2,1)} %get-tuple-element.232), channel_id=1, source_target_pairs={{0,8},{4,12},{8,0},{12,4},{16,24},{20,28},{24,16},{28,20},{1,9},{5... | collective-permute-start | bytes 387080 | tf_op jit(solution)/shard_map/ppermute | solution.py:83
  330.9 13.9 %collective-permute-start.35 = (bf16[112,576]{1,0:T(8,128)(2,1)}, bf16[112,576]{1,0:T(8,128)(2,1)S(1)}, u32[]{:S(2)}, u32[]{:S(2)}) collective-permute-start(bf16[112,576]{1,0:T(8,128)(2,1)} %get-tuple-element.233), channel_id=1, source_target_pairs={{0,16},{4,20},{8,24},{12,28},{16,0},{20,4},{24,8},{28,12},{1,17},{... | collective-permute-start | bytes 387080 | tf_op jit(solution)/shard_map/ppermute | solution.py:83
  333.7 11.1 %collective-permute-start.36 = (bf16[112,576]{1,0:T(8,128)(2,1)S(1)}, bf16[112,576]{1,0:T(8,128)(2,1)S(1)}, u32[]{:S(2)}, u32[]{:S(2)}) collective-permute-start(bf16[112,576]{1,0:T(8,128)(2,1)S(1)} %copy-done.27), channel_id=1, source_target_pairs={{0,24},{4,28},{8,16},{12,20},{16,8},{20,12},{24,0},{28,4},{1,25},{... | collective-permute-start | bytes 387080 | tf_op jit(solution)/shard_map/ppermute | solution.py:83
  348.0 17.6 %collective-permute-start.40 = (bf16[112,576]{1,0:T(8,128)(2,1)}, bf16[112,576]{1,0:T(8,128)(2,1)S(1)}, u32[]{:S(2)}, u32[]{:S(2)}) collective-permute-start(bf16[112,576]{1,0:T(8,128)(2,1)} %gather.5.own), channel_id=1, source_target_pairs={{0,2},{1,3},{2,0},{3,1},{4,6},{5,7},{6,4},{7,5},{8,10},{9,11},{10,... | collective-permute-start | bytes 387080 | tf_op jit(solution)/shard_map/ppermute | solution.py:79
  348.5 17.1 %collective-permute-start.41 = (bf16[112,576]{1,0:T(8,128)(2,1)}, bf16[112,576]{1,0:T(8,128)(2,1)S(1)}, u32[]{:S(2)}, u32[]{:S(2)}) collective-permute-start(bf16[112,576]{1,0:T(8,128)(2,1)} %gather.5.own), channel_id=1, source_target_pairs={{0,1},{1,0},{2,3},{3,2},{4,5},{5,4},{6,7},{7,6},{8,9},{9,8},{10,11... | collective-permute-start | bytes 387080 | tf_op jit(solution)/shard_map/ppermute | solution.py:79
  348.5 17.1 %collective-permute-start.42 = (bf16[112,576]{1,0:T(8,128)(2,1)}, bf16[112,576]{1,0:T(8,128)(2,1)S(1)}, u32[]{:S(2)}, u32[]{:S(2)}) collective-permute-start(bf16[112,576]{1,0:T(8,128)(2,1)} %gather.5.own), channel_id=1, source_target_pairs={{0,3},{1,2},{2,1},{3,0},{4,7},{5,6},{6,5},{7,4},{8,11},{9,10},{10,... | collective-permute-start | bytes 387080 | tf_op jit(solution)/shard_map/ppermute | solution.py:79
  350.8 19.3 %all-to-all-start.3 = ((f32[8,32,96]{2,1,0:T(8,128)}), f32[8,32,96]{2,1,0:T(8,128)S(1)}, u32[]{:S(2)}, u32[]{:S(2)}) async-start(f32[8,32,96]{2,1,0:T(8,128)} %broadcast_in_dim.52), calls=%async_computation.3 | async-start | bytes 262144 | tf_op jit(solution)/shard_map/all_to_all | solution.py:101
  356.3 14.0 %copy-start.23 = (f32[1,32]{1,0:T(1,128)S(1)}, f32[1,32]{1,0:T(1,128)}, u32[]{:S(2)}) copy-start(f32[1,32]{1,0:T(1,128)} %get-tuple-element.251) | copy-start | bytes 388
  (11 other events, 10.5 us)
where the time goes:
time: 374 us; the launch traced here: 371 us
  Pallas kernels  229 us (61%)
  starting transfers between devices  63.8 us (17%)
  waiting for transfers between devices  49.7 us (13%)
  local copies, waits for them, and re-layouts  14.1 us (4%)
  other arithmetic  10.1 us (3%)
    pallas_call x26, Pallas kernels, run(): pl.pallas_call(kernel, grid_spec=pltpu.PrefetchScalarGridSpec(num_scalar_...  229 us
    ppermute x23, starting transfers between devices, dp_swap(): lax.ppermute(value, 'dp', [(d, d ^ mask) for d in range(lax.axis_size('dp...  34.6 us
    ppermute x23, waiting for transfers between devices, dp_swap(): lax.ppermute(value, 'dp', [(d, d ^ mask) for d in range(lax.axis_size('dp...  28.7 us
    all_to_all x4, starting transfers between devices, dp_turn(): lax.all_to_all(value, 'dp', split_axis=0, concat_axis=0, tiled=True, axis...  18.8 us
    ppermute x20, waiting for transfers between devices, seq_swap(): lax.ppermute(value, 'seq', [(s, s ^ mask) for s in range(lax.axis_size('s...  15.7 us
    ppermute x20, starting transfers between devices, seq_swap(): lax.ppermute(value, 'seq', [(s, s ^ mask) for s in range(lax.axis_size('s...  10.3 us
  transfers between devices with their start and end apart: 47, of which 15 were waited for; matrix products, arithmetic and copies ran while one was open for 4% of the time, Pallas kernels for 49%

commit v1 on v0

--- a/solution.py
+++ b/solution.py
@@ -213,6 +213,22 @@
 def unfold(pair):
     width = pair.shape[1] // 2
     return jnp.concatenate([pair[:, :width], pair[:, width:]], axis=0)
+
+
+def flip(value):
+    rows, width = value.shape
+    spare = -width % 128
+    if spare:
+        value = jnp.concatenate([value, jnp.zeros((rows, spare), value.dtype)], axis=1)
+    return jnp.transpose(value)[:width]
+
+
+def unflip(parts):
+    width = sum(p.shape[0] for p in parts)
+    spare = -width % 128
+    if spare:
+        parts = [*parts, jnp.zeros((spare, parts[0].shape[1]), parts[0].dtype)]
+    return jnp.transpose(jnp.concatenate(parts, axis=0))[:, :width]
 
 
 def attend_kernel(base, meta, qa, qb, o0, o1, weights, recips):
@@ -322,32 +338,32 @@
         dv[...] = jnp.zeros_like(dv)
 
     mine = jnp.where(j < 2, qa[0, pl.ds(place, rows), :hw], qb[0, pl.ds(place, rows), :hw])
+    grads = []
+    for h in range(heads):
+        cols = slice(h * HD, (h + 1) * HD)
+        grads.append((go[:, cols] * recips[0, :, h : h + 1]).astype(BF16))
+    turned, turned_q = flip(jnp.concatenate(grads, axis=1)), flip(mine)
     query_grads = []
     for h in range(heads):
         cols = slice(h * HD, (h + 1) * HD)
-        recip = recips[0, :, h : h + 1]
-        grad = (go[:, cols] * recip).astype(BF16)
-        centre = jnp.sum(og[:, cols], axis=1, keepdims=True) * recip
-        q = mine[:, cols]
+        centre = jnp.sum(og[:, cols], axis=1, keepdims=True) * recips[0, :, h : h + 1]
         dq = jnp.zeros((rows, HD), F32)
         for side, ref in enumerate((qa, qb)):
             k = ref[0, :, hw + h * HD : hw + (h + 1) * HD]
             v = ref[0, :, 2 * hw + h * HD : 2 * hw + (h + 1) * HD]
-            e = weights[0, h, :, side * half : (side + 1) * half]
-            ds = (e.astype(F32) * (dot_bt(grad, v) - centre)).astype(BF16)
+            span = slice(side * half, (side + 1) * half)
+            e = weights[0, h, :, span]
+            ds = (e.astype(F32) * (dot_bt(grads[h], v) - centre)).astype(BF16)
             dq = dq + dot(ds, k)
-            span = pl.ds(side * half, half)
-            dk[h, span] += dot_at(ds, q)
-            dv[h, span] += dot_at(e, grad)
+            dk[h, :, span] += dot(turned_q[cols], ds)
+            dv[h, :, span] += dot(turned[cols], e)
         query_grads.append((dq * scale).astype(BF16))
     out[0, pl.ds(pl.multiple_of(j * rows, rows), rows), :hw] = jnp.concatenate(query_grads, axis=1)
 
     @pl.when(j == pl.num_programs(1) - 1)
     def _():
-        out[0, :, hw : 2 * hw] = jnp.concatenate(
-            [dk[h].astype(BF16) for h in range(heads)], axis=1
-        )
-        out[0, :, 2 * hw :] = jnp.concatenate([dv[h].astype(BF16) for h in range(heads)], axis=1)
+        out[0, :, hw : 2 * hw] = unflip([dk[h] for h in range(heads)]).astype(BF16)
+        out[0, :, 2 * hw :] = unflip([dv[h] for h in range(heads)]).astype(BF16)
 
 
 def back_call(meta, base, some, qa, qb, weights, recips, olds, grads, held=()):
@@ -375,8 +391,8 @@
         ins,
         [((count, keys, cols), BF16, (1, keys, cols), piece)],
         scratch=[
-            pltpu.VMEM((heads, keys, HD), F32),
-            pltpu.VMEM((heads, keys, HD), F32),
+            pltpu.VMEM((heads, HD, keys), F32),
+            pltpu.VMEM((heads, HD, keys), F32),
             pltpu.VMEM((rows, hw), F32),
             pltpu.VMEM((rows, hw), F32),
         ],

time: 374 us -> 367 us (0.981)
  Pallas kernels: 229 us -> 223 us
    pallas_call x26, Pallas kernels: 229 us -> 223 us  [run(): pl.pallas_call(kernel, grid_spec=pltpu.PrefetchScalarGridSpec(num_scalar_...]
  transfers between devices with their start and end apart: 47 -> 47, of which waited for: 15 -> 15; matrix products, arithmetic and copies ran while one was open for 4% -> 4% of each run, Pallas kernels for 49% -> 48%
where the time goes in v1:
time: 367 us; the launch traced here: 365 us
  Pallas kernels  223 us (61%)
  starting transfers between devices  63.8 us (17%)
  waiting for transfers between devices  49.7 us (14%)
  local copies, waits for them, and re-layouts  14.1 us (4%)
  other arithmetic  10.1 us (3%)
    pallas_call x26, Pallas kernels, run(): pl.pallas_call(kernel, grid_spec=pltpu.PrefetchScalarGridSpec(num_scalar_...  223 us
    ppermute x23, starting transfers between devices, dp_swap(): lax.ppermute(value, 'dp', [(d, d ^ mask) for d in range(lax.axis_size('dp...  34.6 us
    ppermute x23, waiting for transfers between devices, dp_swap(): lax.ppermute(value, 'dp', [(d, d ^ mask) for d in range(lax.axis_size('dp...  28.7 us
    all_to_all x4, starting transfers between devices, dp_turn(): lax.all_to_all(value, 'dp', split_axis=0, concat_axis=0, tiled=True, axis...  18.8 us
    ppermute x20, waiting for transfers between devices, seq_swap(): lax.ppermute(value, 'seq', [(s, s ^ mask) for s in range(lax.axis_size('s...  15.7 us
    ppermute x20, starting transfers between devices, seq_swap(): lax.ppermute(value, 'seq', [(s, s ^ mask) for s in range(lax.axis_size('s...  10.3 us
  transfers between devices with their start and end apart: 47, of which 15 were waited for; matrix products, arithmetic and copies ran while one was open for 4% of the time, Pallas kernels for 48%

profile of v1, /device:TPU:0, one launch (start us, length us, event | category | flops | bytes accessed | tf_op | source)
XLA Modules:
  0.0 365.0 jit_solution(6080870876337943227)
XLA Ops:
  5.7 2.6 pack_in.1.refs_0_
  8.3 3.0 collective-permute-start
  11.4 2.6 collective-permute-start.1
  14.0 1.7 collective-permute-start.6
  17.7 2.9 pack_rest.1.refs_0_
  20.5 1.9 pad_maximum_fusion.2
  22.4 3.0 collective-permute-done.1.refs_2_
  26.7 1.6 collective-permute-start.4
  28.3 2.2 collective-permute-start.9
  31.5 10.6 %collective-permute-done.4.refs_4_ = bf16[4,112,576]{2,1,0:T(8,128)(2,1)S(1)} collective-permute-done((bf16[4,112,576]{2,1,0:T(8,128)(2,1)S(1)}, bf16[4,112,576]{2,1,0:T(8,128)(2,1)S(1)}, u32[]{:S(2)}, u32[]{:S(2)}) %collective-permute-start.4) | collective-permute-done | bytes 516128 | tf_op jit(solution)/shard_map/ppermute | solution.py:83
  42.9 3.5 place_in.1
  46.4 1.6 collective-permute-start.8
  48.0 4.5 %all-to-all-start = ((bf16[8,32,96]{2,1,0:T(8,128)(2,1)}), bf16[8,32,96]{2,1,0:T(8,128)(2,1)}, u32[]{:S(2)}, u32[]{:S(2)}) async-start(bf16[8,32,96]{2,1,0:T(8,128)(2,1)} %get-tuple-element.152), calls=%async_computation | async-start | bytes 131072 | tf_op jit(solution)/shard_map/all_to_all | solution.py:101
  52.5 1.3 reduce
  53.9 8.4 %qkv.2.qa.refs_0_ = bf16[3,512,576]{2,1,0:T(8,128)(2,1)} custom-call(s32[7]{0:T(128)} %concatenate.13.meta, bf16[3,256,768]{2,1,0:T(8,128)(2,1)} %tokens.3, bf16[3,256,768]{2,1,0:T(8,128)(2,1)} %collective-permute-done.3.x1, f32[1,768]{1,0:T(1,128)} %get-tuple-element.142.gain, f32[1,768]{1,0:T(1,128)} %get-tuple-element.143.bias, ...), custom_call_target="tpu_custom_call" | custom-call | flops 40768634880 | bytes 176947200 | tf_op jit(solution)/shard_map/qkv/pallas_call | solution.py:120
  62.3 1.6 collective-permute-done.8.refs_1_
  63.9 1.6 collective-permute-start.10
  65.5 2.2 collective-permute-start.12
  67.7 8.4 %qkv.3.qb.refs_1_ = bf16[3,512,576]{2,1,0:T(8,128)(2,1)} custom-call(s32[7]{0:T(128)} %concatenate.13.meta, bf16[3,256,768]{2,1,0:T(8,128)(2,1)} %collective-permute-done.6.x0.x2, bf16[3,256,768]{2,1,0:T(8,128)(2,1)} %collective-permute-done.7.x1.x3, f32[1,768]{1,0:T(1,128)} %get-tuple-element.142.gain, f32[1,768]{1,0:T(1,128)} %get-tuple-element.143.bias, ...), custom_call_target="tpu_custom_call" | custom-call | flops 40768634880 | bytes 176947200 | tf_op jit(solution)/shard_map/qkv/pallas_call | solution.py:120
  76.8 14.3 %attend.2 = (bf16[3,128,384]{2,1,0:T(8,128)(2,1)}, bf16[3,128,384]{2,1,0:T(8,128)(2,1)}, bf16[3,3,1024,1024]{3,2,1,0:T(8,128)(2,1)}, f32[3,1024,128]{2,1,0:T(8,128)}) custom-call(s32[7]{0:T(128)} %concatenate.13.meta, bf16[3,512,576]{2,1,0:T(8,128)(2,1)} %qkv.2.qa.refs_0_, bf16[3,512,576]{2,1,0:T(8,128)(2,1)} %qkv.3.qb.refs_1_), custom_call_target="tpu_custom_call" | custom-call | flops 144955146240 | bytes 283115520 | tf_op jit(solution)/shard_map/attend/pallas_call | solution.py:120
  91.1 1.5 collective-permute-start.14
  95.1 4.2 %all-to-all-start.1 = ((f32[8,4,2304]{2,1,0:T(4,128)}), f32[8,4,2304]{2,1,0:T(4,128)}, u32[]{:S(2)}, u32[]{:S(2)}) async-start(f32[8,4,2304]{2,1,0:T(4,128)} %reshape.143), calls=%async_computation.1 | async-start | bytes 589824 | tf_op jit(solution)/shard_map/all_to_all | solution.py:101
  99.3 1.7 collective-permute-start.16
  101.1 14.4 %attend.3 = (bf16[3,128,384]{2,1,0:T(8,128)(2,1)}, bf16[3,128,384]{2,1,0:T(8,128)(2,1)}, bf16[3,3,1024,1024]{3,2,1,0:T(8,128)(2,1)}, f32[3,1024,128]{2,1,0:T(8,128)}) custom-call(s32[7]{0:T(128)} %concatenate.13.meta, bf16[3,512,576]{2,1,0:T(8,128)(2,1)} %qkv.2.qa.refs_0_, ...), custom_call_target="tpu_custom_call", output_to_operand_aliasing={{2}: (3, {}), {3}: (4, {})} | custom-call | flops 144955146240 | bytes 283115520 | tf_op jit(solution)/shard_map/attend/pallas_call | solution.py:120
  115.5 3.2 collective-permute-done.16.refs_7_
  118.7 5.9 %place_rest.1 = (bf16[768,1536]{1,0:T(8,128)(2,1)}, bf16[1536,768]{1,0:T(8,128)(2,1)}, bf16[768,384]{1,0:T(8,128)(2,1)}) custom-call(s32[7]{0:T(128)} %concatenate.13.meta, bf16[96,3456]{1,0:T(8,128)(2,1)} %pack_rest.1.refs_0_, bf16[96,3456]{1,0:T(8,128)(2,1)} %copy-done.7, bf16[96,3456]{1,0:T(8,128)(2,1)} %collective-permute-done.9.refs_2_, ...), custom_call_target="tpu_custom_call" | custom-call | tf_op jit(solution)/shard_map/place_rest/pallas_call | solution.py:120
  128.0 6.4 %mix.1 = (f32[3,256,768]{2,1,0:T(8,128)}, bf16[3,256,768]{2,1,0:T(8,128)(2,1)}, bf16[768,768]{1,0:T(8,128)(2,1)}) custom-call(s32[7]{0:T(128)} %concatenate.13.meta, bf16[3,128,384]{2,1,0:T(8,128)(2,1)} %get-tuple-element.160.m0.o0, bf16[3,128,384]{2,1,0:T(8,128)(2,1)} %copy-done.26, bf16[3,128,384]{2,1,0:T(8,128)(2,1)} %collective-permute-done.14.m2, ...), custom_call_target="tpu_custom_call" | custom-call | flops 27179089920 | bytes 212336640 | tf_op jit(solution)/shard_map/mix/pallas_call | solution.py:120
  134.6 3.0 collective-permute-done.18.x1
  137.6 38.3 %mlp.1 = (f32[3,256,768]{2,1,0:T(8,128)}, f32[3,256,768]{2,1,0:T(8,128)}, bf16[2,3,256,768]{3,2,1,0:T(8,128)(2,1)}, bf16[4,96,1536]{2,1,0:T(8,128)(2,1)}, bf16[4...) custom-call(s32[7]{0:T(128)} %concatenate.13.meta, ...), custom_call_target="tpu_custom_call" | custom-call | flops 652298158080 | bytes 353894400 | tf_op jit(solution)/shard_map/mlp/pallas_call | solution.py:120
  177.2 3.7 %collective-permute-done.20.got = bf16[2,3,256,768]{3,2,1,0:T(8,128)(2,1)} collective-permute-done((bf16[2,3,256,768]{3,2,1,0:T(8,128)(2,1)}, bf16[2,3,256,768]{3,2,1,0:T(8,128)(2,1)}, u32[]{:S(2)}, u32[]{:S(2)}) %collective-permute-start.20) | collective-permute-done | bytes 2359328 | tf_op jit(solution)/shard_map/ppermute | solution.py:79
  180.8 12.8 %turn.1 = (bf16[3,256,768]{2,1,0:T(8,128)(2,1)}, f32[3,256,768]{2,1,0:T(8,128)}, bf16[432,384]{1,0:T(8,128)(2,1)}, bf16[1200,384]{1,0:T(8,128)(2,1)}, bf16[432,3...) custom-call(s32[7]{0:T(128)} %concatenate.13.meta, ...), custom_call_target="tpu_custom_call" | custom-call | flops 54358179840 | bytes 424673280 | tf_op jit(solution)/shard_map/turn/pallas_call | solution.py:120
  197.3 4.6 %join.1 = (bf16[4,96,1920]{2,1,0:T(8,128)(2,1)}, bf16[4,96,1920]{2,1,0:T(8,128)(2,1)}) custom-call(s32[7]{0:T(128)} %concatenate.13.meta, bf16[4,96,1536]{2,1,0:T(8,128)(2,1)} %get-tuple-element.183.down_here, bf16[4,96,1536]{2,1,0:T(8,128)(2,1)} %get-tuple-element.184.down_away, bf16[768,384]{1,0:T(8,128)(2,1)} %get-tuple-element.185.out_here, ...), custom_call_target="tpu_custom_call" | custom-call | tf_op jit(solution)/shard_map/join/pallas_call | solution.py:120
  202.9 1.7 collective-permute-done.22.came
  204.6 3.4 half.2
  208.0 2.6 collective-permute-done.24.g3
  210.6 1.5 collective-permute-start.26
  212.1 2.4 collective-permute-start.27
  215.0 35.4 %attend_back.1.raw = bf16[3,1024,576]{2,1,0:T(8,128)(2,1)} custom-call(s32[7]{0:T(128)} %concatenate.13.meta, bf16[3,512,576]{2,1,0:T(8,128)(2,1)} %qkv.2.qa.refs_0_, bf16[3,512,576]{2,1,0:T(8,128)(2,1)} %qkv.3.qb.refs_1_, bf16[3,3,1024,1024]{3,2,1,0:T(8,128)(2,1)} %get-tuple-element.195.weights, f32[3,1024,128]{2,1,0:T(8,128)} %get-tuple-element.196.recips, ...), custom_call_target="tpu_custom_call" | custom-call | flops 579820584960 | bytes 566231040 | tf_op jit(solution)/shard_map/attend_back/pallas_call | solution.py:120
  250.4 2.8 gather.3.refs_0_
  253.2 3.7 %half.3 = (bf16[96,1920]{1,0:T(8,128)(2,1)}, bf16[96,1920]{1,0:T(8,128)(2,1)}, bf16[96,1920]{1,0:T(8,128)(2,1)}, bf16[96,1920]{1,0:T(8,128)(2,1)}) custom-call(s32[7]{0:T(128)} %concatenate.13.meta, bf16[4,96,1920]{2,1,0:T(8,128)(2,1)} %get-tuple-element.201.here, bf16[4,96,1920]{2,1,0:T(8,128)(2,1)} %collective-permute-done.25.came), custom_call_target="tpu_custom_call" | custom-call | tf_op jit(solution)/shard_map/half/pallas_call | solution.py:120
  257.5 3.3 collective-permute-start.30
  261.3 2.1 rows.1
  263.4 1.5 broadcast_in_dim.51
  264.9 4.6 %all-to-all-start.2 = ((f32[8,4,2304]{2,1,0:T(4,128)}), f32[8,4,2304]{2,1,0:T(4,128)S(1)}, u32[]{:S(2)}, u32[]{:S(2)}) async-start(f32[8,4,2304]{2,1,0:T(4,128)} %broadcast_in_dim.51), calls=%async_computation.2 | async-start | bytes 589824 | tf_op jit(solution)/shard_map/all_to_all | solution.py:101
  269.5 18.7 %proj_grad.1 = (bf16[3,1024,576]{2,1,0:T(8,128)(2,1)}, bf16[4,112,576]{2,1,0:T(8,128)(2,1)}, bf16[4,112,576]{2,1,0:T(8,128)(2,1)}) custom-call(s32[7]{0:T(128)} %concatenate.13.meta, bf16[3,256,768]{2,1,0:T(8,128)(2,1)} %tokens.3, bf16[3,256,768]{2,1,0:T(8,128)(2,1)} %collective-permute-done.3.x1, bf16[3,256,768]{2,1,0:T(8,128)(2,1)} %collective-permute-done.6.x0.x2, ...), custom_call_target="tpu_custom_call" | custom-call | flops 81537269760 | bytes 424673280 | tf_op jit(solution)/shard_map/proj_grad/pallas_call | solution.py:120
  288.2 6.0 %token_grad.1 = bf16[2,3,256,768]{3,2,1,0:T(8,128)(2,1)} custom-call(s32[7]{0:T(128)} %concatenate.13.meta, bf16[3,1024,576]{2,1,0:T(8,128)(2,1)} %get-tuple-element.227.g1.g3.g2.g0, bf16[3,1024,576]{2,1,0:T(8,128)(2,1)} %get-tuple-element.227.g1.g3.g2.g0, bf16[768,576]{1,0:T(8,128)(2,1)} %get-tuple-element.144.w), custom_call_target="tpu_custom_call" | custom-call | tf_op jit(solution)/shard_map/token_grad/pallas_call | solution.py:120
  294.2 5.2 %all-to-all-done.2 = f32[8,4,2304]{2,1,0:T(4,128)S(1)} async-done(((f32[8,4,2304]{2,1,0:T(4,128)}), f32[8,4,2304]{2,1,0:T(4,128)S(1)}, u32[]{:S(2)}, u32[]{:S(2)}) %all-to-all-start.2) | async-done | bytes 294944 | tf_op jit(solution)/shard_map/all_to_all | solution.py:101
  299.5 3.1 gather.4.own
  304.1 3.3 collective-permute-done.32.got
  307.4 5.2 %across.1 = bf16[3,256,768]{2,1,0:T(8,128)(2,1)} custom-call(s32[7]{0:T(128)} %concatenate.13.meta, bf16[3,1024,576]{2,1,0:T(8,128)(2,1)} %get-tuple-element.227.g1.g3.g2.g0, bf16[768,576]{1,0:T(8,128)(2,1)} %get-tuple-element.144.w, bf16[2,3,256,768]{3,2,1,0:T(8,128)(2,1)} %collective-permute-done.32.got), custom_call_target="tpu_custom_call" | custom-call | tf_op jit(solution)/shard_map/across/pallas_call | solution.py:120
  312.7 5.8 %collective-permute-done.33.came = bf16[4,112,576]{2,1,0:T(8,128)(2,1)} collective-permute-done((bf16[4,112,576]{2,1,0:T(8,128)(2,1)}, bf16[4,112,576]{2,1,0:T(8,128)(2,1)}, u32[]{:S(2)}, u32[]{:S(2)}) %collective-permute-start.33) | collective-permute-done | bytes 516128 | tf_op jit(solution)/shard_map/ppermute | solution.py:83
  318.5 2.7 pair.1
  322.5 1.5 collective-permute-start.39
  324.4 2.8 collective-permute-start.35
  327.2 1.4 collective-permute-start.36
  329.3 1.5 fusion.7
  331.3 4.2 %close_rest.1 = (f32[96,3072]{1,0:T(8,128)}, f32[384,768]{1,0:T(8,128)}, f32[96,768]{1,0:T(8,128)}) custom-call(s32[7]{0:T(128)} %concatenate.13.meta, bf16[96,3456]{1,0:T(8,128)(2,1)} %gather.4.own, bf16[96,3456]{1,0:T(8,128)(2,1)} %copy-done.3, bf16[2,96,3456]{2,1,0:T(8,128)(2,1)} %collective-permute-done.38.pair), custom_call_target="tpu_custom_call" | custom-call | tf_op jit(solution)/shard_map/close_rest/pallas_call | solution.py:120
  335.5 2.8 collective-permute-done.35.refs_2_
  339.0 2.5 gather.5.own
  342.0 1.6 collective-permute-start.42
  344.3 5.5 %all-to-all-start.3 = ((f32[8,32,96]{2,1,0:T(8,128)}), f32[8,32,96]{2,1,0:T(8,128)S(1)}, u32[]{:S(2)}, u32[]{:S(2)}) async-start(f32[8,32,96]{2,1,0:T(8,128)} %broadcast_in_dim.52), calls=%async_computation.3 | async-start | bytes 262144 | tf_op jit(solution)/shard_map/all_to_all | solution.py:101
  349.8 1.8 collective-permute-done.39.across
  351.6 7.5 %last.1 = f32[3,256,768]{2,1,0:T(8,128)} custom-call(s32[7]{0:T(128)} %concatenate.13.meta, bf16[3,256,768]{2,1,0:T(8,128)(2,1)} %tokens.3, f32[3,256,768]{2,1,0:T(8,128)} %get-tuple-element.244.resid_grad, bf16[3,1024,576]{2,1,0:T(8,128)(2,1)} %get-tuple-element.227.g1.g3.g2.g0, bf16[768,576]{1,0:T(8,128)(2,1)} %get-tuple-element.144.w, ...), custom_call_target="tpu_custom_call" | custom-call | flops 20384317440 | bytes 353894400 | tf_op jit(solution)/shard_map/last/pallas_call | solution.py:120
  360.5 3.2 close_in.1
  (140 shorter events, 33.3 us)
Async XLA Ops:
  0.6 93.4 %copy-start = (bf16[96,2304]{1,0:T(8,128)(2,1)S(1)}, bf16[96,2304]{1,0:T(8,128)(2,1)}, u32[]{:S(2)}) copy-start(bf16[96,2304]{1,0:T(8,128)(2,1)} %param.30) | copy-start | bytes 1327108
  8.3 14.1 %collective-permute-start = (bf16[112,576]{1,0:T(8,128)(2,1)}, bf16[112,576]{1,0:T(8,128)(2,1)}, u32[]{:S(2)}, u32[]{:S(2)}) collective-permute-start(bf16[112,576]{1,0:T(8,128)(2,1)} %pack_in.1.refs_0_), channel_id=1, source_target_pairs={{0,8},{4,12},{8,0},{12,4},{16,24},{20,28},{24,16},{28,20},{1,9},{5... | collective-permute-start | bytes 387080 | tf_op jit(solution)/shard_map/ppermute | solution.py:83
  11.4 14.0 %collective-permute-start.1 = (bf16[112,576]{1,0:T(8,128)(2,1)}, bf16[112,576]{1,0:T(8,128)(2,1)}, u32[]{:S(2)}, u32[]{:S(2)}) collective-permute-start(bf16[112,576]{1,0:T(8,128)(2,1)} %pack_in.1.refs_0_), channel_id=1, source_target_pairs={{0,16},{4,20},{8,24},{12,28},{16,0},{20,4},{24,8},{28,12},{1,17},{... | collective-permute-start | bytes 387080 | tf_op jit(solution)/shard_map/ppermute | solution.py:83
  14.0 11.5 %collective-permute-start.2 = (bf16[112,576]{1,0:T(8,128)(2,1)}, bf16[112,576]{1,0:T(8,128)(2,1)}, u32[]{:S(2)}, u32[]{:S(2)}) collective-permute-start(bf16[112,576]{1,0:T(8,128)(2,1)} %pack_in.1.refs_0_), channel_id=1, source_target_pairs={{0,24},{4,28},{8,16},{12,20},{16,8},{20,12},{24,0},{28,4},{1,25},{... | collective-permute-start | bytes 387080 | tf_op jit(solution)/shard_map/ppermute | solution.py:83
  14.0 39.9 %collective-permute-start.6 = (bf16[3,256,768]{2,1,0:T(8,128)(2,1)}, bf16[3,256,768]{2,1,0:T(8,128)(2,1)}, u32[]{:S(2)}, u32[]{:S(2)}) collective-permute-start(bf16[3,256,768]{2,1,0:T(8,128)(2,1)} %tokens.3), channel_id=1, source_target_pairs={{0,2},{1,3},{2,0},{3,1},{4,6},{5,7},{6,4},{7,5},{8,10},{9,11},{10,... | collective-permute-start | bytes 3538952 | tf_op jit(solution)/shard_map/ppermute | solution.py:79
  20.5 4.9 %copy-start.4 = (bf16[112,576]{1,0:T(8,128)(2,1)S(1)}, bf16[112,576]{1,0:T(8,128)(2,1)}, u32[]{:S(2)}) copy-start(bf16[112,576]{1,0:T(8,128)(2,1)} %pack_in.1.refs_0_) | copy-start | bytes 387076
  26.6 27.3 %collective-permute-start.3 = (bf16[3,256,768]{2,1,0:T(8,128)(2,1)}, bf16[3,256,768]{2,1,0:T(8,128)(2,1)}, u32[]{:S(2)}, u32[]{:S(2)}) collective-permute-start(bf16[3,256,768]{2,1,0:T(8,128)(2,1)} %tokens.3), channel_id=1, source_target_pairs={{0,1},{1,0},{2,3},{3,2},{4,5},{5,4},{6,7},{7,6},{8,9},{9,8},{10,11... | collective-permute-start | bytes 3538952 | tf_op jit(solution)/shard_map/ppermute | solution.py:79
  26.7 15.4 %collective-permute-start.4 = (bf16[4,112,576]{2,1,0:T(8,128)(2,1)S(1)}, bf16[4,112,576]{2,1,0:T(8,128)(2,1)S(1)}, u32[]{:S(2)}, u32[]{:S(2)}) collective-permute-start(bf16[4,112,576]{2,1,0:T(8,128)(2,1)S(1)} %pad_maximum_fusion.1), channel_id=1, source_target_pairs={{0,4},{4,0},{8,12},{12,8},{16,20},{20,16},{24,28},{28,24},{1,5},{5... | collective-permute-start | bytes 1548296 | tf_op jit(solution)/shard_map/ppermute | solution.py:83
  28.3 35.7 %collective-permute-start.9 = (bf16[96,3456]{1,0:T(8,128)(2,1)}, bf16[96,3456]{1,0:T(8,128)(2,1)}, u32[]{:S(2)}, u32[]{:S(2)}) collective-permute-start(bf16[96,3456]{1,0:T(8,128)(2,1)} %pack_rest.1.refs_0_), channel_id=1, source_target_pairs={{0,8},{4,12},{8,0},{12,4},{16,24},{20,28},{24,16},{28,20},{1,9},{5... | collective-permute-start | bytes 1990664 | tf_op jit(solution)/shard_map/ppermute | solution.py:83
  30.5 33.4 %collective-permute-start.5 = (bf16[96,3456]{1,0:T(8,128)(2,1)}, bf16[96,3456]{1,0:T(8,128)(2,1)}, u32[]{:S(2)}, u32[]{:S(2)}) collective-permute-start(bf16[96,3456]{1,0:T(8,128)(2,1)} %pack_rest.1.refs_0_), channel_id=1, source_target_pairs={{0,16},{4,20},{8,24},{12,28},{16,0},{20,4},{24,8},{28,12},{1,17},{... | collective-permute-start | bytes 1990664 | tf_op jit(solution)/shard_map/ppermute | solution.py:83
  46.4 17.5 %collective-permute-start.8 = (bf16[96,3456]{1,0:T(8,128)(2,1)}, bf16[96,3456]{1,0:T(8,128)(2,1)S(1)}, u32[]{:S(2)}, u32[]{:S(2)}) collective-permute-start(bf16[96,3456]{1,0:T(8,128)(2,1)} %pack_rest.1.refs_0_), channel_id=1, source_target_pairs={{0,4},{4,0},{8,12},{12,8},{16,20},{20,16},{24,28},{28,24},{1,5},{5... | collective-permute-start | bytes 1990664 | tf_op jit(solution)/shard_map/ppermute | solution.py:83
  48.0 44.6 %all-to-all-start = ((bf16[8,32,96]{2,1,0:T(8,128)(2,1)}), bf16[8,32,96]{2,1,0:T(8,128)(2,1)}, u32[]{:S(2)}, u32[]{:S(2)}) async-start(bf16[8,32,96]{2,1,0:T(8,128)(2,1)} %get-tuple-element.152), calls=%async_computation | async-start | bytes 131072 | tf_op jit(solution)/shard_map/all_to_all | solution.py:101
  53.9 13.9 %collective-permute-start.7 = (bf16[3,256,768]{2,1,0:T(8,128)(2,1)}, bf16[3,256,768]{2,1,0:T(8,128)(2,1)}, u32[]{:S(2)}, u32[]{:S(2)}) collective-permute-start(bf16[3,256,768]{2,1,0:T(8,128)(2,1)} %collective-permute-done.6.x0.x2), channel_id=1, source_target_pairs={{0,1},{1,0},{2,3},{3,2},{4,5},{5,4},{6,7},{7,6},{8,9},{9,8},{10,11... | collective-permute-start | bytes 3538952 | tf_op jit(solution)/shard_map/ppermute | solution.py:79
  63.9 12.2 %copy-start.7 = (bf16[96,3456]{1,0:T(8,128)(2,1)}, bf16[96,3456]{1,0:T(8,128)(2,1)S(1)}, u32[]{:S(2)}) copy-start(bf16[96,3456]{1,0:T(8,128)(2,1)S(1)} %collective-permute-done.8.refs_1_) | copy-start | bytes 1990660
  63.9 37.1 %collective-permute-start.10 = (bf16[96,3456]{1,0:T(8,128)(2,1)}, bf16[96,3456]{1,0:T(8,128)(2,1)}, u32[]{:S(2)}, u32[]{:S(2)}) collective-permute-start(bf16[96,3456]{1,0:T(8,128)(2,1)} %collective-permute-done.9.refs_2_), channel_id=1, source_target_pairs={{0,4},{4,0},{8,12},{12,8},{16,20},{20,16},{24,28},{28,24},{1,5},{5... | collective-permute-start | bytes 1990664 | tf_op jit(solution)/shard_map/ppermute | solution.py:83
  65.5 33.8 %collective-permute-start.12 = (bf16[96,3456]{1,0:T(8,128)(2,1)}, bf16[96,3456]{1,0:T(8,128)(2,1)}, u32[]{:S(2)}, u32[]{:S(2)}) collective-permute-start(bf16[96,3456]{1,0:T(8,128)(2,1)} %pack_rest.1.refs_0_), channel_id=1, source_target_pairs={{0,24},{4,28},{8,16},{12,20},{16,8},{20,12},{24,0},{28,4},{1,25},{... | collective-permute-start | bytes 1990664 | tf_op jit(solution)/shard_map/ppermute | solution.py:83
  76.1 24.9 %collective-permute-start.11 = (bf16[96,3456]{1,0:T(8,128)(2,1)}, bf16[96,3456]{1,0:T(8,128)(2,1)}, u32[]{:S(2)}, u32[]{:S(2)}) collective-permute-start(bf16[96,3456]{1,0:T(8,128)(2,1)} %collective-permute-done.5.refs_4_), channel_id=1, source_target_pairs={{0,4},{4,0},{8,12},{12,8},{16,20},{20,16},{24,28},{28,24},{1,5},{5... | collective-permute-start | bytes 1990664 | tf_op jit(solution)/shard_map/ppermute | solution.py:83
  91.1 35.7 %collective-permute-start.14 = (bf16[3,128,384]{2,1,0:T(8,128)(2,1)}, bf16[3,128,384]{2,1,0:T(8,128)(2,1)}, u32[]{:S(2)}, u32[]{:S(2)}) collective-permute-start(bf16[3,128,384]{2,1,0:T(8,128)(2,1)} %get-tuple-element.151.o2), channel_id=1, source_target_pairs={{0,2},{1,3},{2,0},{3,1},{4,6},{5,7},{6,4},{7,5},{8,10},{9,11},{10,... | collective-permute-start | bytes 884744 | tf_op jit(solution)/shard_map/ppermute | solution.py:79
  95.1 20.4 %all-to-all-start.1 = ((f32[8,4,2304]{2,1,0:T(4,128)}), f32[8,4,2304]{2,1,0:T(4,128)}, u32[]{:S(2)}, u32[]{:S(2)}) async-start(f32[8,4,2304]{2,1,0:T(4,128)} %reshape.143), calls=%async_computation.1 | async-start | bytes 589824 | tf_op jit(solution)/shard_map/all_to_all | solution.py:101
  99.3 19.3 %collective-permute-start.16 = (bf16[96,3456]{1,0:T(8,128)(2,1)}, bf16[96,3456]{1,0:T(8,128)(2,1)}, u32[]{:S(2)}, u32[]{:S(2)}) collective-permute-start(bf16[96,3456]{1,0:T(8,128)(2,1)} %collective-permute-done.12.refs_6_), channel_id=1, source_target_pairs={{0,4},{4,0},{8,12},{12,8},{16,20},{20,16},{24,28},{28,24},{1,5},{5... | collective-permute-start | bytes 1990664 | tf_op jit(solution)/shard_map/ppermute | solution.py:83
  101.0 25.7 %collective-permute-start.15 = (bf16[3,128,384]{2,1,0:T(8,128)(2,1)}, bf16[3,128,384]{2,1,0:T(8,128)(2,1)}, u32[]{:S(2)}, u32[]{:S(2)}) collective-permute-start(bf16[3,128,384]{2,1,0:T(8,128)(2,1)} %get-tuple-element.162.o3), channel_id=1, source_target_pairs={{0,3},{1,2},{2,1},{3,0},{4,7},{5,6},{6,5},{7,4},{8,11},{9,10},{10,... | collective-permute-start | bytes 884744 | tf_op jit(solution)/shard_map/ppermute | solution.py:79
  115.4 9.1 %copy-start.25 = (bf16[3,128,384]{2,1,0:T(8,128)(2,1)S(1)}, bf16[3,128,384]{2,1,0:T(8,128)(2,1)}, u32[]{:S(2)}) copy-start(bf16[3,128,384]{2,1,0:T(8,128)(2,1)} %get-tuple-element.161.o1) | copy-start | bytes 884740
  115.4 9.6 %copy-start.24 = (bf16[3,256,768]{2,1,0:T(8,128)(2,1)S(1)}, bf16[3,256,768]{2,1,0:T(8,128)(2,1)}, u32[]{:S(2)}) copy-start(bf16[3,256,768]{2,1,0:T(8,128)(2,1)} %out_grad.1) | copy-start | bytes 3538948
  115.4 10.7 %copy-start.22 = (f32[2304]{0:T(1024)S(1)}, f32[2304]{0:T(1024)}, u32[]{:S(2)}) copy-start(f32[2304]{0:T(1024)} %reduce) | copy-start | bytes 27652
  124.5 3.5 collective-permute-start.17
  124.5 2.7 collective-permute-start.13
  125.0 9.5 %collective-permute-start.19 = (bf16[3,256,768]{2,1,0:T(8,128)(2,1)S(1)}, bf16[3,256,768]{2,1,0:T(8,128)(2,1)}, u32[]{:S(2)}, u32[]{:S(2)}) collective-permute-start(bf16[3,256,768]{2,1,0:T(8,128)(2,1)S(1)} %copy-done.24), channel_id=1, source_target_pairs={{0,1},{1,0},{2,3},{3,2},{4,5},{5,4},{6,7},{7,6},{8,9},{9,8},{10,11... | collective-permute-start | bytes 3538952 | tf_op jit(solution)/shard_map/ppermute | solution.py:79
  134.4 3.2 collective-permute-start.18
  175.9 4.9 %collective-permute-start.20 = (bf16[2,3,256,768]{3,2,1,0:T(8,128)(2,1)}, bf16[2,3,256,768]{3,2,1,0:T(8,128)(2,1)}, u32[]{:S(2)}, u32[]{:S(2)}) collective-permute-start(bf16[2,3,256,768]{3,2,1,0:T(8,128)(2,1)} %get-tuple-element.177), channel_id=1, source_target_pairs={{0,1},{1,0},{2,3},{3,2},{4,5},{5,4},{6,7},{7,6},{8,9},{9,8},{10,11... | collective-permute-start | bytes 7077896 | tf_op jit(solution)/shard_map/ppermute | solution.py:79
  176.1 28.6 %collective-permute-start.22 = (bf16[4,96,1536]{2,1,0:T(8,128)(2,1)}, bf16[4,96,1536]{2,1,0:T(8,128)(2,1)}, u32[]{:S(2)}, u32[]{:S(2)}) collective-permute-start(bf16[4,96,1536]{2,1,0:T(8,128)(2,1)} %get-tuple-element.189), channel_id=1, source_target_pairs={{0,4},{4,0},{8,12},{12,8},{16,20},{20,16},{24,28},{28,24},{1,5},{5... | collective-permute-start | bytes 3538952 | tf_op jit(solution)/shard_map/ppermute | solution.py:83
  193.6 2.8 collective-permute-start.21
  193.8 14.2 %collective-permute-start.23 = (bf16[432,384]{1,0:T(8,128)(2,1)}, bf16[432,384]{1,0:T(8,128)(2,1)S(1)}, u32[]{:S(2)}, u32[]{:S(2)}) collective-permute-start(bf16[432,384]{1,0:T(8,128)(2,1)} %get-tuple-element.198), channel_id=1, source_target_pairs={{0,2},{1,3},{2,0},{3,1},{4,6},{5,7},{6,4},{7,5},{8,10},{9,11},{10,... | collective-permute-start | bytes 995336 | tf_op jit(solution)/shard_map/ppermute | solution.py:79
  194.3 16.3 %collective-permute-start.24 = (bf16[432,384]{1,0:T(8,128)(2,1)}, bf16[432,384]{1,0:T(8,128)(2,1)S(1)}, u32[]{:S(2)}, u32[]{:S(2)}) collective-permute-start(bf16[432,384]{1,0:T(8,128)(2,1)} %get-tuple-element.199), channel_id=1, source_target_pairs={{0,3},{1,2},{2,1},{3,0},{4,7},{5,6},{6,5},{7,4},{8,11},{9,10},{10,... | collective-permute-start | bytes 995336 | tf_op jit(solution)/shard_map/ppermute | solution.py:79
  201.8 51.4 %collective-permute-start.25 = (bf16[4,96,1920]{2,1,0:T(8,128)(2,1)}, bf16[4,96,1920]{2,1,0:T(8,128)(2,1)}, u32[]{:S(2)}, u32[]{:S(2)}) collective-permute-start(bf16[4,96,1920]{2,1,0:T(8,128)(2,1)} %get-tuple-element.187), channel_id=1, source_target_pairs={{0,4},{4,0},{8,12},{12,8},{16,20},{20,16},{24,28},{28,24},{1,5},{5... | collective-permute-start | bytes 4423688 | tf_op jit(solution)/shard_map/ppermute | solution.py:83
  208.0 7.0 %copy-start.12 = (bf16[432,384]{1,0:T(8,128)(2,1)}, bf16[432,384]{1,0:T(8,128)(2,1)S(1)}, u32[]{:S(2)}) copy-start(bf16[432,384]{1,0:T(8,128)(2,1)S(1)} %collective-permute-done.23.g2) | copy-start | bytes 995332
  210.6 4.4 %copy-start.13 = (bf16[432,384]{1,0:T(8,128)(2,1)}, bf16[432,384]{1,0:T(8,128)(2,1)S(1)}, u32[]{:S(2)}) copy-start(bf16[432,384]{1,0:T(8,128)(2,1)S(1)} %collective-permute-done.24.g3) | copy-start | bytes 995332
  210.6 39.8 %collective-permute-start.26 = (bf16[96,1536]{1,0:T(8,128)(2,1)}, bf16[96,1536]{1,0:T(8,128)(2,1)}, u32[]{:S(2)}, u32[]{:S(2)}) collective-permute-start(bf16[96,1536]{1,0:T(8,128)(2,1)} %get-tuple-element.207), channel_id=1, source_target_pairs={{0,8},{4,12},{8,0},{12,4},{16,24},{20,28},{24,16},{28,20},{1,9},{5... | collective-permute-start | bytes 884744 | tf_op jit(solution)/shard_map/ppermute | solution.py:83
  212.1 38.3 %collective-permute-start.27 = (bf16[96,1536]{1,0:T(8,128)(2,1)}, bf16[96,1536]{1,0:T(8,128)(2,1)}, u32[]{:S(2)}, u32[]{:S(2)}) collective-permute-start(bf16[96,1536]{1,0:T(8,128)(2,1)} %get-tuple-element.208), channel_id=1, source_target_pairs={{0,16},{4,20},{8,24},{12,28},{16,0},{20,4},{24,8},{28,12},{1,17},{... | collective-permute-start | bytes 884744 | tf_op jit(solution)/shard_map/ppermute | solution.py:83
  214.5 35.9 %collective-permute-start.28 = (bf16[96,1536]{1,0:T(8,128)(2,1)}, bf16[96,1536]{1,0:T(8,128)(2,1)}, u32[]{:S(2)}, u32[]{:S(2)}) collective-permute-start(bf16[96,1536]{1,0:T(8,128)(2,1)} %get-tuple-element.209), channel_id=1, source_target_pairs={{0,24},{4,28},{8,16},{12,20},{16,8},{20,12},{24,0},{28,4},{1,25},{... | collective-permute-start | bytes 884744 | tf_op jit(solution)/shard_map/ppermute | solution.py:83
  256.9 37.3 %collective-permute-start.29 = (bf16[96,1920]{1,0:T(8,128)(2,1)}, bf16[96,1920]{1,0:T(8,128)(2,1)S(1)}, u32[]{:S(2)}, u32[]{:S(2)}) collective-permute-start(bf16[96,1920]{1,0:T(8,128)(2,1)} %get-tuple-element.203), channel_id=1, source_target_pairs={{0,8},{4,12},{8,0},{12,4},{16,24},{20,28},{24,16},{28,20},{1,9},{5... | collective-permute-start | bytes 1105928 | tf_op jit(solution)/shard_map/ppermute | solution.py:83
  257.5 36.7 %collective-permute-start.30 = (bf16[96,1920]{1,0:T(8,128)(2,1)}, bf16[96,1920]{1,0:T(8,128)(2,1)S(1)}, u32[]{:S(2)}, u32[]{:S(2)}) collective-permute-start(bf16[96,1920]{1,0:T(8,128)(2,1)} %get-tuple-element.204), channel_id=1, source_target_pairs={{0,16},{4,20},{8,24},{12,28},{16,0},{20,4},{24,8},{28,12},{1,17},{... | collective-permute-start | bytes 1105928 | tf_op jit(solution)/shard_map/ppermute | solution.py:83
  260.7 33.4 %collective-permute-start.31 = (bf16[96,1920]{1,0:T(8,128)(2,1)}, bf16[96,1920]{1,0:T(8,128)(2,1)S(1)}, u32[]{:S(2)}, u32[]{:S(2)}) collective-permute-start(bf16[96,1920]{1,0:T(8,128)(2,1)} %get-tuple-element.205), channel_id=1, source_target_pairs={{0,24},{4,28},{8,16},{12,20},{16,8},{20,12},{24,0},{28,4},{1,25},{... | collective-permute-start | bytes 1105928 | tf_op jit(solution)/shard_map/ppermute | solution.py:83
  264.9 34.5 %all-to-all-start.2 = ((f32[8,4,2304]{2,1,0:T(4,128)}), f32[8,4,2304]{2,1,0:T(4,128)S(1)}, u32[]{:S(2)}, u32[]{:S(2)}) async-start(f32[8,4,2304]{2,1,0:T(4,128)} %broadcast_in_dim.51), calls=%async_computation.2 | async-start | bytes 589824 | tf_op jit(solution)/shard_map/all_to_all | solution.py:101
  294.1 5.3 %copy-start.9 = (bf16[96,1920]{1,0:T(8,128)(2,1)}, bf16[96,1920]{1,0:T(8,128)(2,1)S(1)}, u32[]{:S(2)}) copy-start(bf16[96,1920]{1,0:T(8,128)(2,1)S(1)} %collective-permute-done.29.refs_2_) | copy-start | bytes 1105924
  294.2 5.3 %copy-start.10 = (bf16[96,1920]{1,0:T(8,128)(2,1)}, bf16[96,1920]{1,0:T(8,128)(2,1)S(1)}, u32[]{:S(2)}) copy-start(bf16[96,1920]{1,0:T(8,128)(2,1)S(1)} %collective-permute-done.30.refs_3_) | copy-start | bytes 1105924
  294.2 5.3 %copy-start.11 = (bf16[96,1920]{1,0:T(8,128)(2,1)}, bf16[96,1920]{1,0:T(8,128)(2,1)S(1)}, u32[]{:S(2)}) copy-start(bf16[96,1920]{1,0:T(8,128)(2,1)S(1)} %collective-permute-done.31.refs_4_) | copy-start | bytes 1105924
  299.4 3.1 copy-start.5
  302.6 4.9 %collective-permute-start.32 = (bf16[2,3,256,768]{3,2,1,0:T(8,128)(2,1)}, bf16[2,3,256,768]{3,2,1,0:T(8,128)(2,1)}, u32[]{:S(2)}, u32[]{:S(2)}) collective-permute-start(bf16[2,3,256,768]{3,2,1,0:T(8,128)(2,1)} %token_grad.1), channel_id=1, source_target_pairs={{0,1},{1,0},{2,3},{3,2},{4,5},{5,4},{6,7},{7,6},{8,9},{9,8},{10,11... | collective-permute-start | bytes 7077896 | tf_op jit(solution)/shard_map/ppermute | solution.py:79
  302.6 18.7 %collective-permute-start.37 = (bf16[96,3456]{1,0:T(8,128)(2,1)}, bf16[96,3456]{1,0:T(8,128)(2,1)S(1)}, u32[]{:S(2)}, u32[]{:S(2)}) collective-permute-start(bf16[96,3456]{1,0:T(8,128)(2,1)} %gather.4.own), channel_id=1, source_target_pairs={{0,2},{1,3},{2,0},{3,1},{4,6},{5,7},{6,4},{7,5},{8,10},{9,11},{10,... | collective-permute-start | bytes 1990664 | tf_op jit(solution)/shard_map/ppermute | solution.py:79
  303.1 15.4 %collective-permute-start.33 = (bf16[4,112,576]{2,1,0:T(8,128)(2,1)}, bf16[4,112,576]{2,1,0:T(8,128)(2,1)}, u32[]{:S(2)}, u32[]{:S(2)}) collective-permute-start(bf16[4,112,576]{2,1,0:T(8,128)(2,1)} %get-tuple-element.230), channel_id=1, source_target_pairs={{0,4},{4,0},{8,12},{12,8},{16,20},{20,16},{24,28},{28,24},{1,5},{5... | collective-permute-start | bytes 1548296 | tf_op jit(solution)/shard_map/ppermute | solution.py:83
  312.7 8.5 %copy-start.1 = (bf16[96,3456]{1,0:T(8,128)(2,1)S(1)}, bf16[96,3456]{1,0:T(8,128)(2,1)}, u32[]{:S(2)}) copy-start(bf16[96,3456]{1,0:T(8,128)(2,1)} %gather.4.own) | copy-start | bytes 1990660
  321.2 2.8 copy-start.6
  321.2 6.0 %copy-start.27 = (bf16[112,576]{1,0:T(8,128)(2,1)S(1)}, bf16[112,576]{1,0:T(8,128)(2,1)}, u32[]{:S(2)}) copy-start(bf16[112,576]{1,0:T(8,128)(2,1)} %get-tuple-element.234) | copy-start | bytes 387076
  321.3 8.0 %copy-start.15 = (f32[32,96]{1,0:T(8,128)S(1)}, f32[32,96]{1,0:T(8,128)}, u32[]{:S(2)}) copy-start(f32[32,96]{1,0:T(8,128)} %copy-done.14) | copy-start | bytes 36868
  322.5 8.8 %collective-permute-start.38 = (bf16[2,96,3456]{2,1,0:T(8,128)(2,1)}, bf16[2,96,3456]{2,1,0:T(8,128)(2,1)}, u32[]{:S(2)}, u32[]{:S(2)}) collective-permute-start(bf16[2,96,3456]{2,1,0:T(8,128)(2,1)} %pad_maximum_fusion), channel_id=1, source_target_pairs={{0,1},{1,0},{2,3},{3,2},{4,5},{5,4},{6,7},{7,6},{8,9},{9,8},{10,11... | collective-permute-start | bytes 3981320 | tf_op jit(solution)/shard_map/ppermute | solution.py:79
  322.5 29.1 %collective-permute-start.39 = (bf16[3,256,768]{2,1,0:T(8,128)(2,1)}, bf16[3,256,768]{2,1,0:T(8,128)(2,1)}, u32[]{:S(2)}, u32[]{:S(2)}) collective-permute-start(bf16[3,256,768]{2,1,0:T(8,128)(2,1)} %across.1), channel_id=1, source_target_pairs={{0,2},{1,3},{2,0},{3,1},{4,6},{5,7},{6,4},{7,5},{8,10},{9,11},{10,... | collective-permute-start | bytes 3538952 | tf_op jit(solution)/shard_map/ppermute | solution.py:79
  324.2 11.3 %collective-permute-start.34 = (bf16[112,576]{1,0:T(8,128)(2,1)}, bf16[112,576]{1,0:T(8,128)(2,1)S(1)}, u32[]{:S(2)}, u32[]{:S(2)}) collective-permute-start(bf16[112,576]{1,0:T(8,128)(2,1)} %get-tuple-element.232), channel_id=1, source_target_pairs={{0,8},{4,12},{8,0},{12,4},{16,24},{20,28},{24,16},{28,20},{1,9},{5... | collective-permute-start | bytes 387080 | tf_op jit(solution)/shard_map/ppermute | solution.py:83
  324.4 13.9 %collective-permute-start.35 = (bf16[112,576]{1,0:T(8,128)(2,1)}, bf16[112,576]{1,0:T(8,128)(2,1)S(1)}, u32[]{:S(2)}, u32[]{:S(2)}) collective-permute-start(bf16[112,576]{1,0:T(8,128)(2,1)} %get-tuple-element.233), channel_id=1, source_target_pairs={{0,16},{4,20},{8,24},{12,28},{16,0},{20,4},{24,8},{28,12},{1,17},{... | collective-permute-start | bytes 387080 | tf_op jit(solution)/shard_map/ppermute | solution.py:83
  327.2 11.1 %collective-permute-start.36 = (bf16[112,576]{1,0:T(8,128)(2,1)S(1)}, bf16[112,576]{1,0:T(8,128)(2,1)S(1)}, u32[]{:S(2)}, u32[]{:S(2)}) collective-permute-start(bf16[112,576]{1,0:T(8,128)(2,1)S(1)} %copy-done.27), channel_id=1, source_target_pairs={{0,24},{4,28},{8,16},{12,20},{16,8},{20,12},{24,0},{28,4},{1,25},{... | collective-permute-start | bytes 387080 | tf_op jit(solution)/shard_map/ppermute | solution.py:83
  341.5 17.6 %collective-permute-start.40 = (bf16[112,576]{1,0:T(8,128)(2,1)}, bf16[112,576]{1,0:T(8,128)(2,1)S(1)}, u32[]{:S(2)}, u32[]{:S(2)}) collective-permute-start(bf16[112,576]{1,0:T(8,128)(2,1)} %gather.5.own), channel_id=1, source_target_pairs={{0,2},{1,3},{2,0},{3,1},{4,6},{5,7},{6,4},{7,5},{8,10},{9,11},{10,... | collective-permute-start | bytes 387080 | tf_op jit(solution)/shard_map/ppermute | solution.py:79
  342.0 17.1 %collective-permute-start.41 = (bf16[112,576]{1,0:T(8,128)(2,1)}, bf16[112,576]{1,0:T(8,128)(2,1)S(1)}, u32[]{:S(2)}, u32[]{:S(2)}) collective-permute-start(bf16[112,576]{1,0:T(8,128)(2,1)} %gather.5.own), channel_id=1, source_target_pairs={{0,1},{1,0},{2,3},{3,2},{4,5},{5,4},{6,7},{7,6},{8,9},{9,8},{10,11... | collective-permute-start | bytes 387080 | tf_op jit(solution)/shard_map/ppermute | solution.py:79
  342.0 17.1 %collective-permute-start.42 = (bf16[112,576]{1,0:T(8,128)(2,1)}, bf16[112,576]{1,0:T(8,128)(2,1)S(1)}, u32[]{:S(2)}, u32[]{:S(2)}) collective-permute-start(bf16[112,576]{1,0:T(8,128)(2,1)} %gather.5.own), channel_id=1, source_target_pairs={{0,3},{1,2},{2,1},{3,0},{4,7},{5,6},{6,5},{7,4},{8,11},{9,10},{10,... | collective-permute-start | bytes 387080 | tf_op jit(solution)/shard_map/ppermute | solution.py:79
  344.3 19.3 %all-to-all-start.3 = ((f32[8,32,96]{2,1,0:T(8,128)}), f32[8,32,96]{2,1,0:T(8,128)S(1)}, u32[]{:S(2)}, u32[]{:S(2)}) async-start(f32[8,32,96]{2,1,0:T(8,128)} %broadcast_in_dim.52), calls=%async_computation.3 | async-start | bytes 262144 | tf_op jit(solution)/shard_map/all_to_all | solution.py:101
  349.8 14.0 %copy-start.23 = (f32[1,32]{1,0:T(1,128)S(1)}, f32[1,32]{1,0:T(1,128)}, u32[]{:S(2)}) copy-start(f32[1,32]{1,0:T(1,128)} %get-tuple-element.251) | copy-start | bytes 388
  (11 other events, 10.5 us)

commit v2 on v1

--- a/solution.py
+++ b/solution.py
@@ -457,30 +457,17 @@
     )
 
 
-def mlp_kernel(
-    meta,
-    x0,
-    x1,
-    og0,
-    og1,
-    up,
-    up_bias,
-    down,
-    mods,
-    own_branch,
-    own_input,
-    other,
-    up_here,
-    up_away,
-    down_here,
-    down_away,
-    up_bias_grad,
-    up_acc,
-    down_acc,
-):
+def mlp_kernel(ranks, meta, x0, x1, og0, og1, up_bias, mods, *refs):
+    pieces, refs = refs[:ranks], refs[ranks:]
+    own_branch, own_input, other, up_here, up_away, down_here, down_away, *refs = refs
+    up_bias_grad, up_acc, down_acc, up, down = refs
     p, b = pl.program_id(0), pl.program_id(1)
     count = pl.num_programs(1)
     s, i, prefix = meta[0], meta[3], meta[4 + b]
+    @pl.when(jnp.logical_and(p == 0, b == 0))
+    def _():
+        place_ff(meta, pieces, up, down)
+
     rows, width = x0.shape[1:]
     first = p == 0
     x = jnp.where(first, x0[0], x1[0])
@@ -554,16 +541,16 @@
         lax.fori_loop(0, outer, blocks, 0)
 
 
-def mlp_call(meta, x0, x1, og0, og1, up, up_bias, down, mods, ranks):
+def mlp_call(meta, x0, x1, og0, og1, pieces, up_bias, mods):
     count, rows, width = x0.shape
-    hidden = up.shape[1]
+    hidden, ranks = up_bias.shape[1], len(pieces)
     last = count - 1
     block = (1, rows, width)
     first = lambda p, b, m: (jnp.where(p == 0, b, last), 0, 0)
     second = lambda p, b, m: (jnp.where(p == 0, 0, b), 0, 0)
     shared = (ranks // 2, width // ranks, hidden)
     return run(
-        mlp_kernel,
+        functools.partial(mlp_kernel, ranks),
         (2, count),
         meta,
         [
@@ -571,10 +558,9 @@
             (x1, block, second),
             (og0, block, first),
             (og1, block, second),
-            whole(up),
             whole(up_bias),
-            whole(down),
             whole(mods),
+            *(whole(x) for x in pieces),
         ],
         [
             (x0.shape, F32, block, first),
@@ -591,7 +577,12 @@
             out_whole(shared, BF16),
             out_whole((1, hidden), F32),
         ],
-        scratch=[pltpu.VMEM((width, hidden), F32), pltpu.VMEM((hidden, width), F32)],
+        scratch=[
+            pltpu.VMEM((width, hidden), F32),
+            pltpu.VMEM((hidden, width), F32),
+            pltpu.VMEM((width, hidden), BF16),
+            pltpu.VMEM((hidden, width), BF16),
+        ],
         cost=(24 * count * rows * width * hidden, 20 * count * rows * width, 0),
         name="mlp",
     )
@@ -1003,20 +994,24 @@
             out[:, ff + 2 * width :] = proj_out[:, k * width // 2 : (k + 1) * width // 2]
 
 
-def place_rest_kernel(meta, *refs):
-    *pieces, up, down, out = refs
+def place_out_kernel(meta, *refs):
+    *pieces, out = refs
+    d = meta[2]
+    deep = out.shape[0] // len(pieces)
+    for m, piece in enumerate(pieces):
+        out[pl.ds(pl.multiple_of((d ^ m) * deep, deep), deep)] = piece[...]
+
+
+def place_ff(meta, pieces, up, down):
     d = meta[2]
     deep = up.shape[0] // len(pieces)
     ff, width = up.shape[1], down.shape[1]
     for m, piece in enumerate(pieces):
         owner = d ^ m
-        base = pl.multiple_of(owner * deep, deep)
-        up[pl.ds(base, deep)] = piece[:, :ff]
-        out[pl.ds(base, deep)] = piece[:, ff + 2 * width :]
-        base = pl.multiple_of(owner * (2 * deep), deep)
-        down[pl.ds(base, deep)] = piece[:, ff : ff + width]
-        base = pl.multiple_of(owner * (2 * deep) + deep, deep)
-        down[pl.ds(base, deep)] = piece[:, ff + width : ff + 2 * width]
+        up[pl.ds(pl.multiple_of(owner * deep, deep), deep)] = piece[:, :ff]
+        for n in range(2):
+            base = pl.multiple_of(owner * (2 * deep) + n * deep, deep)
+            down[pl.ds(base, deep)] = piece[:, ff + n * width : ff + (n + 1) * width]
 
 
 def half_kernel(meta, here, came, *outs):
@@ -1284,27 +1279,27 @@
     mixed = [mixed_0, mixed_1, mixed_2, mixed_3]
     mixed_own = [mixed_0, seq_swap(mixed_1, 1), across_2, across_3]
     mods = jnp.sum(after(mod_got, mixed_0), axis=0) + ada_bias_full
-    up_w, down_w, out_own = run(
-        place_rest_kernel,
+    pieces = [
+        x for pair in zip([after(pack_rest, mixed_0), *rest_even[1:]], rest_odd) for x in pair
+    ]
+    last_cols = (ff + 2 * width) // half_out
+    out_own = run(
+        place_out_kernel,
         (1,),
         meta,
-        [whole(x) for pair in zip([after(pack_rest, mixed_0), *rest_even[1:]], rest_odd) for x in pair],
-        [
-            out_whole((width, ff), BF16),
-            out_whole((ff, width), BF16),
-            out_whole((width, half_out), BF16),
-        ],
-        name="place_rest",
-    )
+        [(x, (deep, half_out), lambda i, m: (0, last_cols)) for x in pieces],
+        [out_whole((width, half_out), BF16)],
+        name="place_out",
+    )[0]
     out_other = seq_swap(out_own, 1)
-    og_other = seq_swap(after(out_grad, up_w), 1)
+    og_other = seq_swap(after(out_grad, out_own), 1)
 
     residual, mlp_own, out_rel = mix_call(
         meta, mixed_own, tokens, out_own, out_other, out_bias, mods
     )
     mlp_other = seq_swap(mlp_own, 1)
     own_branch, own_input, other, up_here, up_away, down_here, down_away, up_bias_part = mlp_call(
-        meta, mlp_own, mlp_other, out_grad, og_other, up_w, up_b, down_w, mods, ranks
+        meta, mlp_own, mlp_other, out_grad, og_other, pieces, up_b, mods
     )
     got = seq_swap(other, 1)
     up_came = dp_swap(up_away, 1)
@@ -1350,7 +1345,6 @@
     )
     down_half = halves(after(down_here, raw), down_came)
     down_got = spread(down_half)
-    up_sum = gather_call(meta, [after(up_got, raw)])
     row_grad = run(
         rows_kernel,
         (1,),
@@ -1366,7 +1360,7 @@
     grads, in_even, in_odd = proj_grad_call(
         meta,
         (tokens, tok_c, tok_x, tok_d),
-        after(raw, down_half, up_sum, row_grad),
+        after(raw, down_half, up_got, row_grad),
         in_w,
         gain,
         bias,
@@ -1378,7 +1372,7 @@
     )
     in_came = dp_swap(in_odd, 1)
     sent = token_grad_call(meta, grads, in_w, tokens.shape)
-    rest_sum = gather_call(meta, [(up_sum,), after(down_got, sent, rows_got)])
+    rest_sum = gather_call(meta, [up_got, after(down_got, sent, rows_got)])
     came = seq_swap(after(sent, rest_sum), 1)
     rest_x = seq_swap(rest_sum, 2)
     across = across_call(meta, after(grads, rest_sum), in_w, came)

time: 367 us -> 362 us (0.986)
  Pallas kernels: 223 us -> 218 us
    pallas_call x26 -> x25, Pallas kernels: 223 us -> 218 us  [run(): pl.pallas_call(kernel, grid_spec=pltpu.PrefetchScalarGridSpec(num_scalar_...]
where the time goes in v2:
time: 362 us; the launch traced here: 360 us
  Pallas kernels  218 us (60%)
  starting transfers between devices  63.8 us (18%)
  waiting for transfers between devices  49.6 us (14%)
  local copies, waits for them, and re-layouts  14.1 us (4%)
  other arithmetic  10 us (3%)
    pallas_call x25, Pallas kernels, run(): pl.pallas_call(kernel, grid_spec=pltpu.PrefetchScalarGridSpec(num_scalar_...  218 us
    ppermute x23, starting transfers between devices, dp_swap(): lax.ppermute(value, 'dp', [(d, d ^ mask) for d in range(lax.axis_size('dp...  34.6 us
    ppermute x23, waiting for transfers between devices, dp_swap(): lax.ppermute(value, 'dp', [(d, d ^ mask) for d in range(lax.axis_size('dp...  28.8 us
    all_to_all x4, starting transfers between devices, dp_turn(): lax.all_to_all(value, 'dp', split_axis=0, concat_axis=0, tiled=True, axis...  18.8 us
    ppermute x20, waiting for transfers between devices, seq_swap(): lax.ppermute(value, 'seq', [(s, s ^ mask) for s in range(lax.axis_size('s...  15.7 us
    ppermute x20, starting transfers between devices, seq_swap(): lax.ppermute(value, 'seq', [(s, s ^ mask) for s in range(lax.axis_size('s...  10.4 us
  transfers between devices with their start and end apart: 47, of which 15 were waited for; matrix products, arithmetic and copies ran while one was open for 4% of the time, Pallas kernels for 48%

profile of v2, /device:TPU:0, one launch (start us, length us, event | category | flops | bytes accessed | tf_op | source)
XLA Modules:
  0.0 359.8 jit_solution(17356070674212097511)
XLA Ops:
  0.7 1.3 broadcast_in_dim.22.refs_2_
  5.7 2.6 pack_in.1.refs_0_
  8.3 3.0 collective-permute-start
  11.4 2.6 collective-permute-start.1
  14.0 1.7 collective-permute-start.6
  17.6 2.9 pack_rest.1.refs_0_
  20.5 1.9 pad_maximum_fusion.2
  22.4 3.0 collective-permute-done.1.refs_2_
  26.7 1.6 collective-permute-start.4
  28.2 2.2 collective-permute-start.9
  31.5 10.6 %collective-permute-done.4.refs_4_ = bf16[4,112,576]{2,1,0:T(8,128)(2,1)S(1)} collective-permute-done((bf16[4,112,576]{2,1,0:T(8,128)(2,1)S(1)}, bf16[4,112,576]{2,1,0:T(8,128)(2,1)S(1)}, u32[]{:S(2)}, u32[]{:S(2)}) %collective-permute-start.4) | collective-permute-done | bytes 516128 | tf_op jit(solution)/shard_map/ppermute | solution.py:83
  42.9 3.5 place_in.1
  46.4 1.6 collective-permute-start.8
  48.0 4.5 %all-to-all-start = ((bf16[8,32,96]{2,1,0:T(8,128)(2,1)}), bf16[8,32,96]{2,1,0:T(8,128)(2,1)}, u32[]{:S(2)}, u32[]{:S(2)}) async-start(bf16[8,32,96]{2,1,0:T(8,128)(2,1)} %get-tuple-element.145), calls=%async_computation | async-start | bytes 131072 | tf_op jit(solution)/shard_map/all_to_all | solution.py:101
  52.5 1.3 reduce
  53.8 8.4 %qkv.2.qa.refs_0_ = bf16[3,512,576]{2,1,0:T(8,128)(2,1)} custom-call(s32[7]{0:T(128)} %concatenate.13.meta, bf16[3,256,768]{2,1,0:T(8,128)(2,1)} %tokens.3, bf16[3,256,768]{2,1,0:T(8,128)(2,1)} %collective-permute-done.3.x1, f32[1,768]{1,0:T(1,128)} %get-tuple-element.135.gain, f32[1,768]{1,0:T(1,128)} %get-tuple-element.136.bias, ...), custom_call_target="tpu_custom_call" | custom-call | flops 40768634880 | bytes 176947200 | tf_op jit(solution)/shard_map/qkv/pallas_call | solution.py:120
  62.3 1.6 collective-permute-done.8.refs_1_
  63.9 1.6 collective-permute-start.10
  65.5 2.2 collective-permute-start.12
  67.7 8.4 %qkv.3.qb.refs_1_ = bf16[3,512,576]{2,1,0:T(8,128)(2,1)} custom-call(s32[7]{0:T(128)} %concatenate.13.meta, bf16[3,256,768]{2,1,0:T(8,128)(2,1)} %collective-permute-done.6.x0.x2, bf16[3,256,768]{2,1,0:T(8,128)(2,1)} %collective-permute-done.7.x1.x3, f32[1,768]{1,0:T(1,128)} %get-tuple-element.135.gain, f32[1,768]{1,0:T(1,128)} %get-tuple-element.136.bias, ...), custom_call_target="tpu_custom_call" | custom-call | flops 40768634880 | bytes 176947200 | tf_op jit(solution)/shard_map/qkv/pallas_call | solution.py:120
  76.7 14.3 %attend.2 = (bf16[3,128,384]{2,1,0:T(8,128)(2,1)}, bf16[3,128,384]{2,1,0:T(8,128)(2,1)}, bf16[3,3,1024,1024]{3,2,1,0:T(8,128)(2,1)}, f32[3,1024,128]{2,1,0:T(8,128)}) custom-call(s32[7]{0:T(128)} %concatenate.13.meta, bf16[3,512,576]{2,1,0:T(8,128)(2,1)} %qkv.2.qa.refs_0_, bf16[3,512,576]{2,1,0:T(8,128)(2,1)} %qkv.3.qb.refs_1_), custom_call_target="tpu_custom_call" | custom-call | flops 144955146240 | bytes 283115520 | tf_op jit(solution)/shard_map/attend/pallas_call | solution.py:120
  91.0 1.5 collective-permute-start.14
  95.0 4.2 %all-to-all-start.1 = ((f32[8,4,2304]{2,1,0:T(4,128)}), f32[8,4,2304]{2,1,0:T(4,128)}, u32[]{:S(2)}, u32[]{:S(2)}) async-start(f32[8,4,2304]{2,1,0:T(4,128)} %reshape.143), calls=%async_computation.1 | async-start | bytes 589824 | tf_op jit(solution)/shard_map/all_to_all | solution.py:101
  99.3 1.7 collective-permute-start.16
  101.0 14.3 %attend.3 = (bf16[3,128,384]{2,1,0:T(8,128)(2,1)}, bf16[3,128,384]{2,1,0:T(8,128)(2,1)}, bf16[3,3,1024,1024]{3,2,1,0:T(8,128)(2,1)}, f32[3,1024,128]{2,1,0:T(8,128)}) custom-call(s32[7]{0:T(128)} %concatenate.13.meta, bf16[3,512,576]{2,1,0:T(8,128)(2,1)} %qkv.2.qa.refs_0_, ...), custom_call_target="tpu_custom_call", output_to_operand_aliasing={{2}: (3, {}), {3}: (4, {})} | custom-call | flops 144955146240 | bytes 283115520 | tf_op jit(solution)/shard_map/attend/pallas_call | solution.py:120
  115.4 3.3 collective-permute-done.16.refs_7_
  118.6 2.7 place_out.1.w_own
  124.8 6.4 %mix.1 = (f32[3,256,768]{2,1,0:T(8,128)}, bf16[3,256,768]{2,1,0:T(8,128)(2,1)}, bf16[768,768]{1,0:T(8,128)(2,1)}) custom-call(s32[7]{0:T(128)} %concatenate.13.meta, bf16[3,128,384]{2,1,0:T(8,128)(2,1)} %get-tuple-element.153.m0.o0, bf16[3,128,384]{2,1,0:T(8,128)(2,1)} %copy-done.25, bf16[3,128,384]{2,1,0:T(8,128)(2,1)} %collective-permute-done.14.m2, ...), custom_call_target="tpu_custom_call" | custom-call | flops 27179089920 | bytes 212336640 | tf_op jit(solution)/shard_map/mix/pallas_call | solution.py:120
  131.3 3.1 collective-permute-done.18.x1
  134.4 38.7 %mlp.1 = (f32[3,256,768]{2,1,0:T(8,128)}, f32[3,256,768]{2,1,0:T(8,128)}, bf16[2,3,256,768]{3,2,1,0:T(8,128)(2,1)}, bf16[4,96,1536]{2,1,0:T(8,128)(2,1)}, bf16[4...) custom-call(s32[7]{0:T(128)} %concatenate.13.meta, ...), custom_call_target="tpu_custom_call" | custom-call | flops 652298158080 | bytes 353894400 | tf_op jit(solution)/shard_map/mlp/pallas_call | solution.py:120
  174.4 3.7 %collective-permute-done.20.got = bf16[2,3,256,768]{3,2,1,0:T(8,128)(2,1)} collective-permute-done((bf16[2,3,256,768]{3,2,1,0:T(8,128)(2,1)}, bf16[2,3,256,768]{3,2,1,0:T(8,128)(2,1)}, u32[]{:S(2)}, u32[]{:S(2)}) %collective-permute-start.20) | collective-permute-done | bytes 2359328 | tf_op jit(solution)/shard_map/ppermute | solution.py:79
  178.1 12.8 %turn.1 = (bf16[3,256,768]{2,1,0:T(8,128)(2,1)}, f32[3,256,768]{2,1,0:T(8,128)}, bf16[432,384]{1,0:T(8,128)(2,1)}, bf16[1200,384]{1,0:T(8,128)(2,1)}, bf16[432,3...) custom-call(s32[7]{0:T(128)} %concatenate.13.meta, ...), custom_call_target="tpu_custom_call" | custom-call | flops 54358179840 | bytes 424673280 | tf_op jit(solution)/shard_map/turn/pallas_call | solution.py:120
  194.5 4.6 %join.1 = (bf16[4,96,1920]{2,1,0:T(8,128)(2,1)}, bf16[4,96,1920]{2,1,0:T(8,128)(2,1)}) custom-call(s32[7]{0:T(128)} %concatenate.13.meta, bf16[4,96,1536]{2,1,0:T(8,128)(2,1)} %get-tuple-element.173.down_here, bf16[4,96,1536]{2,1,0:T(8,128)(2,1)} %get-tuple-element.174.down_away, bf16[768,384]{1,0:T(8,128)(2,1)} %get-tuple-element.175.out_here, ...), custom_call_target="tpu_custom_call" | custom-call | tf_op jit(solution)/shard_map/join/pallas_call | solution.py:120
  200.2 1.7 collective-permute-done.22.came
  201.9 3.4 half.2
  205.3 2.7 collective-permute-done.24.g3
  208.0 1.5 collective-permute-start.26
  209.5 2.4 collective-permute-start.27
  212.4 35.4 %attend_back.1.raw = bf16[3,1024,576]{2,1,0:T(8,128)(2,1)} custom-call(s32[7]{0:T(128)} %concatenate.13.meta, bf16[3,512,576]{2,1,0:T(8,128)(2,1)} %qkv.2.qa.refs_0_, bf16[3,512,576]{2,1,0:T(8,128)(2,1)} %qkv.3.qb.refs_1_, bf16[3,3,1024,1024]{3,2,1,0:T(8,128)(2,1)} %get-tuple-element.185.weights, f32[3,1024,128]{2,1,0:T(8,128)} %get-tuple-element.186.recips, ...), custom_call_target="tpu_custom_call" | custom-call | flops 579820584960 | bytes 566231040 | tf_op jit(solution)/shard_map/attend_back/pallas_call | solution.py:120
  247.8 3.7 %half.3 = (bf16[96,1920]{1,0:T(8,128)(2,1)}, bf16[96,1920]{1,0:T(8,128)(2,1)}, bf16[96,1920]{1,0:T(8,128)(2,1)}, bf16[96,1920]{1,0:T(8,128)(2,1)}) custom-call(s32[7]{0:T(128)} %concatenate.13.meta, bf16[4,96,1920]{2,1,0:T(8,128)(2,1)} %get-tuple-element.191.here, bf16[4,96,1920]{2,1,0:T(8,128)(2,1)} %collective-permute-done.25.came), custom_call_target="tpu_custom_call" | custom-call | tf_op jit(solution)/shard_map/half/pallas_call | solution.py:120
  252.0 3.3 collective-permute-start.30
  255.3 2.1 rows.1
  258.0 1.5 broadcast_in_dim.51
  259.5 4.6 %all-to-all-start.2 = ((f32[8,4,2304]{2,1,0:T(4,128)}), f32[8,4,2304]{2,1,0:T(4,128)S(1)}, u32[]{:S(2)}, u32[]{:S(2)}) async-start(f32[8,4,2304]{2,1,0:T(4,128)} %broadcast_in_dim.51), calls=%async_computation.2 | async-start | bytes 589824 | tf_op jit(solution)/shard_map/all_to_all | solution.py:101
  264.1 18.7 %proj_grad.1 = (bf16[3,1024,576]{2,1,0:T(8,128)(2,1)}, bf16[4,112,576]{2,1,0:T(8,128)(2,1)}, bf16[4,112,576]{2,1,0:T(8,128)(2,1)}) custom-call(s32[7]{0:T(128)} %concatenate.13.meta, bf16[3,256,768]{2,1,0:T(8,128)(2,1)} %tokens.3, bf16[3,256,768]{2,1,0:T(8,128)(2,1)} %collective-permute-done.3.x1, bf16[3,256,768]{2,1,0:T(8,128)(2,1)} %collective-permute-done.6.x0.x2, ...), custom_call_target="tpu_custom_call" | custom-call | flops 81537269760 | bytes 424673280 | tf_op jit(solution)/shard_map/proj_grad/pallas_call | solution.py:120
  282.8 6.0 %token_grad.1 = bf16[2,3,256,768]{3,2,1,0:T(8,128)(2,1)} custom-call(s32[7]{0:T(128)} %concatenate.13.meta, bf16[3,1024,576]{2,1,0:T(8,128)(2,1)} %get-tuple-element.213.g1.g3.g2.g0, bf16[3,1024,576]{2,1,0:T(8,128)(2,1)} %get-tuple-element.213.g1.g3.g2.g0, bf16[768,576]{1,0:T(8,128)(2,1)} %get-tuple-element.137.w), custom_call_target="tpu_custom_call" | custom-call | tf_op jit(solution)/shard_map/token_grad/pallas_call | solution.py:120
  288.8 5.1 %all-to-all-done.2 = f32[8,4,2304]{2,1,0:T(4,128)S(1)} async-done(((f32[8,4,2304]{2,1,0:T(4,128)}), f32[8,4,2304]{2,1,0:T(4,128)S(1)}, u32[]{:S(2)}, u32[]{:S(2)}) %all-to-all-start.2) | async-done | bytes 294944 | tf_op jit(solution)/shard_map/all_to_all | solution.py:101
  293.9 3.5 gather.2.own
  299.0 3.3 collective-permute-done.32.got
  302.3 5.2 %across.1 = bf16[3,256,768]{2,1,0:T(8,128)(2,1)} custom-call(s32[7]{0:T(128)} %concatenate.13.meta, bf16[3,1024,576]{2,1,0:T(8,128)(2,1)} %get-tuple-element.213.g1.g3.g2.g0, bf16[768,576]{1,0:T(8,128)(2,1)} %get-tuple-element.137.w, bf16[2,3,256,768]{3,2,1,0:T(8,128)(2,1)} %collective-permute-done.32.got), custom_call_target="tpu_custom_call" | custom-call | tf_op jit(solution)/shard_map/across/pallas_call | solution.py:120
  307.5 5.8 %collective-permute-done.33.came = bf16[4,112,576]{2,1,0:T(8,128)(2,1)} collective-permute-done((bf16[4,112,576]{2,1,0:T(8,128)(2,1)}, bf16[4,112,576]{2,1,0:T(8,128)(2,1)}, u32[]{:S(2)}, u32[]{:S(2)}) %collective-permute-start.33) | collective-permute-done | bytes 516128 | tf_op jit(solution)/shard_map/ppermute | solution.py:83
  313.3 2.7 pair.1
  317.3 1.5 collective-permute-start.39
  319.3 2.8 collective-permute-start.35
  322.1 1.4 collective-permute-start.36
  324.1 1.5 fusion.7
  326.1 4.2 %close_rest.1 = (f32[96,3072]{1,0:T(8,128)}, f32[384,768]{1,0:T(8,128)}, f32[96,768]{1,0:T(8,128)}) custom-call(s32[7]{0:T(128)} %concatenate.13.meta, bf16[96,3456]{1,0:T(8,128)(2,1)} %gather.2.own, bf16[96,3456]{1,0:T(8,128)(2,1)} %copy-done.3, bf16[2,96,3456]{2,1,0:T(8,128)(2,1)} %collective-permute-done.38.pair), custom_call_target="tpu_custom_call" | custom-call | tf_op jit(solution)/shard_map/close_rest/pallas_call | solution.py:120
  330.4 2.8 collective-permute-done.35.refs_2_
  333.9 2.5 gather.3.own
  336.8 1.7 collective-permute-start.42
  339.2 5.5 %all-to-all-start.3 = ((f32[8,32,96]{2,1,0:T(8,128)}), f32[8,32,96]{2,1,0:T(8,128)S(1)}, u32[]{:S(2)}, u32[]{:S(2)}) async-start(f32[8,32,96]{2,1,0:T(8,128)} %broadcast_in_dim.52), calls=%async_computation.3 | async-start | bytes 262144 | tf_op jit(solution)/shard_map/all_to_all | solution.py:101
  344.7 1.7 collective-permute-done.39.across
  346.4 7.5 %last.1 = f32[3,256,768]{2,1,0:T(8,128)} custom-call(s32[7]{0:T(128)} %concatenate.13.meta, bf16[3,256,768]{2,1,0:T(8,128)(2,1)} %tokens.3, f32[3,256,768]{2,1,0:T(8,128)} %get-tuple-element.230.resid_grad, bf16[3,1024,576]{2,1,0:T(8,128)(2,1)} %get-tuple-element.213.g1.g3.g2.g0, bf16[768,576]{1,0:T(8,128)(2,1)} %get-tuple-element.137.w, ...), custom_call_target="tpu_custom_call" | custom-call | flops 20384317440 | bytes 353894400 | tf_op jit(solution)/shard_map/last/pallas_call | solution.py:120
  355.3 3.2 close_in.1
  (137 shorter events, 32.0 us)
Async XLA Ops:
  0.6 93.4 %copy-start = (bf16[96,2304]{1,0:T(8,128)(2,1)S(1)}, bf16[96,2304]{1,0:T(8,128)(2,1)}, u32[]{:S(2)}) copy-start(bf16[96,2304]{1,0:T(8,128)(2,1)} %param.30) | copy-start | bytes 1327108
  8.3 14.1 %collective-permute-start = (bf16[112,576]{1,0:T(8,128)(2,1)}, bf16[112,576]{1,0:T(8,128)(2,1)}, u32[]{:S(2)}, u32[]{:S(2)}) collective-permute-start(bf16[112,576]{1,0:T(8,128)(2,1)} %pack_in.1.refs_0_), channel_id=1, source_target_pairs={{0,8},{4,12},{8,0},{12,4},{16,24},{20,28},{24,16},{28,20},{1,9},{5... | collective-permute-start | bytes 387080 | tf_op jit(solution)/shard_map/ppermute | solution.py:83
  11.4 14.0 %collective-permute-start.1 = (bf16[112,576]{1,0:T(8,128)(2,1)}, bf16[112,576]{1,0:T(8,128)(2,1)}, u32[]{:S(2)}, u32[]{:S(2)}) collective-permute-start(bf16[112,576]{1,0:T(8,128)(2,1)} %pack_in.1.refs_0_), channel_id=1, source_target_pairs={{0,16},{4,20},{8,24},{12,28},{16,0},{20,4},{24,8},{28,12},{1,17},{... | collective-permute-start | bytes 387080 | tf_op jit(solution)/shard_map/ppermute | solution.py:83
  14.0 11.5 %collective-permute-start.2 = (bf16[112,576]{1,0:T(8,128)(2,1)}, bf16[112,576]{1,0:T(8,128)(2,1)}, u32[]{:S(2)}, u32[]{:S(2)}) collective-permute-start(bf16[112,576]{1,0:T(8,128)(2,1)} %pack_in.1.refs_0_), channel_id=1, source_target_pairs={{0,24},{4,28},{8,16},{12,20},{16,8},{20,12},{24,0},{28,4},{1,25},{... | collective-permute-start | bytes 387080 | tf_op jit(solution)/shard_map/ppermute | solution.py:83
  14.0 39.9 %collective-permute-start.6 = (bf16[3,256,768]{2,1,0:T(8,128)(2,1)}, bf16[3,256,768]{2,1,0:T(8,128)(2,1)}, u32[]{:S(2)}, u32[]{:S(2)}) collective-permute-start(bf16[3,256,768]{2,1,0:T(8,128)(2,1)} %tokens.3), channel_id=1, source_target_pairs={{0,2},{1,3},{2,0},{3,1},{4,6},{5,7},{6,4},{7,5},{8,10},{9,11},{10,... | collective-permute-start | bytes 3538952 | tf_op jit(solution)/shard_map/ppermute | solution.py:79
  20.5 4.9 %copy-start.4 = (bf16[112,576]{1,0:T(8,128)(2,1)S(1)}, bf16[112,576]{1,0:T(8,128)(2,1)}, u32[]{:S(2)}) copy-start(bf16[112,576]{1,0:T(8,128)(2,1)} %pack_in.1.refs_0_) | copy-start | bytes 387076
  26.6 27.2 %collective-permute-start.3 = (bf16[3,256,768]{2,1,0:T(8,128)(2,1)}, bf16[3,256,768]{2,1,0:T(8,128)(2,1)}, u32[]{:S(2)}, u32[]{:S(2)}) collective-permute-start(bf16[3,256,768]{2,1,0:T(8,128)(2,1)} %tokens.3), channel_id=1, source_target_pairs={{0,1},{1,0},{2,3},{3,2},{4,5},{5,4},{6,7},{7,6},{8,9},{9,8},{10,11... | collective-permute-start | bytes 3538952 | tf_op jit(solution)/shard_map/ppermute | solution.py:79
  26.7 15.4 %collective-permute-start.4 = (bf16[4,112,576]{2,1,0:T(8,128)(2,1)S(1)}, bf16[4,112,576]{2,1,0:T(8,128)(2,1)S(1)}, u32[]{:S(2)}, u32[]{:S(2)}) collective-permute-start(bf16[4,112,576]{2,1,0:T(8,128)(2,1)S(1)} %pad_maximum_fusion.1), channel_id=1, source_target_pairs={{0,4},{4,0},{8,12},{12,8},{16,20},{20,16},{24,28},{28,24},{1,5},{5... | collective-permute-start | bytes 1548296 | tf_op jit(solution)/shard_map/ppermute | solution.py:83
  28.2 35.6 %collective-permute-start.9 = (bf16[96,3456]{1,0:T(8,128)(2,1)}, bf16[96,3456]{1,0:T(8,128)(2,1)}, u32[]{:S(2)}, u32[]{:S(2)}) collective-permute-start(bf16[96,3456]{1,0:T(8,128)(2,1)} %pack_rest.1.refs_0_), channel_id=1, source_target_pairs={{0,8},{4,12},{8,0},{12,4},{16,24},{20,28},{24,16},{28,20},{1,9},{5... | collective-permute-start | bytes 1990664 | tf_op jit(solution)/shard_map/ppermute | solution.py:83
  30.5 33.4 %collective-permute-start.5 = (bf16[96,3456]{1,0:T(8,128)(2,1)}, bf16[96,3456]{1,0:T(8,128)(2,1)}, u32[]{:S(2)}, u32[]{:S(2)}) collective-permute-start(bf16[96,3456]{1,0:T(8,128)(2,1)} %pack_rest.1.refs_0_), channel_id=1, source_target_pairs={{0,16},{4,20},{8,24},{12,28},{16,0},{20,4},{24,8},{28,12},{1,17},{... | collective-permute-start | bytes 1990664 | tf_op jit(solution)/shard_map/ppermute | solution.py:83
  46.4 17.5 %collective-permute-start.8 = (bf16[96,3456]{1,0:T(8,128)(2,1)}, bf16[96,3456]{1,0:T(8,128)(2,1)S(1)}, u32[]{:S(2)}, u32[]{:S(2)}) collective-permute-start(bf16[96,3456]{1,0:T(8,128)(2,1)} %pack_rest.1.refs_0_), channel_id=1, source_target_pairs={{0,4},{4,0},{8,12},{12,8},{16,20},{20,16},{24,28},{28,24},{1,5},{5... | collective-permute-start | bytes 1990664 | tf_op jit(solution)/shard_map/ppermute | solution.py:83
  48.0 44.6 %all-to-all-start = ((bf16[8,32,96]{2,1,0:T(8,128)(2,1)}), bf16[8,32,96]{2,1,0:T(8,128)(2,1)}, u32[]{:S(2)}, u32[]{:S(2)}) async-start(bf16[8,32,96]{2,1,0:T(8,128)(2,1)} %get-tuple-element.145), calls=%async_computation | async-start | bytes 131072 | tf_op jit(solution)/shard_map/all_to_all | solution.py:101
  53.8 13.9 %collective-permute-start.7 = (bf16[3,256,768]{2,1,0:T(8,128)(2,1)}, bf16[3,256,768]{2,1,0:T(8,128)(2,1)}, u32[]{:S(2)}, u32[]{:S(2)}) collective-permute-start(bf16[3,256,768]{2,1,0:T(8,128)(2,1)} %collective-permute-done.6.x0.x2), channel_id=1, source_target_pairs={{0,1},{1,0},{2,3},{3,2},{4,5},{5,4},{6,7},{7,6},{8,9},{9,8},{10,11... | collective-permute-start | bytes 3538952 | tf_op jit(solution)/shard_map/ppermute | solution.py:79
  63.9 12.3 %copy-start.7 = (bf16[96,3456]{1,0:T(8,128)(2,1)}, bf16[96,3456]{1,0:T(8,128)(2,1)S(1)}, u32[]{:S(2)}) copy-start(bf16[96,3456]{1,0:T(8,128)(2,1)S(1)} %collective-permute-done.8.refs_1_) | copy-start | bytes 1990660
  63.9 37.1 %collective-permute-start.10 = (bf16[96,3456]{1,0:T(8,128)(2,1)}, bf16[96,3456]{1,0:T(8,128)(2,1)}, u32[]{:S(2)}, u32[]{:S(2)}) collective-permute-start(bf16[96,3456]{1,0:T(8,128)(2,1)} %collective-permute-done.9.refs_2_), channel_id=1, source_target_pairs={{0,4},{4,0},{8,12},{12,8},{16,20},{20,16},{24,28},{28,24},{1,5},{5... | collective-permute-start | bytes 1990664 | tf_op jit(solution)/shard_map/ppermute | solution.py:83
  65.5 33.8 %collective-permute-start.12 = (bf16[96,3456]{1,0:T(8,128)(2,1)}, bf16[96,3456]{1,0:T(8,128)(2,1)}, u32[]{:S(2)}, u32[]{:S(2)}) collective-permute-start(bf16[96,3456]{1,0:T(8,128)(2,1)} %pack_rest.1.refs_0_), channel_id=1, source_target_pairs={{0,24},{4,28},{8,16},{12,20},{16,8},{20,12},{24,0},{28,4},{1,25},{... | collective-permute-start | bytes 1990664 | tf_op jit(solution)/shard_map/ppermute | solution.py:83
  76.1 24.9 %collective-permute-start.11 = (bf16[96,3456]{1,0:T(8,128)(2,1)}, bf16[96,3456]{1,0:T(8,128)(2,1)}, u32[]{:S(2)}, u32[]{:S(2)}) collective-permute-start(bf16[96,3456]{1,0:T(8,128)(2,1)} %collective-permute-done.5.refs_4_), channel_id=1, source_target_pairs={{0,4},{4,0},{8,12},{12,8},{16,20},{20,16},{24,28},{28,24},{1,5},{5... | collective-permute-start | bytes 1990664 | tf_op jit(solution)/shard_map/ppermute | solution.py:83
  91.0 32.5 %collective-permute-start.14 = (bf16[3,128,384]{2,1,0:T(8,128)(2,1)}, bf16[3,128,384]{2,1,0:T(8,128)(2,1)}, u32[]{:S(2)}, u32[]{:S(2)}) collective-permute-start(bf16[3,128,384]{2,1,0:T(8,128)(2,1)} %get-tuple-element.144.o2), channel_id=1, source_target_pairs={{0,2},{1,3},{2,0},{3,1},{4,6},{5,7},{6,4},{7,5},{8,10},{9,11},{10,... | collective-permute-start | bytes 884744 | tf_op jit(solution)/shard_map/ppermute | solution.py:79
  95.0 20.3 %all-to-all-start.1 = ((f32[8,4,2304]{2,1,0:T(4,128)}), f32[8,4,2304]{2,1,0:T(4,128)}, u32[]{:S(2)}, u32[]{:S(2)}) async-start(f32[8,4,2304]{2,1,0:T(4,128)} %reshape.143), calls=%async_computation.1 | async-start | bytes 589824 | tf_op jit(solution)/shard_map/all_to_all | solution.py:101
  99.3 19.3 %collective-permute-start.16 = (bf16[96,3456]{1,0:T(8,128)(2,1)}, bf16[96,3456]{1,0:T(8,128)(2,1)}, u32[]{:S(2)}, u32[]{:S(2)}) collective-permute-start(bf16[96,3456]{1,0:T(8,128)(2,1)} %collective-permute-done.12.refs_6_), channel_id=1, source_target_pairs={{0,4},{4,0},{8,12},{12,8},{16,20},{20,16},{24,28},{28,24},{1,5},{5... | collective-permute-start | bytes 1990664 | tf_op jit(solution)/shard_map/ppermute | solution.py:83
  101.0 22.6 %collective-permute-start.15 = (bf16[3,128,384]{2,1,0:T(8,128)(2,1)}, bf16[3,128,384]{2,1,0:T(8,128)(2,1)}, u32[]{:S(2)}, u32[]{:S(2)}) collective-permute-start(bf16[3,128,384]{2,1,0:T(8,128)(2,1)} %get-tuple-element.155.o3), channel_id=1, source_target_pairs={{0,3},{1,2},{2,1},{3,0},{4,7},{5,6},{6,5},{7,4},{8,11},{9,10},{10,... | collective-permute-start | bytes 884744 | tf_op jit(solution)/shard_map/ppermute | solution.py:79
  115.4 6.0 %copy-start.24 = (bf16[3,128,384]{2,1,0:T(8,128)(2,1)S(1)}, bf16[3,128,384]{2,1,0:T(8,128)(2,1)}, u32[]{:S(2)}) copy-start(bf16[3,128,384]{2,1,0:T(8,128)(2,1)} %get-tuple-element.154.o1) | copy-start | bytes 884740
  115.4 6.5 %copy-start.23 = (bf16[3,256,768]{2,1,0:T(8,128)(2,1)S(1)}, bf16[3,256,768]{2,1,0:T(8,128)(2,1)}, u32[]{:S(2)}) copy-start(bf16[3,256,768]{2,1,0:T(8,128)(2,1)} %out_grad.1) | copy-start | bytes 3538948
  115.4 7.6 %copy-start.21 = (f32[2304]{0:T(1024)S(1)}, f32[2304]{0:T(1024)}, u32[]{:S(2)}) copy-start(f32[2304]{0:T(1024)} %reduce) | copy-start | bytes 27652
  121.3 3.5 collective-permute-start.17
  121.3 2.7 collective-permute-start.13
  121.8 9.5 %collective-permute-start.19 = (bf16[3,256,768]{2,1,0:T(8,128)(2,1)S(1)}, bf16[3,256,768]{2,1,0:T(8,128)(2,1)}, u32[]{:S(2)}, u32[]{:S(2)}) collective-permute-start(bf16[3,256,768]{2,1,0:T(8,128)(2,1)S(1)} %copy-done.23), channel_id=1, source_target_pairs={{0,1},{1,0},{2,3},{3,2},{4,5},{5,4},{6,7},{7,6},{8,9},{9,8},{10,11... | collective-permute-start | bytes 3538952 | tf_op jit(solution)/shard_map/ppermute | solution.py:79
  131.2 3.2 collective-permute-start.18
  173.1 4.9 %collective-permute-start.20 = (bf16[2,3,256,768]{3,2,1,0:T(8,128)(2,1)}, bf16[2,3,256,768]{3,2,1,0:T(8,128)(2,1)}, u32[]{:S(2)}, u32[]{:S(2)}) collective-permute-start(bf16[2,3,256,768]{3,2,1,0:T(8,128)(2,1)} %get-tuple-element.167), channel_id=1, source_target_pairs={{0,1},{1,0},{2,3},{3,2},{4,5},{5,4},{6,7},{7,6},{8,9},{9,8},{10,11... | collective-permute-start | bytes 7077896 | tf_op jit(solution)/shard_map/ppermute | solution.py:79
  173.3 28.6 %collective-permute-start.22 = (bf16[4,96,1536]{2,1,0:T(8,128)(2,1)}, bf16[4,96,1536]{2,1,0:T(8,128)(2,1)}, u32[]{:S(2)}, u32[]{:S(2)}) collective-permute-start(bf16[4,96,1536]{2,1,0:T(8,128)(2,1)} %get-tuple-element.179), channel_id=1, source_target_pairs={{0,4},{4,0},{8,12},{12,8},{16,20},{20,16},{24,28},{28,24},{1,5},{5... | collective-permute-start | bytes 3538952 | tf_op jit(solution)/shard_map/ppermute | solution.py:83
  190.8 2.8 collective-permute-start.21
  191.0 14.3 %collective-permute-start.23 = (bf16[432,384]{1,0:T(8,128)(2,1)}, bf16[432,384]{1,0:T(8,128)(2,1)S(1)}, u32[]{:S(2)}, u32[]{:S(2)}) collective-permute-start(bf16[432,384]{1,0:T(8,128)(2,1)} %get-tuple-element.188), channel_id=1, source_target_pairs={{0,2},{1,3},{2,0},{3,1},{4,6},{5,7},{6,4},{7,5},{8,10},{9,11},{10,... | collective-permute-start | bytes 995336 | tf_op jit(solution)/shard_map/ppermute | solution.py:79
  191.5 16.4 %collective-permute-start.24 = (bf16[432,384]{1,0:T(8,128)(2,1)}, bf16[432,384]{1,0:T(8,128)(2,1)}, u32[]{:S(2)}, u32[]{:S(2)}) collective-permute-start(bf16[432,384]{1,0:T(8,128)(2,1)} %get-tuple-element.189), channel_id=1, source_target_pairs={{0,3},{1,2},{2,1},{3,0},{4,7},{5,6},{6,5},{7,4},{8,11},{9,10},{10,... | collective-permute-start | bytes 995336 | tf_op jit(solution)/shard_map/ppermute | solution.py:79
  199.1 48.7 %collective-permute-start.25 = (bf16[4,96,1920]{2,1,0:T(8,128)(2,1)}, bf16[4,96,1920]{2,1,0:T(8,128)(2,1)}, u32[]{:S(2)}, u32[]{:S(2)}) collective-permute-start(bf16[4,96,1920]{2,1,0:T(8,128)(2,1)} %get-tuple-element.177), channel_id=1, source_target_pairs={{0,4},{4,0},{8,12},{12,8},{16,20},{20,16},{24,28},{28,24},{1,5},{5... | collective-permute-start | bytes 4423688 | tf_op jit(solution)/shard_map/ppermute | solution.py:83
  205.3 7.1 %copy-start.12 = (bf16[432,384]{1,0:T(8,128)(2,1)}, bf16[432,384]{1,0:T(8,128)(2,1)S(1)}, u32[]{:S(2)}) copy-start(bf16[432,384]{1,0:T(8,128)(2,1)S(1)} %collective-permute-done.23.g2) | copy-start | bytes 995332
  208.0 49.5 %collective-permute-start.26 = (bf16[96,1536]{1,0:T(8,128)(2,1)}, bf16[96,1536]{1,0:T(8,128)(2,1)}, u32[]{:S(2)}, u32[]{:S(2)}) collective-permute-start(bf16[96,1536]{1,0:T(8,128)(2,1)} %get-tuple-element.197), channel_id=1, source_target_pairs={{0,8},{4,12},{8,0},{12,4},{16,24},{20,28},{24,16},{28,20},{1,9},{5... | collective-permute-start | bytes 884744 | tf_op jit(solution)/shard_map/ppermute | solution.py:83
  209.5 48.5 %collective-permute-start.27 = (bf16[96,1536]{1,0:T(8,128)(2,1)}, bf16[96,1536]{1,0:T(8,128)(2,1)}, u32[]{:S(2)}, u32[]{:S(2)}) collective-permute-start(bf16[96,1536]{1,0:T(8,128)(2,1)} %get-tuple-element.198), channel_id=1, source_target_pairs={{0,16},{4,20},{8,24},{12,28},{16,0},{20,4},{24,8},{28,12},{1,17},{... | collective-permute-start | bytes 884744 | tf_op jit(solution)/shard_map/ppermute | solution.py:83
  211.9 46.1 %collective-permute-start.28 = (bf16[96,1536]{1,0:T(8,128)(2,1)}, bf16[96,1536]{1,0:T(8,128)(2,1)}, u32[]{:S(2)}, u32[]{:S(2)}) collective-permute-start(bf16[96,1536]{1,0:T(8,128)(2,1)} %get-tuple-element.199), channel_id=1, source_target_pairs={{0,24},{4,28},{8,16},{12,20},{16,8},{20,12},{24,0},{28,4},{1,25},{... | collective-permute-start | bytes 884744 | tf_op jit(solution)/shard_map/ppermute | solution.py:83
  251.5 37.3 %collective-permute-start.29 = (bf16[96,1920]{1,0:T(8,128)(2,1)}, bf16[96,1920]{1,0:T(8,128)(2,1)S(1)}, u32[]{:S(2)}, u32[]{:S(2)}) collective-permute-start(bf16[96,1920]{1,0:T(8,128)(2,1)} %get-tuple-element.193), channel_id=1, source_target_pairs={{0,8},{4,12},{8,0},{12,4},{16,24},{20,28},{24,16},{28,20},{1,9},{5... | collective-permute-start | bytes 1105928 | tf_op jit(solution)/shard_map/ppermute | solution.py:83
  252.0 36.7 %collective-permute-start.30 = (bf16[96,1920]{1,0:T(8,128)(2,1)}, bf16[96,1920]{1,0:T(8,128)(2,1)S(1)}, u32[]{:S(2)}, u32[]{:S(2)}) collective-permute-start(bf16[96,1920]{1,0:T(8,128)(2,1)} %get-tuple-element.194), channel_id=1, source_target_pairs={{0,16},{4,20},{8,24},{12,28},{16,0},{20,4},{24,8},{28,12},{1,17},{... | collective-permute-start | bytes 1105928 | tf_op jit(solution)/shard_map/ppermute | solution.py:83
  257.5 31.3 %collective-permute-start.31 = (bf16[96,1920]{1,0:T(8,128)(2,1)}, bf16[96,1920]{1,0:T(8,128)(2,1)S(1)}, u32[]{:S(2)}, u32[]{:S(2)}) collective-permute-start(bf16[96,1920]{1,0:T(8,128)(2,1)} %get-tuple-element.195), channel_id=1, source_target_pairs={{0,24},{4,28},{8,16},{12,20},{16,8},{20,12},{24,0},{28,4},{1,25},{... | collective-permute-start | bytes 1105928 | tf_op jit(solution)/shard_map/ppermute | solution.py:83
  259.5 34.4 %all-to-all-start.2 = ((f32[8,4,2304]{2,1,0:T(4,128)}), f32[8,4,2304]{2,1,0:T(4,128)S(1)}, u32[]{:S(2)}, u32[]{:S(2)}) async-start(f32[8,4,2304]{2,1,0:T(4,128)} %broadcast_in_dim.51), calls=%async_computation.2 | async-start | bytes 589824 | tf_op jit(solution)/shard_map/all_to_all | solution.py:101
  288.8 5.1 %copy-start.9 = (bf16[96,1920]{1,0:T(8,128)(2,1)}, bf16[96,1920]{1,0:T(8,128)(2,1)S(1)}, u32[]{:S(2)}) copy-start(bf16[96,1920]{1,0:T(8,128)(2,1)S(1)} %collective-permute-done.29.refs_5_) | copy-start | bytes 1105924
  288.8 5.1 %copy-start.10 = (bf16[96,1920]{1,0:T(8,128)(2,1)}, bf16[96,1920]{1,0:T(8,128)(2,1)S(1)}, u32[]{:S(2)}) copy-start(bf16[96,1920]{1,0:T(8,128)(2,1)S(1)} %collective-permute-done.30.refs_6_) | copy-start | bytes 1105924
  288.8 5.1 %copy-start.11 = (bf16[96,1920]{1,0:T(8,128)(2,1)}, bf16[96,1920]{1,0:T(8,128)(2,1)S(1)}, u32[]{:S(2)}) copy-start(bf16[96,1920]{1,0:T(8,128)(2,1)S(1)} %collective-permute-done.31.refs_7_) | copy-start | bytes 1105924
  293.9 3.5 copy-start.5
  297.4 4.9 %collective-permute-start.32 = (bf16[2,3,256,768]{3,2,1,0:T(8,128)(2,1)}, bf16[2,3,256,768]{3,2,1,0:T(8,128)(2,1)}, u32[]{:S(2)}, u32[]{:S(2)}) collective-permute-start(bf16[2,3,256,768]{3,2,1,0:T(8,128)(2,1)} %token_grad.1), channel_id=1, source_target_pairs={{0,1},{1,0},{2,3},{3,2},{4,5},{5,4},{6,7},{7,6},{8,9},{9,8},{10,11... | collective-permute-start | bytes 7077896 | tf_op jit(solution)/shard_map/ppermute | solution.py:79
  297.4 18.6 %collective-permute-start.37 = (bf16[96,3456]{1,0:T(8,128)(2,1)}, bf16[96,3456]{1,0:T(8,128)(2,1)S(1)}, u32[]{:S(2)}, u32[]{:S(2)}) collective-permute-start(bf16[96,3456]{1,0:T(8,128)(2,1)} %gather.2.own), channel_id=1, source_target_pairs={{0,2},{1,3},{2,0},{3,1},{4,6},{5,7},{6,4},{7,5},{8,10},{9,11},{10,... | collective-permute-start | bytes 1990664 | tf_op jit(solution)/shard_map/ppermute | solution.py:79
  298.0 15.4 %collective-permute-start.33 = (bf16[4,112,576]{2,1,0:T(8,128)(2,1)}, bf16[4,112,576]{2,1,0:T(8,128)(2,1)}, u32[]{:S(2)}, u32[]{:S(2)}) collective-permute-start(bf16[4,112,576]{2,1,0:T(8,128)(2,1)} %get-tuple-element.216), channel_id=1, source_target_pairs={{0,4},{4,0},{8,12},{12,8},{16,20},{20,16},{24,28},{28,24},{1,5},{5... | collective-permute-start | bytes 1548296 | tf_op jit(solution)/shard_map/ppermute | solution.py:83
  307.5 8.5 %copy-start.1 = (bf16[96,3456]{1,0:T(8,128)(2,1)S(1)}, bf16[96,3456]{1,0:T(8,128)(2,1)}, u32[]{:S(2)}) copy-start(bf16[96,3456]{1,0:T(8,128)(2,1)} %gather.2.own) | copy-start | bytes 1990660
  316.1 2.8 copy-start.6
  316.1 6.0 %copy-start.26 = (bf16[112,576]{1,0:T(8,128)(2,1)S(1)}, bf16[112,576]{1,0:T(8,128)(2,1)}, u32[]{:S(2)}) copy-start(bf16[112,576]{1,0:T(8,128)(2,1)} %get-tuple-element.220) | copy-start | bytes 387076
  316.1 8.1 %copy-start.14 = (f32[32,96]{1,0:T(8,128)S(1)}, f32[32,96]{1,0:T(8,128)}, u32[]{:S(2)}) copy-start(f32[32,96]{1,0:T(8,128)} %copy-done.13) | copy-start | bytes 36868
  317.3 8.8 %collective-permute-start.38 = (bf16[2,96,3456]{2,1,0:T(8,128)(2,1)}, bf16[2,96,3456]{2,1,0:T(8,128)(2,1)}, u32[]{:S(2)}, u32[]{:S(2)}) collective-permute-start(bf16[2,96,3456]{2,1,0:T(8,128)(2,1)} %pad_maximum_fusion), channel_id=1, source_target_pairs={{0,1},{1,0},{2,3},{3,2},{4,5},{5,4},{6,7},{7,6},{8,9},{9,8},{10,11... | collective-permute-start | bytes 3981320 | tf_op jit(solution)/shard_map/ppermute | solution.py:79
  317.3 29.1 %collective-permute-start.39 = (bf16[3,256,768]{2,1,0:T(8,128)(2,1)}, bf16[3,256,768]{2,1,0:T(8,128)(2,1)}, u32[]{:S(2)}, u32[]{:S(2)}) collective-permute-start(bf16[3,256,768]{2,1,0:T(8,128)(2,1)} %across.1), channel_id=1, source_target_pairs={{0,2},{1,3},{2,0},{3,1},{4,6},{5,7},{6,4},{7,5},{8,10},{9,11},{10,... | collective-permute-start | bytes 3538952 | tf_op jit(solution)/shard_map/ppermute | solution.py:79
  319.0 11.3 %collective-permute-start.34 = (bf16[112,576]{1,0:T(8,128)(2,1)}, bf16[112,576]{1,0:T(8,128)(2,1)S(1)}, u32[]{:S(2)}, u32[]{:S(2)}) collective-permute-start(bf16[112,576]{1,0:T(8,128)(2,1)} %get-tuple-element.218), channel_id=1, source_target_pairs={{0,8},{4,12},{8,0},{12,4},{16,24},{20,28},{24,16},{28,20},{1,9},{5... | collective-permute-start | bytes 387080 | tf_op jit(solution)/shard_map/ppermute | solution.py:83
  319.3 13.9 %collective-permute-start.35 = (bf16[112,576]{1,0:T(8,128)(2,1)}, bf16[112,576]{1,0:T(8,128)(2,1)S(1)}, u32[]{:S(2)}, u32[]{:S(2)}) collective-permute-start(bf16[112,576]{1,0:T(8,128)(2,1)} %get-tuple-element.219), channel_id=1, source_target_pairs={{0,16},{4,20},{8,24},{12,28},{16,0},{20,4},{24,8},{28,12},{1,17},{... | collective-permute-start | bytes 387080 | tf_op jit(solution)/shard_map/ppermute | solution.py:83
  322.1 11.1 %collective-permute-start.36 = (bf16[112,576]{1,0:T(8,128)(2,1)S(1)}, bf16[112,576]{1,0:T(8,128)(2,1)S(1)}, u32[]{:S(2)}, u32[]{:S(2)}) collective-permute-start(bf16[112,576]{1,0:T(8,128)(2,1)S(1)} %copy-done.26), channel_id=1, source_target_pairs={{0,24},{4,28},{8,16},{12,20},{16,8},{20,12},{24,0},{28,4},{1,25},{... | collective-permute-start | bytes 387080 | tf_op jit(solution)/shard_map/ppermute | solution.py:83
  330.4 2.8 copy-start.17
  336.4 17.5 %collective-permute-start.40 = (bf16[112,576]{1,0:T(8,128)(2,1)}, bf16[112,576]{1,0:T(8,128)(2,1)S(1)}, u32[]{:S(2)}, u32[]{:S(2)}) collective-permute-start(bf16[112,576]{1,0:T(8,128)(2,1)} %gather.3.own), channel_id=1, source_target_pairs={{0,2},{1,3},{2,0},{3,1},{4,6},{5,7},{6,4},{7,5},{8,10},{9,11},{10,... | collective-permute-start | bytes 387080 | tf_op jit(solution)/shard_map/ppermute | solution.py:79
  336.8 17.1 %collective-permute-start.41 = (bf16[112,576]{1,0:T(8,128)(2,1)}, bf16[112,576]{1,0:T(8,128)(2,1)S(1)}, u32[]{:S(2)}, u32[]{:S(2)}) collective-permute-start(bf16[112,576]{1,0:T(8,128)(2,1)} %gather.3.own), channel_id=1, source_target_pairs={{0,1},{1,0},{2,3},{3,2},{4,5},{5,4},{6,7},{7,6},{8,9},{9,8},{10,11... | collective-permute-start | bytes 387080 | tf_op jit(solution)/shard_map/ppermute | solution.py:79
  336.8 17.1 %collective-permute-start.42 = (bf16[112,576]{1,0:T(8,128)(2,1)}, bf16[112,576]{1,0:T(8,128)(2,1)S(1)}, u32[]{:S(2)}, u32[]{:S(2)}) collective-permute-start(bf16[112,576]{1,0:T(8,128)(2,1)} %gather.3.own), channel_id=1, source_target_pairs={{0,3},{1,2},{2,1},{3,0},{4,7},{5,6},{6,5},{7,4},{8,11},{9,10},{10,... | collective-permute-start | bytes 387080 | tf_op jit(solution)/shard_map/ppermute | solution.py:79
  339.2 19.3 %all-to-all-start.3 = ((f32[8,32,96]{2,1,0:T(8,128)}), f32[8,32,96]{2,1,0:T(8,128)S(1)}, u32[]{:S(2)}, u32[]{:S(2)}) async-start(f32[8,32,96]{2,1,0:T(8,128)} %broadcast_in_dim.52), calls=%async_computation.3 | async-start | bytes 262144 | tf_op jit(solution)/shard_map/all_to_all | solution.py:101
  344.7 14.0 %copy-start.22 = (f32[1,32]{1,0:T(1,128)S(1)}, f32[1,32]{1,0:T(1,128)}, u32[]{:S(2)}) copy-start(f32[1,32]{1,0:T(1,128)} %get-tuple-element.237) | copy-start | bytes 388
  (10 other events, 7.7 us)

commit v3 on v2

--- a/solution.py
+++ b/solution.py
@@ -909,8 +909,8 @@
                 out[:deep, t * hw : (t + 1) * hw] = proj_in[:, start : start + hw]
 
     out[deep:] = jnp.zeros((out.shape[0] - deep, cols), BF16)
-    steps = vectors.pop()[...]
-    vectors = [v[...].astype(F32) for v in vectors]
+    steps = vectors.pop()[...][None]
+    vectors = [v[...].astype(F32)[None] for v in vectors]
     vectors += [(steps >> 5).astype(F32), (steps & 31).astype(F32)]
     vec = jnp.concatenate(vectors, axis=1)
     size = vec.shape[1]
@@ -1199,7 +1199,7 @@
         pack_in_kernel,
         (1,),
         meta,
-        [whole(proj_in), *(whole(v[None]) for v in vectors)],
+        [whole(proj_in), *(whole(v) for v in vectors)],
         [out_whole((deep + EXTRA, 3 * hw), BF16)],
         name="pack_in",
     )[0]

time: 362 us -> 358 us (0.989)
  local copies, waits for them, and re-layouts: 14.1 us -> 10.4 us
    broadcast_in_dim x3 -> x0, local copies, waits for them, and re-layouts: 3.78 us -> none  [shards(): v[None]]
  transfers between devices with their start and end apart: 47 -> 47, of which waited for: 15 -> 15; matrix products, arithmetic and copies ran while one was open for 4% -> 4% of each run, Pallas kernels for 48% -> 49%
where the time goes in v3:
time: 358 us; the launch traced here: 356 us
  Pallas kernels  218 us (61%)
  starting transfers between devices  63.8 us (18%)
  waiting for transfers between devices  49.6 us (14%)
  local copies, waits for them, and re-layouts  10.4 us (3%)
  other arithmetic  10 us (3%)
    pallas_call x25, Pallas kernels, run(): pl.pallas_call(kernel, grid_spec=pltpu.PrefetchScalarGridSpec(num_scalar_...  218 us
    ppermute x23, starting transfers between devices, dp_swap(): lax.ppermute(value, 'dp', [(d, d ^ mask) for d in range(lax.axis_size('dp...  34.6 us
    ppermute x23, waiting for transfers between devices, dp_swap(): lax.ppermute(value, 'dp', [(d, d ^ mask) for d in range(lax.axis_size('dp...  28.8 us
    all_to_all x4, starting transfers between devices, dp_turn(): lax.all_to_all(value, 'dp', split_axis=0, concat_axis=0, tiled=True, axis...  18.8 us
    ppermute x20, waiting for transfers between devices, seq_swap(): lax.ppermute(value, 'seq', [(s, s ^ mask) for s in range(lax.axis_size('s...  15.7 us
    ppermute x20, starting transfers between devices, seq_swap(): lax.ppermute(value, 'seq', [(s, s ^ mask) for s in range(lax.axis_size('s...  10.4 us
  transfers between devices with their start and end apart: 47, of which 15 were waited for; matrix products, arithmetic and copies ran while one was open for 4% of the time, Pallas kernels for 49%

profile of v3, /device:TPU:0, one launch (start us, length us, event | category | flops | bytes accessed | tf_op | source)
XLA Modules:
  0.0 356.0 jit_solution(16527533399713084957)
XLA Ops:
  0.7 1.3 concatenate.13.meta
  2.0 2.6 pack_in.1.refs_0_
  4.6 3.0 collective-permute-start
  7.6 2.6 collective-permute-start.1
  10.2 1.7 collective-permute-start.6
  13.9 2.9 pack_rest.1.refs_0_
  16.8 1.9 pad_maximum_fusion.2
  18.7 3.0 collective-permute-done.1.refs_2_
  22.9 1.6 collective-permute-start.4
  24.5 2.2 collective-permute-start.9
  27.8 10.6 %collective-permute-done.4.refs_4_ = bf16[4,112,576]{2,1,0:T(8,128)(2,1)S(1)} collective-permute-done((bf16[4,112,576]{2,1,0:T(8,128)(2,1)S(1)}, bf16[4,112,576]{2,1,0:T(8,128)(2,1)S(1)}, u32[]{:S(2)}, u32[]{:S(2)}) %collective-permute-start.4) | collective-permute-done | bytes 516128 | tf_op jit(solution)/shard_map/ppermute | solution.py:83
  39.1 3.5 place_in.1
  42.7 1.6 collective-permute-start.8
  44.2 4.5 %all-to-all-start = ((bf16[8,32,96]{2,1,0:T(8,128)(2,1)}), bf16[8,32,96]{2,1,0:T(8,128)(2,1)}, u32[]{:S(2)}, u32[]{:S(2)}) async-start(bf16[8,32,96]{2,1,0:T(8,128)(2,1)} %get-tuple-element.145), calls=%async_computation | async-start | bytes 131072 | tf_op jit(solution)/shard_map/all_to_all | solution.py:101
  48.8 1.3 reduce
  50.1 8.4 %qkv.2.qa.refs_0_ = bf16[3,512,576]{2,1,0:T(8,128)(2,1)} custom-call(s32[7]{0:T(128)} %concatenate.13.meta, bf16[3,256,768]{2,1,0:T(8,128)(2,1)} %tokens.3, bf16[3,256,768]{2,1,0:T(8,128)(2,1)} %collective-permute-done.3.x1, f32[1,768]{1,0:T(1,128)} %get-tuple-element.135.gain, f32[1,768]{1,0:T(1,128)} %get-tuple-element.136.bias, ...), custom_call_target="tpu_custom_call" | custom-call | flops 40768634880 | bytes 176947200 | tf_op jit(solution)/shard_map/qkv/pallas_call | solution.py:120
  58.5 1.6 collective-permute-done.8.refs_1_
  60.2 1.6 collective-permute-start.10
  61.8 2.2 collective-permute-start.12
  64.0 8.4 %qkv.3.qb.refs_1_ = bf16[3,512,576]{2,1,0:T(8,128)(2,1)} custom-call(s32[7]{0:T(128)} %concatenate.13.meta, bf16[3,256,768]{2,1,0:T(8,128)(2,1)} %collective-permute-done.6.x0.x2, bf16[3,256,768]{2,1,0:T(8,128)(2,1)} %collective-permute-done.7.x1.x3, f32[1,768]{1,0:T(1,128)} %get-tuple-element.135.gain, f32[1,768]{1,0:T(1,128)} %get-tuple-element.136.bias, ...), custom_call_target="tpu_custom_call" | custom-call | flops 40768634880 | bytes 176947200 | tf_op jit(solution)/shard_map/qkv/pallas_call | solution.py:120
  73.0 14.3 %attend.2 = (bf16[3,128,384]{2,1,0:T(8,128)(2,1)}, bf16[3,128,384]{2,1,0:T(8,128)(2,1)}, bf16[3,3,1024,1024]{3,2,1,0:T(8,128)(2,1)}, f32[3,1024,128]{2,1,0:T(8,128)}) custom-call(s32[7]{0:T(128)} %concatenate.13.meta, bf16[3,512,576]{2,1,0:T(8,128)(2,1)} %qkv.2.qa.refs_0_, bf16[3,512,576]{2,1,0:T(8,128)(2,1)} %qkv.3.qb.refs_1_), custom_call_target="tpu_custom_call" | custom-call | flops 144955146240 | bytes 283115520 | tf_op jit(solution)/shard_map/attend/pallas_call | solution.py:120
  87.3 1.5 collective-permute-start.14
  91.3 4.2 %all-to-all-start.1 = ((f32[8,4,2304]{2,1,0:T(4,128)}), f32[8,4,2304]{2,1,0:T(4,128)}, u32[]{:S(2)}, u32[]{:S(2)}) async-start(f32[8,4,2304]{2,1,0:T(4,128)} %reshape.143), calls=%async_computation.1 | async-start | bytes 589824 | tf_op jit(solution)/shard_map/all_to_all | solution.py:101
  95.6 1.7 collective-permute-start.16
  97.3 14.3 %attend.3 = (bf16[3,128,384]{2,1,0:T(8,128)(2,1)}, bf16[3,128,384]{2,1,0:T(8,128)(2,1)}, bf16[3,3,1024,1024]{3,2,1,0:T(8,128)(2,1)}, f32[3,1024,128]{2,1,0:T(8,128)}) custom-call(s32[7]{0:T(128)} %concatenate.13.meta, bf16[3,512,576]{2,1,0:T(8,128)(2,1)} %qkv.2.qa.refs_0_, ...), custom_call_target="tpu_custom_call", output_to_operand_aliasing={{2}: (3, {}), {3}: (4, {})} | custom-call | flops 144955146240 | bytes 283115520 | tf_op jit(solution)/shard_map/attend/pallas_call | solution.py:120
  111.7 3.3 collective-permute-done.16.refs_7_
  114.9 2.7 place_out.1.w_own
  121.0 6.4 %mix.1 = (f32[3,256,768]{2,1,0:T(8,128)}, bf16[3,256,768]{2,1,0:T(8,128)(2,1)}, bf16[768,768]{1,0:T(8,128)(2,1)}) custom-call(s32[7]{0:T(128)} %concatenate.13.meta, bf16[3,128,384]{2,1,0:T(8,128)(2,1)} %get-tuple-element.153.m0.o0, bf16[3,128,384]{2,1,0:T(8,128)(2,1)} %copy-done.25, bf16[3,128,384]{2,1,0:T(8,128)(2,1)} %collective-permute-done.14.m2, ...), custom_call_target="tpu_custom_call" | custom-call | flops 27179089920 | bytes 212336640 | tf_op jit(solution)/shard_map/mix/pallas_call | solution.py:120
  127.6 3.1 collective-permute-done.18.x1
  130.7 38.7 %mlp.1 = (f32[3,256,768]{2,1,0:T(8,128)}, f32[3,256,768]{2,1,0:T(8,128)}, bf16[2,3,256,768]{3,2,1,0:T(8,128)(2,1)}, bf16[4,96,1536]{2,1,0:T(8,128)(2,1)}, bf16[4...) custom-call(s32[7]{0:T(128)} %concatenate.13.meta, ...), custom_call_target="tpu_custom_call" | custom-call | flops 652298158080 | bytes 353894400 | tf_op jit(solution)/shard_map/mlp/pallas_call | solution.py:120
  170.7 3.7 %collective-permute-done.20.got = bf16[2,3,256,768]{3,2,1,0:T(8,128)(2,1)} collective-permute-done((bf16[2,3,256,768]{3,2,1,0:T(8,128)(2,1)}, bf16[2,3,256,768]{3,2,1,0:T(8,128)(2,1)}, u32[]{:S(2)}, u32[]{:S(2)}) %collective-permute-start.20) | collective-permute-done | bytes 2359328 | tf_op jit(solution)/shard_map/ppermute | solution.py:79
  174.4 12.8 %turn.1 = (bf16[3,256,768]{2,1,0:T(8,128)(2,1)}, f32[3,256,768]{2,1,0:T(8,128)}, bf16[432,384]{1,0:T(8,128)(2,1)}, bf16[1200,384]{1,0:T(8,128)(2,1)}, bf16[432,3...) custom-call(s32[7]{0:T(128)} %concatenate.13.meta, ...), custom_call_target="tpu_custom_call" | custom-call | flops 54358179840 | bytes 424673280 | tf_op jit(solution)/shard_map/turn/pallas_call | solution.py:120
  190.8 4.6 %join.1 = (bf16[4,96,1920]{2,1,0:T(8,128)(2,1)}, bf16[4,96,1920]{2,1,0:T(8,128)(2,1)}) custom-call(s32[7]{0:T(128)} %concatenate.13.meta, bf16[4,96,1536]{2,1,0:T(8,128)(2,1)} %get-tuple-element.173.down_here, bf16[4,96,1536]{2,1,0:T(8,128)(2,1)} %get-tuple-element.174.down_away, bf16[768,384]{1,0:T(8,128)(2,1)} %get-tuple-element.175.out_here, ...), custom_call_target="tpu_custom_call" | custom-call | tf_op jit(solution)/shard_map/join/pallas_call | solution.py:120
  196.4 1.7 collective-permute-done.22.came
  198.2 3.4 half.2
  201.6 2.7 collective-permute-done.24.g3
  204.3 1.5 collective-permute-start.26
  205.7 2.4 collective-permute-start.27
  208.7 35.4 %attend_back.1.raw = bf16[3,1024,576]{2,1,0:T(8,128)(2,1)} custom-call(s32[7]{0:T(128)} %concatenate.13.meta, bf16[3,512,576]{2,1,0:T(8,128)(2,1)} %qkv.2.qa.refs_0_, bf16[3,512,576]{2,1,0:T(8,128)(2,1)} %qkv.3.qb.refs_1_, bf16[3,3,1024,1024]{3,2,1,0:T(8,128)(2,1)} %get-tuple-element.185.weights, f32[3,1024,128]{2,1,0:T(8,128)} %get-tuple-element.186.recips, ...), custom_call_target="tpu_custom_call" | custom-call | flops 579820584960 | bytes 566231040 | tf_op jit(solution)/shard_map/attend_back/pallas_call | solution.py:120
  244.1 3.7 %half.3 = (bf16[96,1920]{1,0:T(8,128)(2,1)}, bf16[96,1920]{1,0:T(8,128)(2,1)}, bf16[96,1920]{1,0:T(8,128)(2,1)}, bf16[96,1920]{1,0:T(8,128)(2,1)}) custom-call(s32[7]{0:T(128)} %concatenate.13.meta, bf16[4,96,1920]{2,1,0:T(8,128)(2,1)} %get-tuple-element.191.here, bf16[4,96,1920]{2,1,0:T(8,128)(2,1)} %collective-permute-done.25.came), custom_call_target="tpu_custom_call" | custom-call | tf_op jit(solution)/shard_map/half/pallas_call | solution.py:120
  248.3 3.3 collective-permute-start.30
  251.6 2.1 rows.1
  254.3 1.5 broadcast_in_dim.4
  255.8 4.6 %all-to-all-start.2 = ((f32[8,4,2304]{2,1,0:T(4,128)}), f32[8,4,2304]{2,1,0:T(4,128)S(1)}, u32[]{:S(2)}, u32[]{:S(2)}) async-start(f32[8,4,2304]{2,1,0:T(4,128)} %broadcast_in_dim.4), calls=%async_computation.2 | async-start | bytes 589824 | tf_op jit(solution)/shard_map/all_to_all | solution.py:101
  260.4 18.7 %proj_grad.1 = (bf16[3,1024,576]{2,1,0:T(8,128)(2,1)}, bf16[4,112,576]{2,1,0:T(8,128)(2,1)}, bf16[4,112,576]{2,1,0:T(8,128)(2,1)}) custom-call(s32[7]{0:T(128)} %concatenate.13.meta, bf16[3,256,768]{2,1,0:T(8,128)(2,1)} %tokens.3, bf16[3,256,768]{2,1,0:T(8,128)(2,1)} %collective-permute-done.3.x1, bf16[3,256,768]{2,1,0:T(8,128)(2,1)} %collective-permute-done.6.x0.x2, ...), custom_call_target="tpu_custom_call" | custom-call | flops 81537269760 | bytes 424673280 | tf_op jit(solution)/shard_map/proj_grad/pallas_call | solution.py:120
  279.1 6.0 %token_grad.1 = bf16[2,3,256,768]{3,2,1,0:T(8,128)(2,1)} custom-call(s32[7]{0:T(128)} %concatenate.13.meta, bf16[3,1024,576]{2,1,0:T(8,128)(2,1)} %get-tuple-element.213.g1.g3.g2.g0, bf16[3,1024,576]{2,1,0:T(8,128)(2,1)} %get-tuple-element.213.g1.g3.g2.g0, bf16[768,576]{1,0:T(8,128)(2,1)} %get-tuple-element.137.w), custom_call_target="tpu_custom_call" | custom-call | tf_op jit(solution)/shard_map/token_grad/pallas_call | solution.py:120
  285.1 5.1 %all-to-all-done.2 = f32[8,4,2304]{2,1,0:T(4,128)S(1)} async-done(((f32[8,4,2304]{2,1,0:T(4,128)}), f32[8,4,2304]{2,1,0:T(4,128)S(1)}, u32[]{:S(2)}, u32[]{:S(2)}) %all-to-all-start.2) | async-done | bytes 294944 | tf_op jit(solution)/shard_map/all_to_all | solution.py:101
  290.2 3.5 gather.2.own
  295.3 3.3 collective-permute-done.32.got
  298.6 5.2 %across.1 = bf16[3,256,768]{2,1,0:T(8,128)(2,1)} custom-call(s32[7]{0:T(128)} %concatenate.13.meta, bf16[3,1024,576]{2,1,0:T(8,128)(2,1)} %get-tuple-element.213.g1.g3.g2.g0, bf16[768,576]{1,0:T(8,128)(2,1)} %get-tuple-element.137.w, bf16[2,3,256,768]{3,2,1,0:T(8,128)(2,1)} %collective-permute-done.32.got), custom_call_target="tpu_custom_call" | custom-call | tf_op jit(solution)/shard_map/across/pallas_call | solution.py:120
  303.8 5.8 %collective-permute-done.33.came = bf16[4,112,576]{2,1,0:T(8,128)(2,1)} collective-permute-done((bf16[4,112,576]{2,1,0:T(8,128)(2,1)}, bf16[4,112,576]{2,1,0:T(8,128)(2,1)}, u32[]{:S(2)}, u32[]{:S(2)}) %collective-permute-start.33) | collective-permute-done | bytes 516128 | tf_op jit(solution)/shard_map/ppermute | solution.py:83
  309.6 2.7 pair.1
  313.6 1.5 collective-permute-start.39
  315.5 2.8 collective-permute-start.35
  318.3 1.4 collective-permute-start.36
  320.4 1.5 fusion.7
  322.4 4.2 %close_rest.1 = (f32[96,3072]{1,0:T(8,128)}, f32[384,768]{1,0:T(8,128)}, f32[96,768]{1,0:T(8,128)}) custom-call(s32[7]{0:T(128)} %concatenate.13.meta, bf16[96,3456]{1,0:T(8,128)(2,1)} %gather.2.own, bf16[96,3456]{1,0:T(8,128)(2,1)} %copy-done.3, bf16[2,96,3456]{2,1,0:T(8,128)(2,1)} %collective-permute-done.38.pair), custom_call_target="tpu_custom_call" | custom-call | tf_op jit(solution)/shard_map/close_rest/pallas_call | solution.py:120
  326.6 2.8 collective-permute-done.35.refs_2_
  330.1 2.5 gather.3.own
  333.1 1.7 collective-permute-start.42
  335.4 5.5 %all-to-all-start.3 = ((f32[8,32,96]{2,1,0:T(8,128)}), f32[8,32,96]{2,1,0:T(8,128)S(1)}, u32[]{:S(2)}, u32[]{:S(2)}) async-start(f32[8,32,96]{2,1,0:T(8,128)} %broadcast_in_dim.5), calls=%async_computation.3 | async-start | bytes 262144 | tf_op jit(solution)/shard_map/all_to_all | solution.py:101
  341.0 1.7 collective-permute-done.39.across
  342.7 7.5 %last.1 = f32[3,256,768]{2,1,0:T(8,128)} custom-call(s32[7]{0:T(128)} %concatenate.13.meta, bf16[3,256,768]{2,1,0:T(8,128)(2,1)} %tokens.3, f32[3,256,768]{2,1,0:T(8,128)} %get-tuple-element.230.resid_grad, bf16[3,1024,576]{2,1,0:T(8,128)(2,1)} %get-tuple-element.213.g1.g3.g2.g0, bf16[768,576]{1,0:T(8,128)(2,1)} %get-tuple-element.137.w, ...), custom_call_target="tpu_custom_call" | custom-call | flops 20384317440 | bytes 353894400 | tf_op jit(solution)/shard_map/last/pallas_call | solution.py:120
  351.5 3.2 close_in.1
  (134 shorter events, 28.2 us)
Async XLA Ops:
  0.6 89.7 %copy-start = (bf16[96,2304]{1,0:T(8,128)(2,1)S(1)}, bf16[96,2304]{1,0:T(8,128)(2,1)}, u32[]{:S(2)}) copy-start(bf16[96,2304]{1,0:T(8,128)(2,1)} %param.30) | copy-start | bytes 1327108
  4.6 14.1 %collective-permute-start = (bf16[112,576]{1,0:T(8,128)(2,1)}, bf16[112,576]{1,0:T(8,128)(2,1)}, u32[]{:S(2)}, u32[]{:S(2)}) collective-permute-start(bf16[112,576]{1,0:T(8,128)(2,1)} %pack_in.1.refs_0_), channel_id=1, source_target_pairs={{0,8},{4,12},{8,0},{12,4},{16,24},{20,28},{24,16},{28,20},{1,9},{5... | collective-permute-start | bytes 387080 | tf_op jit(solution)/shard_map/ppermute | solution.py:83
  7.6 14.0 %collective-permute-start.1 = (bf16[112,576]{1,0:T(8,128)(2,1)}, bf16[112,576]{1,0:T(8,128)(2,1)}, u32[]{:S(2)}, u32[]{:S(2)}) collective-permute-start(bf16[112,576]{1,0:T(8,128)(2,1)} %pack_in.1.refs_0_), channel_id=1, source_target_pairs={{0,16},{4,20},{8,24},{12,28},{16,0},{20,4},{24,8},{28,12},{1,17},{... | collective-permute-start | bytes 387080 | tf_op jit(solution)/shard_map/ppermute | solution.py:83
  10.2 11.5 %collective-permute-start.2 = (bf16[112,576]{1,0:T(8,128)(2,1)}, bf16[112,576]{1,0:T(8,128)(2,1)}, u32[]{:S(2)}, u32[]{:S(2)}) collective-permute-start(bf16[112,576]{1,0:T(8,128)(2,1)} %pack_in.1.refs_0_), channel_id=1, source_target_pairs={{0,24},{4,28},{8,16},{12,20},{16,8},{20,12},{24,0},{28,4},{1,25},{... | collective-permute-start | bytes 387080 | tf_op jit(solution)/shard_map/ppermute | solution.py:83
  10.2 39.9 %collective-permute-start.6 = (bf16[3,256,768]{2,1,0:T(8,128)(2,1)}, bf16[3,256,768]{2,1,0:T(8,128)(2,1)}, u32[]{:S(2)}, u32[]{:S(2)}) collective-permute-start(bf16[3,256,768]{2,1,0:T(8,128)(2,1)} %tokens.3), channel_id=1, source_target_pairs={{0,2},{1,3},{2,0},{3,1},{4,6},{5,7},{6,4},{7,5},{8,10},{9,11},{10,... | collective-permute-start | bytes 3538952 | tf_op jit(solution)/shard_map/ppermute | solution.py:79
  16.8 4.9 %copy-start.4 = (bf16[112,576]{1,0:T(8,128)(2,1)S(1)}, bf16[112,576]{1,0:T(8,128)(2,1)}, u32[]{:S(2)}) copy-start(bf16[112,576]{1,0:T(8,128)(2,1)} %pack_in.1.refs_0_) | copy-start | bytes 387076
  22.9 27.2 %collective-permute-start.3 = (bf16[3,256,768]{2,1,0:T(8,128)(2,1)}, bf16[3,256,768]{2,1,0:T(8,128)(2,1)}, u32[]{:S(2)}, u32[]{:S(2)}) collective-permute-start(bf16[3,256,768]{2,1,0:T(8,128)(2,1)} %tokens.3), channel_id=1, source_target_pairs={{0,1},{1,0},{2,3},{3,2},{4,5},{5,4},{6,7},{7,6},{8,9},{9,8},{10,11... | collective-permute-start | bytes 3538952 | tf_op jit(solution)/shard_map/ppermute | solution.py:79
  22.9 15.4 %collective-permute-start.4 = (bf16[4,112,576]{2,1,0:T(8,128)(2,1)S(1)}, bf16[4,112,576]{2,1,0:T(8,128)(2,1)S(1)}, u32[]{:S(2)}, u32[]{:S(2)}) collective-permute-start(bf16[4,112,576]{2,1,0:T(8,128)(2,1)S(1)} %pad_maximum_fusion.1), channel_id=1, source_target_pairs={{0,4},{4,0},{8,12},{12,8},{16,20},{20,16},{24,28},{28,24},{1,5},{5... | collective-permute-start | bytes 1548296 | tf_op jit(solution)/shard_map/ppermute | solution.py:83
  24.5 35.6 %collective-permute-start.9 = (bf16[96,3456]{1,0:T(8,128)(2,1)}, bf16[96,3456]{1,0:T(8,128)(2,1)}, u32[]{:S(2)}, u32[]{:S(2)}) collective-permute-start(bf16[96,3456]{1,0:T(8,128)(2,1)} %pack_rest.1.refs_0_), channel_id=1, source_target_pairs={{0,8},{4,12},{8,0},{12,4},{16,24},{20,28},{24,16},{28,20},{1,9},{5... | collective-permute-start | bytes 1990664 | tf_op jit(solution)/shard_map/ppermute | solution.py:83
  26.8 33.4 %collective-permute-start.5 = (bf16[96,3456]{1,0:T(8,128)(2,1)}, bf16[96,3456]{1,0:T(8,128)(2,1)}, u32[]{:S(2)}, u32[]{:S(2)}) collective-permute-start(bf16[96,3456]{1,0:T(8,128)(2,1)} %pack_rest.1.refs_0_), channel_id=1, source_target_pairs={{0,16},{4,20},{8,24},{12,28},{16,0},{20,4},{24,8},{28,12},{1,17},{... | collective-permute-start | bytes 1990664 | tf_op jit(solution)/shard_map/ppermute | solution.py:83
  42.7 17.5 %collective-permute-start.8 = (bf16[96,3456]{1,0:T(8,128)(2,1)}, bf16[96,3456]{1,0:T(8,128)(2,1)S(1)}, u32[]{:S(2)}, u32[]{:S(2)}) collective-permute-start(bf16[96,3456]{1,0:T(8,128)(2,1)} %pack_rest.1.refs_0_), channel_id=1, source_target_pairs={{0,4},{4,0},{8,12},{12,8},{16,20},{20,16},{24,28},{28,24},{1,5},{5... | collective-permute-start | bytes 1990664 | tf_op jit(solution)/shard_map/ppermute | solution.py:83
  44.2 44.6 %all-to-all-start = ((bf16[8,32,96]{2,1,0:T(8,128)(2,1)}), bf16[8,32,96]{2,1,0:T(8,128)(2,1)}, u32[]{:S(2)}, u32[]{:S(2)}) async-start(bf16[8,32,96]{2,1,0:T(8,128)(2,1)} %get-tuple-element.145), calls=%async_computation | async-start | bytes 131072 | tf_op jit(solution)/shard_map/all_to_all | solution.py:101
  50.1 13.9 %collective-permute-start.7 = (bf16[3,256,768]{2,1,0:T(8,128)(2,1)}, bf16[3,256,768]{2,1,0:T(8,128)(2,1)}, u32[]{:S(2)}, u32[]{:S(2)}) collective-permute-start(bf16[3,256,768]{2,1,0:T(8,128)(2,1)} %collective-permute-done.6.x0.x2), channel_id=1, source_target_pairs={{0,1},{1,0},{2,3},{3,2},{4,5},{5,4},{6,7},{7,6},{8,9},{9,8},{10,11... | collective-permute-start | bytes 3538952 | tf_op jit(solution)/shard_map/ppermute | solution.py:79
  60.2 12.3 %copy-start.7 = (bf16[96,3456]{1,0:T(8,128)(2,1)}, bf16[96,3456]{1,0:T(8,128)(2,1)S(1)}, u32[]{:S(2)}) copy-start(bf16[96,3456]{1,0:T(8,128)(2,1)S(1)} %collective-permute-done.8.refs_1_) | copy-start | bytes 1990660
  60.2 37.1 %collective-permute-start.10 = (bf16[96,3456]{1,0:T(8,128)(2,1)}, bf16[96,3456]{1,0:T(8,128)(2,1)}, u32[]{:S(2)}, u32[]{:S(2)}) collective-permute-start(bf16[96,3456]{1,0:T(8,128)(2,1)} %collective-permute-done.9.refs_2_), channel_id=1, source_target_pairs={{0,4},{4,0},{8,12},{12,8},{16,20},{20,16},{24,28},{28,24},{1,5},{5... | collective-permute-start | bytes 1990664 | tf_op jit(solution)/shard_map/ppermute | solution.py:83
  61.8 33.8 %collective-permute-start.12 = (bf16[96,3456]{1,0:T(8,128)(2,1)}, bf16[96,3456]{1,0:T(8,128)(2,1)}, u32[]{:S(2)}, u32[]{:S(2)}) collective-permute-start(bf16[96,3456]{1,0:T(8,128)(2,1)} %pack_rest.1.refs_0_), channel_id=1, source_target_pairs={{0,24},{4,28},{8,16},{12,20},{16,8},{20,12},{24,0},{28,4},{1,25},{... | collective-permute-start | bytes 1990664 | tf_op jit(solution)/shard_map/ppermute | solution.py:83
  72.4 24.9 %collective-permute-start.11 = (bf16[96,3456]{1,0:T(8,128)(2,1)}, bf16[96,3456]{1,0:T(8,128)(2,1)}, u32[]{:S(2)}, u32[]{:S(2)}) collective-permute-start(bf16[96,3456]{1,0:T(8,128)(2,1)} %collective-permute-done.5.refs_4_), channel_id=1, source_target_pairs={{0,4},{4,0},{8,12},{12,8},{16,20},{20,16},{24,28},{28,24},{1,5},{5... | collective-permute-start | bytes 1990664 | tf_op jit(solution)/shard_map/ppermute | solution.py:83
  87.3 32.5 %collective-permute-start.14 = (bf16[3,128,384]{2,1,0:T(8,128)(2,1)}, bf16[3,128,384]{2,1,0:T(8,128)(2,1)}, u32[]{:S(2)}, u32[]{:S(2)}) collective-permute-start(bf16[3,128,384]{2,1,0:T(8,128)(2,1)} %get-tuple-element.144.o2), channel_id=1, source_target_pairs={{0,2},{1,3},{2,0},{3,1},{4,6},{5,7},{6,4},{7,5},{8,10},{9,11},{10,... | collective-permute-start | bytes 884744 | tf_op jit(solution)/shard_map/ppermute | solution.py:79
  91.3 20.3 %all-to-all-start.1 = ((f32[8,4,2304]{2,1,0:T(4,128)}), f32[8,4,2304]{2,1,0:T(4,128)}, u32[]{:S(2)}, u32[]{:S(2)}) async-start(f32[8,4,2304]{2,1,0:T(4,128)} %reshape.143), calls=%async_computation.1 | async-start | bytes 589824 | tf_op jit(solution)/shard_map/all_to_all | solution.py:101
  95.6 19.3 %collective-permute-start.16 = (bf16[96,3456]{1,0:T(8,128)(2,1)}, bf16[96,3456]{1,0:T(8,128)(2,1)}, u32[]{:S(2)}, u32[]{:S(2)}) collective-permute-start(bf16[96,3456]{1,0:T(8,128)(2,1)} %collective-permute-done.12.refs_6_), channel_id=1, source_target_pairs={{0,4},{4,0},{8,12},{12,8},{16,20},{20,16},{24,28},{28,24},{1,5},{5... | collective-permute-start | bytes 1990664 | tf_op jit(solution)/shard_map/ppermute | solution.py:83
  97.3 22.6 %collective-permute-start.15 = (bf16[3,128,384]{2,1,0:T(8,128)(2,1)}, bf16[3,128,384]{2,1,0:T(8,128)(2,1)}, u32[]{:S(2)}, u32[]{:S(2)}) collective-permute-start(bf16[3,128,384]{2,1,0:T(8,128)(2,1)} %get-tuple-element.155.o3), channel_id=1, source_target_pairs={{0,3},{1,2},{2,1},{3,0},{4,7},{5,6},{6,5},{7,4},{8,11},{9,10},{10,... | collective-permute-start | bytes 884744 | tf_op jit(solution)/shard_map/ppermute | solution.py:79
  111.6 6.0 %copy-start.24 = (bf16[3,128,384]{2,1,0:T(8,128)(2,1)S(1)}, bf16[3,128,384]{2,1,0:T(8,128)(2,1)}, u32[]{:S(2)}) copy-start(bf16[3,128,384]{2,1,0:T(8,128)(2,1)} %get-tuple-element.154.o1) | copy-start | bytes 884740
  111.6 6.5 %copy-start.23 = (bf16[3,256,768]{2,1,0:T(8,128)(2,1)S(1)}, bf16[3,256,768]{2,1,0:T(8,128)(2,1)}, u32[]{:S(2)}) copy-start(bf16[3,256,768]{2,1,0:T(8,128)(2,1)} %out_grad.1) | copy-start | bytes 3538948
  111.6 7.6 %copy-start.21 = (f32[2304]{0:T(1024)S(1)}, f32[2304]{0:T(1024)}, u32[]{:S(2)}) copy-start(f32[2304]{0:T(1024)} %reduce) | copy-start | bytes 27652
  117.6 3.5 collective-permute-start.17
  117.6 2.7 collective-permute-start.13
  118.1 9.5 %collective-permute-start.19 = (bf16[3,256,768]{2,1,0:T(8,128)(2,1)S(1)}, bf16[3,256,768]{2,1,0:T(8,128)(2,1)}, u32[]{:S(2)}, u32[]{:S(2)}) collective-permute-start(bf16[3,256,768]{2,1,0:T(8,128)(2,1)S(1)} %copy-done.23), channel_id=1, source_target_pairs={{0,1},{1,0},{2,3},{3,2},{4,5},{5,4},{6,7},{7,6},{8,9},{9,8},{10,11... | collective-permute-start | bytes 3538952 | tf_op jit(solution)/shard_map/ppermute | solution.py:79
  127.5 3.2 collective-permute-start.18
  169.4 4.9 %collective-permute-start.20 = (bf16[2,3,256,768]{3,2,1,0:T(8,128)(2,1)}, bf16[2,3,256,768]{3,2,1,0:T(8,128)(2,1)}, u32[]{:S(2)}, u32[]{:S(2)}) collective-permute-start(bf16[2,3,256,768]{3,2,1,0:T(8,128)(2,1)} %get-tuple-element.167), channel_id=1, source_target_pairs={{0,1},{1,0},{2,3},{3,2},{4,5},{5,4},{6,7},{7,6},{8,9},{9,8},{10,11... | collective-permute-start | bytes 7077896 | tf_op jit(solution)/shard_map/ppermute | solution.py:79
  169.6 28.6 %collective-permute-start.22 = (bf16[4,96,1536]{2,1,0:T(8,128)(2,1)}, bf16[4,96,1536]{2,1,0:T(8,128)(2,1)}, u32[]{:S(2)}, u32[]{:S(2)}) collective-permute-start(bf16[4,96,1536]{2,1,0:T(8,128)(2,1)} %get-tuple-element.179), channel_id=1, source_target_pairs={{0,4},{4,0},{8,12},{12,8},{16,20},{20,16},{24,28},{28,24},{1,5},{5... | collective-permute-start | bytes 3538952 | tf_op jit(solution)/shard_map/ppermute | solution.py:83
  187.1 2.8 collective-permute-start.21
  187.3 14.3 %collective-permute-start.23 = (bf16[432,384]{1,0:T(8,128)(2,1)}, bf16[432,384]{1,0:T(8,128)(2,1)S(1)}, u32[]{:S(2)}, u32[]{:S(2)}) collective-permute-start(bf16[432,384]{1,0:T(8,128)(2,1)} %get-tuple-element.188), channel_id=1, source_target_pairs={{0,2},{1,3},{2,0},{3,1},{4,6},{5,7},{6,4},{7,5},{8,10},{9,11},{10,... | collective-permute-start | bytes 995336 | tf_op jit(solution)/shard_map/ppermute | solution.py:79
  187.8 16.4 %collective-permute-start.24 = (bf16[432,384]{1,0:T(8,128)(2,1)}, bf16[432,384]{1,0:T(8,128)(2,1)}, u32[]{:S(2)}, u32[]{:S(2)}) collective-permute-start(bf16[432,384]{1,0:T(8,128)(2,1)} %get-tuple-element.189), channel_id=1, source_target_pairs={{0,3},{1,2},{2,1},{3,0},{4,7},{5,6},{6,5},{7,4},{8,11},{9,10},{10,... | collective-permute-start | bytes 995336 | tf_op jit(solution)/shard_map/ppermute | solution.py:79
  195.4 48.7 %collective-permute-start.25 = (bf16[4,96,1920]{2,1,0:T(8,128)(2,1)}, bf16[4,96,1920]{2,1,0:T(8,128)(2,1)}, u32[]{:S(2)}, u32[]{:S(2)}) collective-permute-start(bf16[4,96,1920]{2,1,0:T(8,128)(2,1)} %get-tuple-element.177), channel_id=1, source_target_pairs={{0,4},{4,0},{8,12},{12,8},{16,20},{20,16},{24,28},{28,24},{1,5},{5... | collective-permute-start | bytes 4423688 | tf_op jit(solution)/shard_map/ppermute | solution.py:83
  201.6 7.1 %copy-start.12 = (bf16[432,384]{1,0:T(8,128)(2,1)}, bf16[432,384]{1,0:T(8,128)(2,1)S(1)}, u32[]{:S(2)}) copy-start(bf16[432,384]{1,0:T(8,128)(2,1)S(1)} %collective-permute-done.23.g2) | copy-start | bytes 995332
  204.3 49.5 %collective-permute-start.26 = (bf16[96,1536]{1,0:T(8,128)(2,1)}, bf16[96,1536]{1,0:T(8,128)(2,1)}, u32[]{:S(2)}, u32[]{:S(2)}) collective-permute-start(bf16[96,1536]{1,0:T(8,128)(2,1)} %get-tuple-element.197), channel_id=1, source_target_pairs={{0,8},{4,12},{8,0},{12,4},{16,24},{20,28},{24,16},{28,20},{1,9},{5... | collective-permute-start | bytes 884744 | tf_op jit(solution)/shard_map/ppermute | solution.py:83
  205.7 48.5 %collective-permute-start.27 = (bf16[96,1536]{1,0:T(8,128)(2,1)}, bf16[96,1536]{1,0:T(8,128)(2,1)}, u32[]{:S(2)}, u32[]{:S(2)}) collective-permute-start(bf16[96,1536]{1,0:T(8,128)(2,1)} %get-tuple-element.198), channel_id=1, source_target_pairs={{0,16},{4,20},{8,24},{12,28},{16,0},{20,4},{24,8},{28,12},{1,17},{... | collective-permute-start | bytes 884744 | tf_op jit(solution)/shard_map/ppermute | solution.py:83
  208.2 46.1 %collective-permute-start.28 = (bf16[96,1536]{1,0:T(8,128)(2,1)}, bf16[96,1536]{1,0:T(8,128)(2,1)}, u32[]{:S(2)}, u32[]{:S(2)}) collective-permute-start(bf16[96,1536]{1,0:T(8,128)(2,1)} %get-tuple-element.199), channel_id=1, source_target_pairs={{0,24},{4,28},{8,16},{12,20},{16,8},{20,12},{24,0},{28,4},{1,25},{... | collective-permute-start | bytes 884744 | tf_op jit(solution)/shard_map/ppermute | solution.py:83
  247.7 37.3 %collective-permute-start.29 = (bf16[96,1920]{1,0:T(8,128)(2,1)}, bf16[96,1920]{1,0:T(8,128)(2,1)S(1)}, u32[]{:S(2)}, u32[]{:S(2)}) collective-permute-start(bf16[96,1920]{1,0:T(8,128)(2,1)} %get-tuple-element.193), channel_id=1, source_target_pairs={{0,8},{4,12},{8,0},{12,4},{16,24},{20,28},{24,16},{28,20},{1,9},{5... | collective-permute-start | bytes 1105928 | tf_op jit(solution)/shard_map/ppermute | solution.py:83
  248.3 36.7 %collective-permute-start.30 = (bf16[96,1920]{1,0:T(8,128)(2,1)}, bf16[96,1920]{1,0:T(8,128)(2,1)S(1)}, u32[]{:S(2)}, u32[]{:S(2)}) collective-permute-start(bf16[96,1920]{1,0:T(8,128)(2,1)} %get-tuple-element.194), channel_id=1, source_target_pairs={{0,16},{4,20},{8,24},{12,28},{16,0},{20,4},{24,8},{28,12},{1,17},{... | collective-permute-start | bytes 1105928 | tf_op jit(solution)/shard_map/ppermute | solution.py:83
  253.7 31.3 %collective-permute-start.31 = (bf16[96,1920]{1,0:T(8,128)(2,1)}, bf16[96,1920]{1,0:T(8,128)(2,1)S(1)}, u32[]{:S(2)}, u32[]{:S(2)}) collective-permute-start(bf16[96,1920]{1,0:T(8,128)(2,1)} %get-tuple-element.195), channel_id=1, source_target_pairs={{0,24},{4,28},{8,16},{12,20},{16,8},{20,12},{24,0},{28,4},{1,25},{... | collective-permute-start | bytes 1105928 | tf_op jit(solution)/shard_map/ppermute | solution.py:83
  255.8 34.4 %all-to-all-start.2 = ((f32[8,4,2304]{2,1,0:T(4,128)}), f32[8,4,2304]{2,1,0:T(4,128)S(1)}, u32[]{:S(2)}, u32[]{:S(2)}) async-start(f32[8,4,2304]{2,1,0:T(4,128)} %broadcast_in_dim.4), calls=%async_computation.2 | async-start | bytes 589824 | tf_op jit(solution)/shard_map/all_to_all | solution.py:101
  285.0 5.1 %copy-start.9 = (bf16[96,1920]{1,0:T(8,128)(2,1)}, bf16[96,1920]{1,0:T(8,128)(2,1)S(1)}, u32[]{:S(2)}) copy-start(bf16[96,1920]{1,0:T(8,128)(2,1)S(1)} %collective-permute-done.29.refs_5_) | copy-start | bytes 1105924
  285.1 5.1 %copy-start.10 = (bf16[96,1920]{1,0:T(8,128)(2,1)}, bf16[96,1920]{1,0:T(8,128)(2,1)S(1)}, u32[]{:S(2)}) copy-start(bf16[96,1920]{1,0:T(8,128)(2,1)S(1)} %collective-permute-done.30.refs_6_) | copy-start | bytes 1105924
  285.1 5.1 %copy-start.11 = (bf16[96,1920]{1,0:T(8,128)(2,1)}, bf16[96,1920]{1,0:T(8,128)(2,1)S(1)}, u32[]{:S(2)}) copy-start(bf16[96,1920]{1,0:T(8,128)(2,1)S(1)} %collective-permute-done.31.refs_7_) | copy-start | bytes 1105924
  290.2 3.5 copy-start.5
  293.7 4.9 %collective-permute-start.32 = (bf16[2,3,256,768]{3,2,1,0:T(8,128)(2,1)}, bf16[2,3,256,768]{3,2,1,0:T(8,128)(2,1)}, u32[]{:S(2)}, u32[]{:S(2)}) collective-permute-start(bf16[2,3,256,768]{3,2,1,0:T(8,128)(2,1)} %token_grad.1), channel_id=1, source_target_pairs={{0,1},{1,0},{2,3},{3,2},{4,5},{5,4},{6,7},{7,6},{8,9},{9,8},{10,11... | collective-permute-start | bytes 7077896 | tf_op jit(solution)/shard_map/ppermute | solution.py:79
  293.7 18.6 %collective-permute-start.37 = (bf16[96,3456]{1,0:T(8,128)(2,1)}, bf16[96,3456]{1,0:T(8,128)(2,1)S(1)}, u32[]{:S(2)}, u32[]{:S(2)}) collective-permute-start(bf16[96,3456]{1,0:T(8,128)(2,1)} %gather.2.own), channel_id=1, source_target_pairs={{0,2},{1,3},{2,0},{3,1},{4,6},{5,7},{6,4},{7,5},{8,10},{9,11},{10,... | collective-permute-start | bytes 1990664 | tf_op jit(solution)/shard_map/ppermute | solution.py:79
  294.2 15.4 %collective-permute-start.33 = (bf16[4,112,576]{2,1,0:T(8,128)(2,1)}, bf16[4,112,576]{2,1,0:T(8,128)(2,1)}, u32[]{:S(2)}, u32[]{:S(2)}) collective-permute-start(bf16[4,112,576]{2,1,0:T(8,128)(2,1)} %get-tuple-element.216), channel_id=1, source_target_pairs={{0,4},{4,0},{8,12},{12,8},{16,20},{20,16},{24,28},{28,24},{1,5},{5... | collective-permute-start | bytes 1548296 | tf_op jit(solution)/shard_map/ppermute | solution.py:83
  303.8 8.5 %copy-start.1 = (bf16[96,3456]{1,0:T(8,128)(2,1)S(1)}, bf16[96,3456]{1,0:T(8,128)(2,1)}, u32[]{:S(2)}) copy-start(bf16[96,3456]{1,0:T(8,128)(2,1)} %gather.2.own) | copy-start | bytes 1990660
  312.3 2.8 copy-start.6
  312.3 6.0 %copy-start.26 = (bf16[112,576]{1,0:T(8,128)(2,1)S(1)}, bf16[112,576]{1,0:T(8,128)(2,1)}, u32[]{:S(2)}) copy-start(bf16[112,576]{1,0:T(8,128)(2,1)} %get-tuple-element.220) | copy-start | bytes 387076
  312.4 8.1 %copy-start.14 = (f32[32,96]{1,0:T(8,128)S(1)}, f32[32,96]{1,0:T(8,128)}, u32[]{:S(2)}) copy-start(f32[32,96]{1,0:T(8,128)} %copy-done.13) | copy-start | bytes 36868
  313.6 8.8 %collective-permute-start.38 = (bf16[2,96,3456]{2,1,0:T(8,128)(2,1)}, bf16[2,96,3456]{2,1,0:T(8,128)(2,1)}, u32[]{:S(2)}, u32[]{:S(2)}) collective-permute-start(bf16[2,96,3456]{2,1,0:T(8,128)(2,1)} %pad_maximum_fusion), channel_id=1, source_target_pairs={{0,1},{1,0},{2,3},{3,2},{4,5},{5,4},{6,7},{7,6},{8,9},{9,8},{10,11... | collective-permute-start | bytes 3981320 | tf_op jit(solution)/shard_map/ppermute | solution.py:79
  313.6 29.1 %collective-permute-start.39 = (bf16[3,256,768]{2,1,0:T(8,128)(2,1)}, bf16[3,256,768]{2,1,0:T(8,128)(2,1)}, u32[]{:S(2)}, u32[]{:S(2)}) collective-permute-start(bf16[3,256,768]{2,1,0:T(8,128)(2,1)} %across.1), channel_id=1, source_target_pairs={{0,2},{1,3},{2,0},{3,1},{4,6},{5,7},{6,4},{7,5},{8,10},{9,11},{10,... | collective-permute-start | bytes 3538952 | tf_op jit(solution)/shard_map/ppermute | solution.py:79
  315.3 11.3 %collective-permute-start.34 = (bf16[112,576]{1,0:T(8,128)(2,1)}, bf16[112,576]{1,0:T(8,128)(2,1)S(1)}, u32[]{:S(2)}, u32[]{:S(2)}) collective-permute-start(bf16[112,576]{1,0:T(8,128)(2,1)} %get-tuple-element.218), channel_id=1, source_target_pairs={{0,8},{4,12},{8,0},{12,4},{16,24},{20,28},{24,16},{28,20},{1,9},{5... | collective-permute-start | bytes 387080 | tf_op jit(solution)/shard_map/ppermute | solution.py:83
  315.5 13.9 %collective-permute-start.35 = (bf16[112,576]{1,0:T(8,128)(2,1)}, bf16[112,576]{1,0:T(8,128)(2,1)S(1)}, u32[]{:S(2)}, u32[]{:S(2)}) collective-permute-start(bf16[112,576]{1,0:T(8,128)(2,1)} %get-tuple-element.219), channel_id=1, source_target_pairs={{0,16},{4,20},{8,24},{12,28},{16,0},{20,4},{24,8},{28,12},{1,17},{... | collective-permute-start | bytes 387080 | tf_op jit(solution)/shard_map/ppermute | solution.py:83
  318.3 11.1 %collective-permute-start.36 = (bf16[112,576]{1,0:T(8,128)(2,1)S(1)}, bf16[112,576]{1,0:T(8,128)(2,1)S(1)}, u32[]{:S(2)}, u32[]{:S(2)}) collective-permute-start(bf16[112,576]{1,0:T(8,128)(2,1)S(1)} %copy-done.26), channel_id=1, source_target_pairs={{0,24},{4,28},{8,16},{12,20},{16,8},{20,12},{24,0},{28,4},{1,25},{... | collective-permute-start | bytes 387080 | tf_op jit(solution)/shard_map/ppermute | solution.py:83
  326.6 2.8 copy-start.17
  332.6 17.5 %collective-permute-start.40 = (bf16[112,576]{1,0:T(8,128)(2,1)}, bf16[112,576]{1,0:T(8,128)(2,1)S(1)}, u32[]{:S(2)}, u32[]{:S(2)}) collective-permute-start(bf16[112,576]{1,0:T(8,128)(2,1)} %gather.3.own), channel_id=1, source_target_pairs={{0,2},{1,3},{2,0},{3,1},{4,6},{5,7},{6,4},{7,5},{8,10},{9,11},{10,... | collective-permute-start | bytes 387080 | tf_op jit(solution)/shard_map/ppermute | solution.py:79
  333.1 17.1 %collective-permute-start.41 = (bf16[112,576]{1,0:T(8,128)(2,1)}, bf16[112,576]{1,0:T(8,128)(2,1)S(1)}, u32[]{:S(2)}, u32[]{:S(2)}) collective-permute-start(bf16[112,576]{1,0:T(8,128)(2,1)} %gather.3.own), channel_id=1, source_target_pairs={{0,1},{1,0},{2,3},{3,2},{4,5},{5,4},{6,7},{7,6},{8,9},{9,8},{10,11... | collective-permute-start | bytes 387080 | tf_op jit(solution)/shard_map/ppermute | solution.py:79
  333.1 17.1 %collective-permute-start.42 = (bf16[112,576]{1,0:T(8,128)(2,1)}, bf16[112,576]{1,0:T(8,128)(2,1)S(1)}, u32[]{:S(2)}, u32[]{:S(2)}) collective-permute-start(bf16[112,576]{1,0:T(8,128)(2,1)} %gather.3.own), channel_id=1, source_target_pairs={{0,3},{1,2},{2,1},{3,0},{4,7},{5,6},{6,5},{7,4},{8,11},{9,10},{10,... | collective-permute-start | bytes 387080 | tf_op jit(solution)/shard_map/ppermute | solution.py:79
  335.4 19.3 %all-to-all-start.3 = ((f32[8,32,96]{2,1,0:T(8,128)}), f32[8,32,96]{2,1,0:T(8,128)S(1)}, u32[]{:S(2)}, u32[]{:S(2)}) async-start(f32[8,32,96]{2,1,0:T(8,128)} %broadcast_in_dim.5), calls=%async_computation.3 | async-start | bytes 262144 | tf_op jit(solution)/shard_map/all_to_all | solution.py:101
  340.9 14.0 %copy-start.22 = (f32[1,32]{1,0:T(1,128)S(1)}, f32[1,32]{1,0:T(1,128)}, u32[]{:S(2)}) copy-start(f32[1,32]{1,0:T(1,128)} %get-tuple-element.237) | copy-start | bytes 388
  (10 other events, 7.7 us)

commit v4 on v3

--- a/solution.py
+++ b/solution.py
@@ -1198,7 +1198,7 @@
     pack_in = run(
         pack_in_kernel,
         (1,),
-        meta,
+        s.astype(jnp.int32)[None],
         [whole(proj_in), *(whole(v) for v in vectors)],
         [out_whole((deep + EXTRA, 3 * hw), BF16)],
         name="pack_in",
@@ -1378,23 +1378,23 @@
     across = across_call(meta, after(grads, rest_sum), in_w, came)
     across_got = seq_swap(across, 2)
 
+    exact = functools.partial(lax.dot_general, precision=HIGHEST, preferred_element_type=F32)
+    all_rows = after(rows_got, across).reshape(ranks * kinds, 3 * width)
+    act_rows_grad = exact(all_rows, ada_weight.astype(F32), (((1,), (1,)), ((), ())))
+    embed_grad = jax.vjp(jax.nn.silu, embedded)[1](act_rows_grad)[0]
+    ada_bias_grad = lax.dynamic_slice_in_dim(
+        jnp.sum(all_rows, axis=0), d * ada_bias.shape[0], ada_bias.shape[0], 0
+    )
+    ada_grad = exact(activated.astype(F32), all_rows, (((0,), (0,)), ((), ())))
     in_pieces = run(
         pair_kernel,
         (1,),
         meta,
-        [whole(after(in_even, across)), whole(in_came)],
+        [whole(after(in_even, across, embed_grad, ada_grad, ada_bias_grad)), whole(in_came)],
         [out_whole(in_even.shape[1:], BF16) for _ in range(outer)],
         name="pair",
     )
     in_got = spread(in_pieces)
-    exact = functools.partial(lax.dot_general, precision=HIGHEST, preferred_element_type=F32)
-    all_rows = after(rows_got, in_pieces[0]).reshape(ranks * kinds, 3 * width)
-    act_rows_grad = exact(all_rows, ada_weight.astype(F32), (((1,), (1,)), ((), ())))
-    embed_grad = jax.vjp(jax.nn.silu, embedded)[1](act_rows_grad)[0]
-    ada_bias_grad = lax.dynamic_slice_in_dim(
-        jnp.sum(after(all_rows, in_pieces[0]), axis=0), d * ada_bias.shape[0], ada_bias.shape[0], 0
-    )
-    ada_grad = exact(activated.astype(F32), after(all_rows, in_pieces[0]), (((0,), (0,)), ((), ())))
     rest_x = after(rest_x, in_pieces[0])
     rest_pair = seq_swap(jnp.stack([rest_sum, rest_x]), 1)
     up_final, down_final, out_final = run(
@@ -1412,7 +1412,7 @@
 
     in_sum = gather_call(meta, [after(in_got, ada_bias_grad, ada_grad, up_final)])
     in_parts = [in_sum] + [seq_swap(in_sum, j) for j in (2, 1, 3)]
-    embed_got = dp_all(after(embed_grad, in_sum))
+    embed_got = dp_all(after(embed_grad, up_final))
     tokens_grad = last_call(
         meta, tokens, after(resid_grad, in_sum), grads, in_w, came, across_got, gain
     )

time: 358 us -> 356 us (level)
  no operation moved by 1% of the time
where the time goes in v4:
time: 356 us; the launch traced here: 354 us
  Pallas kernels  217 us (61%)
  starting transfers between devices  63 us (18%)
  waiting for transfers between devices  49.1 us (14%)
  local copies, waits for them, and re-layouts  11 us (3%)
  other arithmetic  9.01 us (3%)
    pallas_call x25, Pallas kernels, run(): pl.pallas_call(kernel, grid_spec=pltpu.PrefetchScalarGridSpec(num_scalar_...  217 us
    ppermute x23, starting transfers between devices, dp_swap(): lax.ppermute(value, 'dp', [(d, d ^ mask) for d in range(lax.axis_size('dp...  34.5 us
    ppermute x23, waiting for transfers between devices, dp_swap(): lax.ppermute(value, 'dp', [(d, d ^ mask) for d in range(lax.axis_size('dp...  28 us
    all_to_all x4, starting transfers between devices, dp_turn(): lax.all_to_all(value, 'dp', split_axis=0, concat_axis=0, tiled=True, axis...  18.2 us
    ppermute x20, waiting for transfers between devices, seq_swap(): lax.ppermute(value, 'seq', [(s, s ^ mask) for s in range(lax.axis_size('s...  15.9 us
    ppermute x20, starting transfers between devices, seq_swap(): lax.ppermute(value, 'seq', [(s, s ^ mask) for s in range(lax.axis_size('s...  10.3 us
  transfers between devices with their start and end apart: 47, of which 15 were waited for; matrix products, arithmetic and copies ran while one was open for 4% of the time, Pallas kernels for 49%

profile of v4, /device:TPU:0, one launch (start us, length us, event | category | flops | bytes accessed | tf_op | source)
XLA Modules:
  0.0 353.7 jit_solution(12929951384919645873)
XLA Ops:
  0.7 2.0 pack_in.1.refs_0_
  2.7 3.0 collective-permute-start
  5.7 2.6 collective-permute-start.1
  8.3 1.7 collective-permute-start.6
  12.7 2.9 pack_rest.1.refs_0_
  15.5 1.9 pad_maximum_fusion.2
  17.4 2.4 collective-permute-done.1.refs_2_
  21.0 1.6 collective-permute-start.4
  22.6 2.2 collective-permute-start.9
  25.9 10.6 %collective-permute-done.4.refs_4_ = bf16[4,112,576]{2,1,0:T(8,128)(2,1)S(1)} collective-permute-done((bf16[4,112,576]{2,1,0:T(8,128)(2,1)S(1)}, bf16[4,112,576]{2,1,0:T(8,128)(2,1)S(1)}, u32[]{:S(2)}, u32[]{:S(2)}) %collective-permute-start.4) | collective-permute-done | bytes 516128 | tf_op jit(solution)/shard_map/ppermute | solution.py:83
  37.2 3.5 %place_in.1 = (bf16[768,576]{1,0:T(8,128)(2,1)}, f32[1,768]{1,0:T(1,128)}, f32[1,768]{1,0:T(1,128)}, f32[1,576]{1,0:T(1,128)}, f32[1,768]{1,0:T(1,128)}, /*index...) custom-call(s32[7]{0:T(128)} %concatenate.13.meta, ...), custom_call_target="tpu_custom_call" | custom-call | tf_op jit(solution)/shard_map/place_in/pallas_call | solution.py:120
  40.8 1.6 collective-permute-start.8
  42.3 4.5 %all-to-all-start = ((bf16[8,32,96]{2,1,0:T(8,128)(2,1)}), bf16[8,32,96]{2,1,0:T(8,128)(2,1)}, u32[]{:S(2)}, u32[]{:S(2)}) async-start(bf16[8,32,96]{2,1,0:T(8,128)(2,1)} %get-tuple-element.144), calls=%async_computation | async-start | bytes 131072 | tf_op jit(solution)/shard_map/all_to_all | solution.py:101
  46.9 1.3 reduce.1
  48.2 8.4 %qkv.2.qa.refs_0_ = bf16[3,512,576]{2,1,0:T(8,128)(2,1)} custom-call(s32[7]{0:T(128)} %concatenate.13.meta, bf16[3,256,768]{2,1,0:T(8,128)(2,1)} %tokens.3, bf16[3,256,768]{2,1,0:T(8,128)(2,1)} %collective-permute-done.3.x1, f32[1,768]{1,0:T(1,128)} %get-tuple-element.134.gain, f32[1,768]{1,0:T(1,128)} %get-tuple-element.135.bias, ...), custom_call_target="tpu_custom_call" | custom-call | flops 40768634880 | bytes 176947200 | tf_op jit(solution)/shard_map/qkv/pallas_call | solution.py:120
  56.6 1.6 collective-permute-done.8.refs_1_
  58.3 1.6 collective-permute-start.10
  59.9 2.2 collective-permute-start.12
  62.1 8.4 %qkv.3.qb.refs_1_ = bf16[3,512,576]{2,1,0:T(8,128)(2,1)} custom-call(s32[7]{0:T(128)} %concatenate.13.meta, bf16[3,256,768]{2,1,0:T(8,128)(2,1)} %collective-permute-done.6.x0.x2, bf16[3,256,768]{2,1,0:T(8,128)(2,1)} %collective-permute-done.7.x1.x3, f32[1,768]{1,0:T(1,128)} %get-tuple-element.134.gain, f32[1,768]{1,0:T(1,128)} %get-tuple-element.135.bias, ...), custom_call_target="tpu_custom_call" | custom-call | flops 40768634880 | bytes 176947200 | tf_op jit(solution)/shard_map/qkv/pallas_call | solution.py:120
  71.1 14.3 %attend.2 = (bf16[3,128,384]{2,1,0:T(8,128)(2,1)}, bf16[3,128,384]{2,1,0:T(8,128)(2,1)}, bf16[3,3,1024,1024]{3,2,1,0:T(8,128)(2,1)}, f32[3,1024,128]{2,1,0:T(8,128)}) custom-call(s32[7]{0:T(128)} %concatenate.13.meta, bf16[3,512,576]{2,1,0:T(8,128)(2,1)} %qkv.2.qa.refs_0_, bf16[3,512,576]{2,1,0:T(8,128)(2,1)} %qkv.3.qb.refs_1_), custom_call_target="tpu_custom_call" | custom-call | flops 144955146240 | bytes 283115520 | tf_op jit(solution)/shard_map/attend/pallas_call | solution.py:120
  85.4 1.5 collective-permute-start.14
  89.4 4.2 %all-to-all-start.1 = ((f32[8,4,2304]{2,1,0:T(4,128)}), f32[8,4,2304]{2,1,0:T(4,128)}, u32[]{:S(2)}, u32[]{:S(2)}) async-start(f32[8,4,2304]{2,1,0:T(4,128)} %reshape.143), calls=%async_computation.1 | async-start | bytes 589824 | tf_op jit(solution)/shard_map/all_to_all | solution.py:101
  93.6 1.7 collective-permute-start.16
  95.4 14.3 %attend.3 = (bf16[3,128,384]{2,1,0:T(8,128)(2,1)}, bf16[3,128,384]{2,1,0:T(8,128)(2,1)}, bf16[3,3,1024,1024]{3,2,1,0:T(8,128)(2,1)}, f32[3,1024,128]{2,1,0:T(8,128)}) custom-call(s32[7]{0:T(128)} %concatenate.13.meta, bf16[3,512,576]{2,1,0:T(8,128)(2,1)} %qkv.2.qa.refs_0_, ...), custom_call_target="tpu_custom_call", output_to_operand_aliasing={{2}: (3, {}), {3}: (4, {})} | custom-call | flops 144955146240 | bytes 283115520 | tf_op jit(solution)/shard_map/attend/pallas_call | solution.py:120
  109.7 3.2 collective-permute-done.16.refs_7_
  113.0 2.7 place_out.1.w_own
  119.1 6.4 %mix.1 = (f32[3,256,768]{2,1,0:T(8,128)}, bf16[3,256,768]{2,1,0:T(8,128)(2,1)}, bf16[768,768]{1,0:T(8,128)(2,1)}) custom-call(s32[7]{0:T(128)} %concatenate.13.meta, bf16[3,128,384]{2,1,0:T(8,128)(2,1)} %get-tuple-element.152.m0.o0, bf16[3,128,384]{2,1,0:T(8,128)(2,1)} %copy-done.24, bf16[3,128,384]{2,1,0:T(8,128)(2,1)} %collective-permute-done.14.m2, ...), custom_call_target="tpu_custom_call" | custom-call | flops 27179089920 | bytes 212336640 | tf_op jit(solution)/shard_map/mix/pallas_call | solution.py:120
  125.7 3.0 collective-permute-done.18.x1
  128.8 38.7 %mlp.1 = (f32[3,256,768]{2,1,0:T(8,128)}, f32[3,256,768]{2,1,0:T(8,128)}, bf16[2,3,256,768]{3,2,1,0:T(8,128)(2,1)}, bf16[4,96,1536]{2,1,0:T(8,128)(2,1)}, bf16[4...) custom-call(s32[7]{0:T(128)} %concatenate.13.meta, ...), custom_call_target="tpu_custom_call" | custom-call | flops 652298158080 | bytes 353894400 | tf_op jit(solution)/shard_map/mlp/pallas_call | solution.py:120
  168.8 3.7 %collective-permute-done.20.got = bf16[2,3,256,768]{3,2,1,0:T(8,128)(2,1)} collective-permute-done((bf16[2,3,256,768]{3,2,1,0:T(8,128)(2,1)}, bf16[2,3,256,768]{3,2,1,0:T(8,128)(2,1)}, u32[]{:S(2)}, u32[]{:S(2)}) %collective-permute-start.20) | collective-permute-done | bytes 2359328 | tf_op jit(solution)/shard_map/ppermute | solution.py:79
  172.4 12.8 %turn.1 = (bf16[3,256,768]{2,1,0:T(8,128)(2,1)}, f32[3,256,768]{2,1,0:T(8,128)}, bf16[432,384]{1,0:T(8,128)(2,1)}, bf16[1200,384]{1,0:T(8,128)(2,1)}, bf16[432,3...) custom-call(s32[7]{0:T(128)} %concatenate.13.meta, ...), custom_call_target="tpu_custom_call" | custom-call | flops 54358179840 | bytes 424673280 | tf_op jit(solution)/shard_map/turn/pallas_call | solution.py:120
  185.9 1.2 collective-permute-start.24
  188.9 4.6 %join.1 = (bf16[4,96,1920]{2,1,0:T(8,128)(2,1)}, bf16[4,96,1920]{2,1,0:T(8,128)(2,1)}) custom-call(s32[7]{0:T(128)} %concatenate.13.meta, bf16[4,96,1536]{2,1,0:T(8,128)(2,1)} %get-tuple-element.172.down_here, bf16[4,96,1536]{2,1,0:T(8,128)(2,1)} %get-tuple-element.173.down_away, bf16[768,384]{1,0:T(8,128)(2,1)} %get-tuple-element.174.out_here, ...), custom_call_target="tpu_custom_call" | custom-call | tf_op jit(solution)/shard_map/join/pallas_call | solution.py:120
  194.5 1.7 collective-permute-done.22.came
  196.2 3.4 half.2
  199.7 2.5 collective-permute-done.24.g3
  202.2 1.5 collective-permute-start.26
  203.7 2.4 collective-permute-start.27
  206.6 35.4 %attend_back.1.raw = bf16[3,1024,576]{2,1,0:T(8,128)(2,1)} custom-call(s32[7]{0:T(128)} %concatenate.13.meta, bf16[3,512,576]{2,1,0:T(8,128)(2,1)} %qkv.2.qa.refs_0_, bf16[3,512,576]{2,1,0:T(8,128)(2,1)} %qkv.3.qb.refs_1_, bf16[3,3,1024,1024]{3,2,1,0:T(8,128)(2,1)} %get-tuple-element.184.weights, f32[3,1024,128]{2,1,0:T(8,128)} %get-tuple-element.185.recips, ...), custom_call_target="tpu_custom_call" | custom-call | flops 579820584960 | bytes 566231040 | tf_op jit(solution)/shard_map/attend_back/pallas_call | solution.py:120
  242.0 3.7 %half.3 = (bf16[96,1920]{1,0:T(8,128)(2,1)}, bf16[96,1920]{1,0:T(8,128)(2,1)}, bf16[96,1920]{1,0:T(8,128)(2,1)}, bf16[96,1920]{1,0:T(8,128)(2,1)}) custom-call(s32[7]{0:T(128)} %concatenate.13.meta, bf16[4,96,1920]{2,1,0:T(8,128)(2,1)} %get-tuple-element.190.here, bf16[4,96,1920]{2,1,0:T(8,128)(2,1)} %collective-permute-done.25.came), custom_call_target="tpu_custom_call" | custom-call | tf_op jit(solution)/shard_map/half/pallas_call | solution.py:120
  246.3 3.3 collective-permute-start.30
  249.5 2.1 rows.1
  252.2 1.5 broadcast_in_dim.4
  253.7 4.6 %all-to-all-start.2 = ((f32[8,4,2304]{2,1,0:T(4,128)}), f32[8,4,2304]{2,1,0:T(4,128)S(1)}, u32[]{:S(2)}, u32[]{:S(2)}) async-start(f32[8,4,2304]{2,1,0:T(4,128)} %broadcast_in_dim.4), calls=%async_computation.2 | async-start | bytes 589824 | tf_op jit(solution)/shard_map/all_to_all | solution.py:101
  258.3 18.7 %proj_grad.1 = (bf16[3,1024,576]{2,1,0:T(8,128)(2,1)}, bf16[4,112,576]{2,1,0:T(8,128)(2,1)}, bf16[4,112,576]{2,1,0:T(8,128)(2,1)}) custom-call(s32[7]{0:T(128)} %concatenate.13.meta, bf16[3,256,768]{2,1,0:T(8,128)(2,1)} %tokens.3, bf16[3,256,768]{2,1,0:T(8,128)(2,1)} %collective-permute-done.3.x1, bf16[3,256,768]{2,1,0:T(8,128)(2,1)} %collective-permute-done.6.x0.x2, ...), custom_call_target="tpu_custom_call" | custom-call | flops 81537269760 | bytes 424673280 | tf_op jit(solution)/shard_map/proj_grad/pallas_call | solution.py:120
  277.0 6.0 %token_grad.1 = bf16[2,3,256,768]{3,2,1,0:T(8,128)(2,1)} custom-call(s32[7]{0:T(128)} %concatenate.13.meta, bf16[3,1024,576]{2,1,0:T(8,128)(2,1)} %get-tuple-element.212.g1.g3.g2.g0, bf16[3,1024,576]{2,1,0:T(8,128)(2,1)} %get-tuple-element.212.g1.g3.g2.g0, bf16[768,576]{1,0:T(8,128)(2,1)} %get-tuple-element.136.w), custom_call_target="tpu_custom_call" | custom-call | tf_op jit(solution)/shard_map/token_grad/pallas_call | solution.py:120
  283.0 5.2 %all-to-all-done.2 = f32[8,4,2304]{2,1,0:T(4,128)S(1)} async-done(((f32[8,4,2304]{2,1,0:T(4,128)}), f32[8,4,2304]{2,1,0:T(4,128)S(1)}, u32[]{:S(2)}, u32[]{:S(2)}) %all-to-all-start.2) | async-done | bytes 294944 | tf_op jit(solution)/shard_map/all_to_all | solution.py:101
  288.2 3.5 gather.2.own
  293.3 3.3 collective-permute-done.32.got
  296.6 5.2 %across.1 = bf16[3,256,768]{2,1,0:T(8,128)(2,1)} custom-call(s32[7]{0:T(128)} %concatenate.13.meta, bf16[3,1024,576]{2,1,0:T(8,128)(2,1)} %get-tuple-element.212.g1.g3.g2.g0, bf16[768,576]{1,0:T(8,128)(2,1)} %get-tuple-element.136.w, bf16[2,3,256,768]{3,2,1,0:T(8,128)(2,1)} %collective-permute-done.32.got), custom_call_target="tpu_custom_call" | custom-call | tf_op jit(solution)/shard_map/across/pallas_call | solution.py:120
  303.2 1.5 fusion.7
  304.7 3.0 collective-permute-done.33.came
  307.7 2.7 pair.1
  311.3 1.5 collective-permute-start.39
  313.0 2.8 collective-permute-start.35
  315.8 1.4 collective-permute-start.36
  317.2 4.2 %close_rest.1 = (f32[96,3072]{1,0:T(8,128)}, f32[384,768]{1,0:T(8,128)}, f32[96,768]{1,0:T(8,128)}) custom-call(s32[7]{0:T(128)} %concatenate.13.meta, bf16[96,3456]{1,0:T(8,128)(2,1)} %gather.2.own, bf16[96,3456]{1,0:T(8,128)(2,1)} %copy-done.3, bf16[2,96,3456]{2,1,0:T(8,128)(2,1)} %collective-permute-done.38.pair), custom_call_target="tpu_custom_call" | custom-call | tf_op jit(solution)/shard_map/close_rest/pallas_call | solution.py:120
  321.4 5.4 %collective-permute-done.35.refs_2_ = bf16[112,576]{1,0:T(8,128)(2,1)S(1)} collective-permute-done((bf16[112,576]{1,0:T(8,128)(2,1)}, bf16[112,576]{1,0:T(8,128)(2,1)S(1)}, u32[]{:S(2)}, u32[]{:S(2)}) %collective-permute-start.35) | collective-permute-done | bytes 129056 | tf_op jit(solution)/shard_map/ppermute | solution.py:83
  328.2 2.5 gather.3.own
  331.2 1.7 collective-permute-start.42
  333.5 4.8 %all-to-all-start.3 = ((f32[8,32,96]{2,1,0:T(8,128)}), f32[8,32,96]{2,1,0:T(8,128)S(1)}, u32[]{:S(2)}, u32[]{:S(2)}) async-start(f32[8,32,96]{2,1,0:T(8,128)} %broadcast_in_dim.5), calls=%async_computation.3 | async-start | bytes 262144 | tf_op jit(solution)/shard_map/all_to_all | solution.py:101
  338.3 2.0 collective-permute-done.39.across
  340.3 7.5 %last.1 = f32[3,256,768]{2,1,0:T(8,128)} custom-call(s32[7]{0:T(128)} %concatenate.13.meta, bf16[3,256,768]{2,1,0:T(8,128)(2,1)} %tokens.3, f32[3,256,768]{2,1,0:T(8,128)} %get-tuple-element.228.resid_grad, bf16[3,1024,576]{2,1,0:T(8,128)(2,1)} %get-tuple-element.212.g1.g3.g2.g0, bf16[768,576]{1,0:T(8,128)(2,1)} %get-tuple-element.136.w, ...), custom_call_target="tpu_custom_call" | custom-call | flops 20384317440 | bytes 353894400 | tf_op jit(solution)/shard_map/last/pallas_call | solution.py:120
  349.2 3.2 close_in.1
  (132 shorter events, 27.8 us)
Async XLA Ops:
  0.6 87.7 %copy-start = (bf16[96,2304]{1,0:T(8,128)(2,1)S(1)}, bf16[96,2304]{1,0:T(8,128)(2,1)}, u32[]{:S(2)}) copy-start(bf16[96,2304]{1,0:T(8,128)(2,1)} %param.30) | copy-start | bytes 1327108
  2.7 9.3 %copy-start.20 = (s32[3]{0:T(128)S(1)}, s32[3]{0:T(128)}, u32[]{:S(2)}) copy-start(s32[3]{0:T(128)} %param.21) | copy-start | bytes 40
  2.7 14.7 %collective-permute-start = (bf16[112,576]{1,0:T(8,128)(2,1)}, bf16[112,576]{1,0:T(8,128)(2,1)}, u32[]{:S(2)}, u32[]{:S(2)}) collective-permute-start(bf16[112,576]{1,0:T(8,128)(2,1)} %pack_in.1.refs_0_), channel_id=1, source_target_pairs={{0,8},{4,12},{8,0},{12,4},{16,24},{20,28},{24,16},{28,20},{1,9},{5... | collective-permute-start | bytes 387080 | tf_op jit(solution)/shard_map/ppermute | solution.py:83
  5.7 14.0 %collective-permute-start.1 = (bf16[112,576]{1,0:T(8,128)(2,1)}, bf16[112,576]{1,0:T(8,128)(2,1)}, u32[]{:S(2)}, u32[]{:S(2)}) collective-permute-start(bf16[112,576]{1,0:T(8,128)(2,1)} %pack_in.1.refs_0_), channel_id=1, source_target_pairs={{0,16},{4,20},{8,24},{12,28},{16,0},{20,4},{24,8},{28,12},{1,17},{... | collective-permute-start | bytes 387080 | tf_op jit(solution)/shard_map/ppermute | solution.py:83
  8.3 11.5 %collective-permute-start.2 = (bf16[112,576]{1,0:T(8,128)(2,1)}, bf16[112,576]{1,0:T(8,128)(2,1)}, u32[]{:S(2)}, u32[]{:S(2)}) collective-permute-start(bf16[112,576]{1,0:T(8,128)(2,1)} %pack_in.1.refs_0_), channel_id=1, source_target_pairs={{0,24},{4,28},{8,16},{12,20},{16,8},{20,12},{24,0},{28,4},{1,25},{... | collective-permute-start | bytes 387080 | tf_op jit(solution)/shard_map/ppermute | solution.py:83
  8.3 39.9 %collective-permute-start.6 = (bf16[3,256,768]{2,1,0:T(8,128)(2,1)}, bf16[3,256,768]{2,1,0:T(8,128)(2,1)}, u32[]{:S(2)}, u32[]{:S(2)}) collective-permute-start(bf16[3,256,768]{2,1,0:T(8,128)(2,1)} %tokens.3), channel_id=1, source_target_pairs={{0,2},{1,3},{2,0},{3,1},{4,6},{5,7},{6,4},{7,5},{8,10},{9,11},{10,... | collective-permute-start | bytes 3538952 | tf_op jit(solution)/shard_map/ppermute | solution.py:79
  15.5 4.2 %copy-start.4 = (bf16[112,576]{1,0:T(8,128)(2,1)S(1)}, bf16[112,576]{1,0:T(8,128)(2,1)}, u32[]{:S(2)}) copy-start(bf16[112,576]{1,0:T(8,128)(2,1)} %pack_in.1.refs_0_) | copy-start | bytes 387076
  20.9 27.2 %collective-permute-start.3 = (bf16[3,256,768]{2,1,0:T(8,128)(2,1)}, bf16[3,256,768]{2,1,0:T(8,128)(2,1)}, u32[]{:S(2)}, u32[]{:S(2)}) collective-permute-start(bf16[3,256,768]{2,1,0:T(8,128)(2,1)} %tokens.3), channel_id=1, source_target_pairs={{0,1},{1,0},{2,3},{3,2},{4,5},{5,4},{6,7},{7,6},{8,9},{9,8},{10,11... | collective-permute-start | bytes 3538952 | tf_op jit(solution)/shard_map/ppermute | solution.py:79
  21.0 15.4 %collective-permute-start.4 = (bf16[4,112,576]{2,1,0:T(8,128)(2,1)S(1)}, bf16[4,112,576]{2,1,0:T(8,128)(2,1)S(1)}, u32[]{:S(2)}, u32[]{:S(2)}) collective-permute-start(bf16[4,112,576]{2,1,0:T(8,128)(2,1)S(1)} %pad_maximum_fusion.1), channel_id=1, source_target_pairs={{0,4},{4,0},{8,12},{12,8},{16,20},{20,16},{24,28},{28,24},{1,5},{5... | collective-permute-start | bytes 1548296 | tf_op jit(solution)/shard_map/ppermute | solution.py:83
  22.6 35.7 %collective-permute-start.9 = (bf16[96,3456]{1,0:T(8,128)(2,1)}, bf16[96,3456]{1,0:T(8,128)(2,1)}, u32[]{:S(2)}, u32[]{:S(2)}) collective-permute-start(bf16[96,3456]{1,0:T(8,128)(2,1)} %pack_rest.1.refs_0_), channel_id=1, source_target_pairs={{0,8},{4,12},{8,0},{12,4},{16,24},{20,28},{24,16},{28,20},{1,9},{5... | collective-permute-start | bytes 1990664 | tf_op jit(solution)/shard_map/ppermute | solution.py:83
  24.9 33.4 %collective-permute-start.5 = (bf16[96,3456]{1,0:T(8,128)(2,1)}, bf16[96,3456]{1,0:T(8,128)(2,1)}, u32[]{:S(2)}, u32[]{:S(2)}) collective-permute-start(bf16[96,3456]{1,0:T(8,128)(2,1)} %pack_rest.1.refs_0_), channel_id=1, source_target_pairs={{0,16},{4,20},{8,24},{12,28},{16,0},{20,4},{24,8},{28,12},{1,17},{... | collective-permute-start | bytes 1990664 | tf_op jit(solution)/shard_map/ppermute | solution.py:83
  40.8 17.5 %collective-permute-start.8 = (bf16[96,3456]{1,0:T(8,128)(2,1)}, bf16[96,3456]{1,0:T(8,128)(2,1)S(1)}, u32[]{:S(2)}, u32[]{:S(2)}) collective-permute-start(bf16[96,3456]{1,0:T(8,128)(2,1)} %pack_rest.1.refs_0_), channel_id=1, source_target_pairs={{0,4},{4,0},{8,12},{12,8},{16,20},{20,16},{24,28},{28,24},{1,5},{5... | collective-permute-start | bytes 1990664 | tf_op jit(solution)/shard_map/ppermute | solution.py:83
  42.3 44.6 %all-to-all-start = ((bf16[8,32,96]{2,1,0:T(8,128)(2,1)}), bf16[8,32,96]{2,1,0:T(8,128)(2,1)}, u32[]{:S(2)}, u32[]{:S(2)}) async-start(bf16[8,32,96]{2,1,0:T(8,128)(2,1)} %get-tuple-element.144), calls=%async_computation | async-start | bytes 131072 | tf_op jit(solution)/shard_map/all_to_all | solution.py:101
  48.2 13.9 %collective-permute-start.7 = (bf16[3,256,768]{2,1,0:T(8,128)(2,1)}, bf16[3,256,768]{2,1,0:T(8,128)(2,1)}, u32[]{:S(2)}, u32[]{:S(2)}) collective-permute-start(bf16[3,256,768]{2,1,0:T(8,128)(2,1)} %collective-permute-done.6.x0.x2), channel_id=1, source_target_pairs={{0,1},{1,0},{2,3},{3,2},{4,5},{5,4},{6,7},{7,6},{8,9},{9,8},{10,11... | collective-permute-start | bytes 3538952 | tf_op jit(solution)/shard_map/ppermute | solution.py:79
  58.3 12.2 %copy-start.5 = (bf16[96,3456]{1,0:T(8,128)(2,1)}, bf16[96,3456]{1,0:T(8,128)(2,1)S(1)}, u32[]{:S(2)}) copy-start(bf16[96,3456]{1,0:T(8,128)(2,1)S(1)} %collective-permute-done.8.refs_1_) | copy-start | bytes 1990660
  58.3 37.1 %collective-permute-start.10 = (bf16[96,3456]{1,0:T(8,128)(2,1)}, bf16[96,3456]{1,0:T(8,128)(2,1)}, u32[]{:S(2)}, u32[]{:S(2)}) collective-permute-start(bf16[96,3456]{1,0:T(8,128)(2,1)} %collective-permute-done.9.refs_2_), channel_id=1, source_target_pairs={{0,4},{4,0},{8,12},{12,8},{16,20},{20,16},{24,28},{28,24},{1,5},{5... | collective-permute-start | bytes 1990664 | tf_op jit(solution)/shard_map/ppermute | solution.py:83
  59.9 33.8 %collective-permute-start.12 = (bf16[96,3456]{1,0:T(8,128)(2,1)}, bf16[96,3456]{1,0:T(8,128)(2,1)}, u32[]{:S(2)}, u32[]{:S(2)}) collective-permute-start(bf16[96,3456]{1,0:T(8,128)(2,1)} %pack_rest.1.refs_0_), channel_id=1, source_target_pairs={{0,24},{4,28},{8,16},{12,20},{16,8},{20,12},{24,0},{28,4},{1,25},{... | collective-permute-start | bytes 1990664 | tf_op jit(solution)/shard_map/ppermute | solution.py:83
  70.5 24.9 %collective-permute-start.11 = (bf16[96,3456]{1,0:T(8,128)(2,1)}, bf16[96,3456]{1,0:T(8,128)(2,1)}, u32[]{:S(2)}, u32[]{:S(2)}) collective-permute-start(bf16[96,3456]{1,0:T(8,128)(2,1)} %collective-permute-done.5.refs_4_), channel_id=1, source_target_pairs={{0,4},{4,0},{8,12},{12,8},{16,20},{20,16},{24,28},{28,24},{1,5},{5... | collective-permute-start | bytes 1990664 | tf_op jit(solution)/shard_map/ppermute | solution.py:83
  85.4 32.5 %collective-permute-start.14 = (bf16[3,128,384]{2,1,0:T(8,128)(2,1)}, bf16[3,128,384]{2,1,0:T(8,128)(2,1)}, u32[]{:S(2)}, u32[]{:S(2)}) collective-permute-start(bf16[3,128,384]{2,1,0:T(8,128)(2,1)} %get-tuple-element.143.o2), channel_id=1, source_target_pairs={{0,2},{1,3},{2,0},{3,1},{4,6},{5,7},{6,4},{7,5},{8,10},{9,11},{10,... | collective-permute-start | bytes 884744 | tf_op jit(solution)/shard_map/ppermute | solution.py:79
  89.4 20.3 %all-to-all-start.1 = ((f32[8,4,2304]{2,1,0:T(4,128)}), f32[8,4,2304]{2,1,0:T(4,128)}, u32[]{:S(2)}, u32[]{:S(2)}) async-start(f32[8,4,2304]{2,1,0:T(4,128)} %reshape.143), calls=%async_computation.1 | async-start | bytes 589824 | tf_op jit(solution)/shard_map/all_to_all | solution.py:101
  93.6 19.3 %collective-permute-start.16 = (bf16[96,3456]{1,0:T(8,128)(2,1)}, bf16[96,3456]{1,0:T(8,128)(2,1)}, u32[]{:S(2)}, u32[]{:S(2)}) collective-permute-start(bf16[96,3456]{1,0:T(8,128)(2,1)} %collective-permute-done.12.refs_6_), channel_id=1, source_target_pairs={{0,4},{4,0},{8,12},{12,8},{16,20},{20,16},{24,28},{28,24},{1,5},{5... | collective-permute-start | bytes 1990664 | tf_op jit(solution)/shard_map/ppermute | solution.py:83
  95.4 22.6 %collective-permute-start.15 = (bf16[3,128,384]{2,1,0:T(8,128)(2,1)}, bf16[3,128,384]{2,1,0:T(8,128)(2,1)}, u32[]{:S(2)}, u32[]{:S(2)}) collective-permute-start(bf16[3,128,384]{2,1,0:T(8,128)(2,1)} %get-tuple-element.154.o3), channel_id=1, source_target_pairs={{0,3},{1,2},{2,1},{3,0},{4,7},{5,6},{6,5},{7,4},{8,11},{9,10},{10,... | collective-permute-start | bytes 884744 | tf_op jit(solution)/shard_map/ppermute | solution.py:79
  109.7 6.0 %copy-start.23 = (bf16[3,128,384]{2,1,0:T(8,128)(2,1)S(1)}, bf16[3,128,384]{2,1,0:T(8,128)(2,1)}, u32[]{:S(2)}) copy-start(bf16[3,128,384]{2,1,0:T(8,128)(2,1)} %get-tuple-element.153.o1) | copy-start | bytes 884740
  109.7 6.5 %copy-start.22 = (bf16[3,256,768]{2,1,0:T(8,128)(2,1)S(1)}, bf16[3,256,768]{2,1,0:T(8,128)(2,1)}, u32[]{:S(2)}) copy-start(bf16[3,256,768]{2,1,0:T(8,128)(2,1)} %out_grad.1) | copy-start | bytes 3538948
  109.7 7.6 %copy-start.19 = (f32[2304]{0:T(1024)S(1)}, f32[2304]{0:T(1024)}, u32[]{:S(2)}) copy-start(f32[2304]{0:T(1024)} %reduce.1) | copy-start | bytes 27652
  115.7 3.5 collective-permute-start.17
  115.7 2.7 collective-permute-start.13
  116.2 9.5 %collective-permute-start.19 = (bf16[3,256,768]{2,1,0:T(8,128)(2,1)S(1)}, bf16[3,256,768]{2,1,0:T(8,128)(2,1)}, u32[]{:S(2)}, u32[]{:S(2)}) collective-permute-start(bf16[3,256,768]{2,1,0:T(8,128)(2,1)S(1)} %copy-done.22), channel_id=1, source_target_pairs={{0,1},{1,0},{2,3},{3,2},{4,5},{5,4},{6,7},{7,6},{8,9},{9,8},{10,11... | collective-permute-start | bytes 3538952 | tf_op jit(solution)/shard_map/ppermute | solution.py:79
  125.6 3.2 collective-permute-start.18
  167.5 4.9 %collective-permute-start.20 = (bf16[2,3,256,768]{3,2,1,0:T(8,128)(2,1)}, bf16[2,3,256,768]{3,2,1,0:T(8,128)(2,1)}, u32[]{:S(2)}, u32[]{:S(2)}) collective-permute-start(bf16[2,3,256,768]{3,2,1,0:T(8,128)(2,1)} %get-tuple-element.166), channel_id=1, source_target_pairs={{0,1},{1,0},{2,3},{3,2},{4,5},{5,4},{6,7},{7,6},{8,9},{9,8},{10,11... | collective-permute-start | bytes 7077896 | tf_op jit(solution)/shard_map/ppermute | solution.py:79
  167.7 28.6 %collective-permute-start.22 = (bf16[4,96,1536]{2,1,0:T(8,128)(2,1)}, bf16[4,96,1536]{2,1,0:T(8,128)(2,1)}, u32[]{:S(2)}, u32[]{:S(2)}) collective-permute-start(bf16[4,96,1536]{2,1,0:T(8,128)(2,1)} %get-tuple-element.178), channel_id=1, source_target_pairs={{0,4},{4,0},{8,12},{12,8},{16,20},{20,16},{24,28},{28,24},{1,5},{5... | collective-permute-start | bytes 3538952 | tf_op jit(solution)/shard_map/ppermute | solution.py:83
  185.2 2.8 collective-permute-start.21
  185.4 14.3 %collective-permute-start.23 = (bf16[432,384]{1,0:T(8,128)(2,1)}, bf16[432,384]{1,0:T(8,128)(2,1)S(1)}, u32[]{:S(2)}, u32[]{:S(2)}) collective-permute-start(bf16[432,384]{1,0:T(8,128)(2,1)} %get-tuple-element.187), channel_id=1, source_target_pairs={{0,2},{1,3},{2,0},{3,1},{4,6},{5,7},{6,4},{7,5},{8,10},{9,11},{10,... | collective-permute-start | bytes 995336 | tf_op jit(solution)/shard_map/ppermute | solution.py:79
  185.9 16.3 %collective-permute-start.24 = (bf16[432,384]{1,0:T(8,128)(2,1)}, bf16[432,384]{1,0:T(8,128)(2,1)S(1)}, u32[]{:S(2)}, u32[]{:S(2)}) collective-permute-start(bf16[432,384]{1,0:T(8,128)(2,1)} %get-tuple-element.188), channel_id=1, source_target_pairs={{0,3},{1,2},{2,1},{3,0},{4,7},{5,6},{6,5},{7,4},{8,11},{9,10},{10,... | collective-permute-start | bytes 995336 | tf_op jit(solution)/shard_map/ppermute | solution.py:79
  187.9 0.9 copy-start.2
  193.4 48.5 %collective-permute-start.25 = (bf16[4,96,1920]{2,1,0:T(8,128)(2,1)}, bf16[4,96,1920]{2,1,0:T(8,128)(2,1)}, u32[]{:S(2)}, u32[]{:S(2)}) collective-permute-start(bf16[4,96,1920]{2,1,0:T(8,128)(2,1)} %get-tuple-element.176), channel_id=1, source_target_pairs={{0,4},{4,0},{8,12},{12,8},{16,20},{20,16},{24,28},{28,24},{1,5},{5... | collective-permute-start | bytes 4423688 | tf_op jit(solution)/shard_map/ppermute | solution.py:83
  199.7 6.9 %copy-start.9 = (bf16[432,384]{1,0:T(8,128)(2,1)}, bf16[432,384]{1,0:T(8,128)(2,1)S(1)}, u32[]{:S(2)}) copy-start(bf16[432,384]{1,0:T(8,128)(2,1)S(1)} %collective-permute-done.23.g2) | copy-start | bytes 995332
  202.2 4.4 %copy-start.10 = (bf16[432,384]{1,0:T(8,128)(2,1)}, bf16[432,384]{1,0:T(8,128)(2,1)S(1)}, u32[]{:S(2)}) copy-start(bf16[432,384]{1,0:T(8,128)(2,1)S(1)} %collective-permute-done.24.g3) | copy-start | bytes 995332
  202.2 49.5 %collective-permute-start.26 = (bf16[96,1536]{1,0:T(8,128)(2,1)}, bf16[96,1536]{1,0:T(8,128)(2,1)}, u32[]{:S(2)}, u32[]{:S(2)}) collective-permute-start(bf16[96,1536]{1,0:T(8,128)(2,1)} %get-tuple-element.196), channel_id=1, source_target_pairs={{0,8},{4,12},{8,0},{12,4},{16,24},{20,28},{24,16},{28,20},{1,9},{5... | collective-permute-start | bytes 884744 | tf_op jit(solution)/shard_map/ppermute | solution.py:83
  203.7 48.5 %collective-permute-start.27 = (bf16[96,1536]{1,0:T(8,128)(2,1)}, bf16[96,1536]{1,0:T(8,128)(2,1)}, u32[]{:S(2)}, u32[]{:S(2)}) collective-permute-start(bf16[96,1536]{1,0:T(8,128)(2,1)} %get-tuple-element.197), channel_id=1, source_target_pairs={{0,16},{4,20},{8,24},{12,28},{16,0},{20,4},{24,8},{28,12},{1,17},{... | collective-permute-start | bytes 884744 | tf_op jit(solution)/shard_map/ppermute | solution.py:83
  206.1 46.1 %collective-permute-start.28 = (bf16[96,1536]{1,0:T(8,128)(2,1)}, bf16[96,1536]{1,0:T(8,128)(2,1)}, u32[]{:S(2)}, u32[]{:S(2)}) collective-permute-start(bf16[96,1536]{1,0:T(8,128)(2,1)} %get-tuple-element.198), channel_id=1, source_target_pairs={{0,24},{4,28},{8,16},{12,20},{16,8},{20,12},{24,0},{28,4},{1,25},{... | collective-permute-start | bytes 884744 | tf_op jit(solution)/shard_map/ppermute | solution.py:83
  245.7 37.3 %collective-permute-start.29 = (bf16[96,1920]{1,0:T(8,128)(2,1)}, bf16[96,1920]{1,0:T(8,128)(2,1)S(1)}, u32[]{:S(2)}, u32[]{:S(2)}) collective-permute-start(bf16[96,1920]{1,0:T(8,128)(2,1)} %get-tuple-element.192), channel_id=1, source_target_pairs={{0,8},{4,12},{8,0},{12,4},{16,24},{20,28},{24,16},{28,20},{1,9},{5... | collective-permute-start | bytes 1105928 | tf_op jit(solution)/shard_map/ppermute | solution.py:83
  246.3 36.7 %collective-permute-start.30 = (bf16[96,1920]{1,0:T(8,128)(2,1)}, bf16[96,1920]{1,0:T(8,128)(2,1)S(1)}, u32[]{:S(2)}, u32[]{:S(2)}) collective-permute-start(bf16[96,1920]{1,0:T(8,128)(2,1)} %get-tuple-element.193), channel_id=1, source_target_pairs={{0,16},{4,20},{8,24},{12,28},{16,0},{20,4},{24,8},{28,12},{1,17},{... | collective-permute-start | bytes 1105928 | tf_op jit(solution)/shard_map/ppermute | solution.py:83
  251.7 31.3 %collective-permute-start.31 = (bf16[96,1920]{1,0:T(8,128)(2,1)}, bf16[96,1920]{1,0:T(8,128)(2,1)}, u32[]{:S(2)}, u32[]{:S(2)}) collective-permute-start(bf16[96,1920]{1,0:T(8,128)(2,1)} %get-tuple-element.194), channel_id=1, source_target_pairs={{0,24},{4,28},{8,16},{12,20},{16,8},{20,12},{24,0},{28,4},{1,25},{... | collective-permute-start | bytes 1105928 | tf_op jit(solution)/shard_map/ppermute | solution.py:83
  253.7 34.5 %all-to-all-start.2 = ((f32[8,4,2304]{2,1,0:T(4,128)}), f32[8,4,2304]{2,1,0:T(4,128)S(1)}, u32[]{:S(2)}, u32[]{:S(2)}) async-start(f32[8,4,2304]{2,1,0:T(4,128)} %broadcast_in_dim.4), calls=%async_computation.2 | async-start | bytes 589824 | tf_op jit(solution)/shard_map/all_to_all | solution.py:101
  283.0 5.3 %copy-start.7 = (bf16[96,1920]{1,0:T(8,128)(2,1)}, bf16[96,1920]{1,0:T(8,128)(2,1)S(1)}, u32[]{:S(2)}) copy-start(bf16[96,1920]{1,0:T(8,128)(2,1)S(1)} %collective-permute-done.29.refs_5_) | copy-start | bytes 1105924
  283.0 5.2 %copy-start.8 = (bf16[96,1920]{1,0:T(8,128)(2,1)}, bf16[96,1920]{1,0:T(8,128)(2,1)S(1)}, u32[]{:S(2)}) copy-start(bf16[96,1920]{1,0:T(8,128)(2,1)S(1)} %collective-permute-done.30.refs_6_) | copy-start | bytes 1105924
  291.7 4.9 %collective-permute-start.32 = (bf16[2,3,256,768]{3,2,1,0:T(8,128)(2,1)}, bf16[2,3,256,768]{3,2,1,0:T(8,128)(2,1)}, u32[]{:S(2)}, u32[]{:S(2)}) collective-permute-start(bf16[2,3,256,768]{3,2,1,0:T(8,128)(2,1)} %token_grad.1), channel_id=1, source_target_pairs={{0,1},{1,0},{2,3},{3,2},{4,5},{5,4},{6,7},{7,6},{8,9},{9,8},{10,11... | collective-permute-start | bytes 7077896 | tf_op jit(solution)/shard_map/ppermute | solution.py:79
  291.7 18.6 %collective-permute-start.37 = (bf16[96,3456]{1,0:T(8,128)(2,1)}, bf16[96,3456]{1,0:T(8,128)(2,1)S(1)}, u32[]{:S(2)}, u32[]{:S(2)}) collective-permute-start(bf16[96,3456]{1,0:T(8,128)(2,1)} %gather.2.own), channel_id=1, source_target_pairs={{0,2},{1,3},{2,0},{3,1},{4,6},{5,7},{6,4},{7,5},{8,10},{9,11},{10,... | collective-permute-start | bytes 1990664 | tf_op jit(solution)/shard_map/ppermute | solution.py:79
  292.2 15.4 %collective-permute-start.33 = (bf16[4,112,576]{2,1,0:T(8,128)(2,1)}, bf16[4,112,576]{2,1,0:T(8,128)(2,1)}, u32[]{:S(2)}, u32[]{:S(2)}) collective-permute-start(bf16[4,112,576]{2,1,0:T(8,128)(2,1)} %get-tuple-element.216), channel_id=1, source_target_pairs={{0,4},{4,0},{8,12},{12,8},{16,20},{20,16},{24,28},{28,24},{1,5},{5... | collective-permute-start | bytes 1548296 | tf_op jit(solution)/shard_map/ppermute | solution.py:83
  293.3 9.4 %copy-start.12 = (f32[32,96]{1,0:T(8,128)S(1)}, f32[32,96]{1,0:T(8,128)}, u32[]{:S(2)}) copy-start(f32[32,96]{1,0:T(8,128)} %copy-done.11) | copy-start | bytes 36868
  303.2 7.2 %copy-start.1 = (bf16[96,3456]{1,0:T(8,128)(2,1)S(1)}, bf16[96,3456]{1,0:T(8,128)(2,1)}, u32[]{:S(2)}) copy-start(bf16[96,3456]{1,0:T(8,128)(2,1)} %gather.2.own) | copy-start | bytes 1990660
  310.4 5.4 %copy-start.25 = (bf16[112,576]{1,0:T(8,128)(2,1)S(1)}, bf16[112,576]{1,0:T(8,128)(2,1)}, u32[]{:S(2)}) copy-start(bf16[112,576]{1,0:T(8,128)(2,1)} %get-tuple-element.220) | copy-start | bytes 387076
  311.3 5.9 %collective-permute-start.38 = (bf16[2,96,3456]{2,1,0:T(8,128)(2,1)S(1)}, bf16[2,96,3456]{2,1,0:T(8,128)(2,1)}, u32[]{:S(2)}, u32[]{:S(2)}) collective-permute-start(bf16[2,96,3456]{2,1,0:T(8,128)(2,1)S(1)} %pad_maximum_fusion), channel_id=1, source_target_pairs={{0,1},{1,0},{2,3},{3,2},{4,5},{5,4},{6,7},{7,6},{8,9},{9,8},{10,11... | collective-permute-start | bytes 3981320 | tf_op jit(solution)/shard_map/ppermute | solution.py:79
  311.3 29.1 %collective-permute-start.39 = (bf16[3,256,768]{2,1,0:T(8,128)(2,1)}, bf16[3,256,768]{2,1,0:T(8,128)(2,1)}, u32[]{:S(2)}, u32[]{:S(2)}) collective-permute-start(bf16[3,256,768]{2,1,0:T(8,128)(2,1)} %across.1), channel_id=1, source_target_pairs={{0,2},{1,3},{2,0},{3,1},{4,6},{5,7},{6,4},{7,5},{8,10},{9,11},{10,... | collective-permute-start | bytes 3538952 | tf_op jit(solution)/shard_map/ppermute | solution.py:79
  312.8 8.6 %collective-permute-start.34 = (bf16[112,576]{1,0:T(8,128)(2,1)}, bf16[112,576]{1,0:T(8,128)(2,1)S(1)}, u32[]{:S(2)}, u32[]{:S(2)}) collective-permute-start(bf16[112,576]{1,0:T(8,128)(2,1)} %get-tuple-element.218), channel_id=1, source_target_pairs={{0,8},{4,12},{8,0},{12,4},{16,24},{20,28},{24,16},{28,20},{1,9},{5... | collective-permute-start | bytes 387080 | tf_op jit(solution)/shard_map/ppermute | solution.py:83
  313.0 13.9 %collective-permute-start.35 = (bf16[112,576]{1,0:T(8,128)(2,1)}, bf16[112,576]{1,0:T(8,128)(2,1)S(1)}, u32[]{:S(2)}, u32[]{:S(2)}) collective-permute-start(bf16[112,576]{1,0:T(8,128)(2,1)} %get-tuple-element.219), channel_id=1, source_target_pairs={{0,16},{4,20},{8,24},{12,28},{16,0},{20,4},{24,8},{28,12},{1,17},{... | collective-permute-start | bytes 387080 | tf_op jit(solution)/shard_map/ppermute | solution.py:83
  315.8 11.1 %collective-permute-start.36 = (bf16[112,576]{1,0:T(8,128)(2,1)S(1)}, bf16[112,576]{1,0:T(8,128)(2,1)S(1)}, u32[]{:S(2)}, u32[]{:S(2)}) collective-permute-start(bf16[112,576]{1,0:T(8,128)(2,1)S(1)} %copy-done.25), channel_id=1, source_target_pairs={{0,24},{4,28},{8,16},{12,20},{16,8},{20,12},{24,0},{28,4},{1,25},{... | collective-permute-start | bytes 387080 | tf_op jit(solution)/shard_map/ppermute | solution.py:83
  321.4 5.4 %copy-start.15 = (bf16[112,576]{1,0:T(8,128)(2,1)}, bf16[112,576]{1,0:T(8,128)(2,1)S(1)}, u32[]{:S(2)}) copy-start(bf16[112,576]{1,0:T(8,128)(2,1)S(1)} %collective-permute-done.34.refs_1_) | copy-start | bytes 387076
  330.7 17.1 %collective-permute-start.40 = (bf16[112,576]{1,0:T(8,128)(2,1)}, bf16[112,576]{1,0:T(8,128)(2,1)S(1)}, u32[]{:S(2)}, u32[]{:S(2)}) collective-permute-start(bf16[112,576]{1,0:T(8,128)(2,1)} %gather.3.own), channel_id=1, source_target_pairs={{0,2},{1,3},{2,0},{3,1},{4,6},{5,7},{6,4},{7,5},{8,10},{9,11},{10,... | collective-permute-start | bytes 387080 | tf_op jit(solution)/shard_map/ppermute | solution.py:79
  331.2 16.6 %collective-permute-start.41 = (bf16[112,576]{1,0:T(8,128)(2,1)}, bf16[112,576]{1,0:T(8,128)(2,1)S(1)}, u32[]{:S(2)}, u32[]{:S(2)}) collective-permute-start(bf16[112,576]{1,0:T(8,128)(2,1)} %gather.3.own), channel_id=1, source_target_pairs={{0,1},{1,0},{2,3},{3,2},{4,5},{5,4},{6,7},{7,6},{8,9},{9,8},{10,11... | collective-permute-start | bytes 387080 | tf_op jit(solution)/shard_map/ppermute | solution.py:79
  331.2 16.7 %collective-permute-start.42 = (bf16[112,576]{1,0:T(8,128)(2,1)}, bf16[112,576]{1,0:T(8,128)(2,1)S(1)}, u32[]{:S(2)}, u32[]{:S(2)}) collective-permute-start(bf16[112,576]{1,0:T(8,128)(2,1)} %gather.3.own), channel_id=1, source_target_pairs={{0,3},{1,2},{2,1},{3,0},{4,7},{5,6},{6,5},{7,4},{8,11},{9,10},{10,... | collective-permute-start | bytes 387080 | tf_op jit(solution)/shard_map/ppermute | solution.py:79
  333.5 18.9 %all-to-all-start.3 = ((f32[8,32,96]{2,1,0:T(8,128)}), f32[8,32,96]{2,1,0:T(8,128)S(1)}, u32[]{:S(2)}, u32[]{:S(2)}) async-start(f32[8,32,96]{2,1,0:T(8,128)} %broadcast_in_dim.5), calls=%async_computation.3 | async-start | bytes 262144 | tf_op jit(solution)/shard_map/all_to_all | solution.py:101
  338.3 14.3 %copy-start.21 = (f32[1,32]{1,0:T(1,128)S(1)}, f32[1,32]{1,0:T(1,128)}, u32[]{:S(2)}) copy-start(f32[1,32]{1,0:T(1,128)} %get-tuple-element.235) | copy-start | bytes 388
  (9 other events, 6.3 us)
